TPU v7x, 128 devices: a whole 4x4x4 slice. The times are simulated.
128 devices in a mesh: table: 8 (over y, core), ray: 16 (over x, z).
Axes of the slice: x: 4, y: 4, z: 4, core: 2. Of those that a mesh axis runs over, the one named last changes fastest.
Arguments:
- table: float32 [2, 8192, 4, 512], P(None, ('table', 'ray')), may hold values from -6 to 6
- moment1: float32 [2, 8192, 4, 512], P(None, ('table', 'ray')), may hold values from -2 to 2
- moment2: float32 [2, 8192, 4, 512], P(None, ('table', 'ray')), may hold values from 0.01 to 1
- block_ids: int32 [8, 2, 128, 4], replicated, may hold values from 0 to 63, as said below
- sample_slot: int32 [2, 65536], P(None, ('table', 'ray')), may hold values from 0 to 511, as said below
- corners: int32 [2, 8, 65536], P(None, None, ('table', 'ray')), may hold values from 0 to 511
- fractions: float32 [2, 3, 65536], P(None, None, ('table', 'ray')), may hold values from 0 to 1
- feat_cot: float32 [2, 4, 65536], P(None, None, ('table', 'ray')), may hold values from -24 to 24
- weight_in: float32 [64, 8], replicated, may hold values from -2 to 2
- weight_out: float32 [16, 64], replicated, may hold values from -0.75 to 0.75
Outputs:
- table_new: float32 [2, 8192, 4, 512], P(None, ('table', 'ray'))
- moment1_new: float32 [2, 8192, 4, 512], P(None, ('table', 'ray'))
- moment2_new: float32 [2, 8192, 4, 512], P(None, ('table', 'ray'))
- mlp_out: float32 [16, 65536], P(None, ('table', 'ray'))
Inputs may be any that keep to these rules, and one draw needn't show every extreme that they name: `block_ids`: for every group, level and owner the 4 listed blocks are distinct local block numbers of that owner. `sample_slot`: each device's 512 samples of a level come in 16 runs of 512 // 16 in order; the samples of run i read only blocks of owners o with o % 16 == i.
All inputs are finite; a program needn't handle non-finite values.
Results may differ from a plain program's by a relative error of at most 0.000075.
Values sent between devices are 32-bit elements; how exact they have to be, the bound alone decides.
No kernel may reach another device: no remote copies, remote signals or barrier semaphores. Data moves between devices by JAX's collectives and lax.ppermute only.
A program may use at most 64 MiB of HBM per device.

v0:
```python
import jax
import jax.numpy as jnp
from jax import lax
from jax.sharding import PartitionSpec as P

beta_one = 0.9
beta_two = 0.99
learn_rate = 0.01
adam_eps = 1e-15


def hat_weights(fractions):
    columns = []
    for corner in range(8):
        weight = jnp.ones_like(fractions[:, 0, :])
        for dimension in range(3):
            if corner >> dimension & 1:
                weight = weight * fractions[:, dimension, :]
            else:
                weight = weight * (1.0 - fractions[:, dimension, :])
        columns.append(weight)
    return jnp.stack(columns, axis=1)


def corner_spread(weights, corners, block_rows):
    entry = jnp.arange(block_rows, dtype=jnp.int32)
    total = jnp.zeros(weights[:, 0].shape + (block_rows,), jnp.float32)
    for corner in range(8):
        hit = corners[:, corner, :, :, None] == entry
        total = total + jnp.where(hit, weights[:, corner, :, :, None], 0.0)
    return total


def candidate_onehot(slots, ray_size, slot_count, candidates):
    local_slot = slots // slot_count // ray_size * slot_count + slots % slot_count
    return (local_slot[..., None] == jnp.arange(candidates, dtype=jnp.int32)).astype(jnp.float32)


def block_partials(onehot, cot, spread):
    levels, runs, run_len, candidates = onehot.shape
    cot_rows = jnp.transpose(cot, (0, 2, 3, 1))
    scaled = onehot[:, :, :, :, None] * cot_rows[:, :, :, None, :]
    scaled = scaled.reshape(levels, runs, run_len, candidates * 4)
    return jnp.einsum("lrjc,lrje->lrce", scaled, spread, precision=lax.Precision.HIGHEST)


def on_device(
    table,
    moment1,
    moment2,
    block_ids,
    sample_slot,
    corners,
    fractions,
    feat_cot,
    weight_in,
    weight_out,
):
    table_size = lax.axis_size("table")
    ray_size = lax.axis_size("ray")
    levels, blocks_dev, features, block_rows = table.shape
    slot_count = block_ids.shape[3]
    samples = sample_slot.shape[1]
    candidates = table_size * slot_count
    run_len = samples // ray_size
    owner_here = lax.axis_index("table") * ray_size + lax.axis_index("ray")
    weights = hat_weights(fractions)
    spread = corner_spread(
        weights.reshape(levels, 8, ray_size, run_len),
        corners.reshape(levels, 8, ray_size, run_len),
        block_rows,
    )
    onehot = candidate_onehot(
        sample_slot.reshape(levels, ray_size, run_len), ray_size, slot_count, candidates
    )
    partial_value = block_partials(onehot, feat_cot.reshape(levels, 4, ray_size, run_len), spread)
    partial_value = partial_value.reshape(levels, ray_size, table_size, slot_count, 4, block_rows)
    partial_value = jnp.transpose(partial_value, (0, 2, 1, 3, 4, 5))
    routed = lax.all_to_all(partial_value, "table", split_axis=1, concat_axis=1, tiled=True)
    summed = lax.psum_scatter(routed, "ray", scatter_dimension=2, tiled=True)
    received = summed.reshape(levels, table_size * slot_count, 4 * block_rows)
    own_ids = lax.dynamic_index_in_dim(block_ids, owner_here, axis=2, keepdims=False)
    requests = jnp.transpose(own_ids, (1, 0, 2)).reshape(levels, table_size * slot_count)
    block_range = jnp.arange(blocks_dev, dtype=jnp.int32)
    selector = (requests[:, None, :] == block_range[None, :, None]).astype(jnp.float32)
    gradient = jnp.einsum("lbk,lkf->lbf", selector, received, precision=lax.Precision.HIGHEST)
    gradient = gradient.reshape(table.shape)
    first_new = beta_one * moment1 + (1.0 - beta_one) * gradient
    second_new = beta_two * moment2 + (1.0 - beta_two) * gradient * gradient
    table_new = table - learn_rate * first_new / (jnp.sqrt(second_new) + adam_eps)
    flat_table = table_new.reshape(levels, blocks_dev, 4 * block_rows)
    picked = jnp.take_along_axis(flat_table, requests[:, :, None], axis=1)
    picked = picked.reshape(levels, table_size, 1, slot_count, 4, block_rows)
    returned = lax.all_to_all(picked, "table", split_axis=1, concat_axis=1, tiled=True)
    fetched = lax.all_gather(returned, "ray", axis=2, tiled=True)
    run_tables = jnp.transpose(fetched, (0, 2, 1, 3, 4, 5)).reshape(
        levels, ray_size, candidates * 4, block_rows
    )
    looked = jnp.einsum("lrje,lrce->lrjc", spread, run_tables, precision=lax.Precision.HIGHEST)
    looked = looked.reshape(levels, ray_size, run_len, candidates, 4)
    values = jnp.sum(onehot[:, :, :, :, None] * looked, axis=3)
    encoded = jnp.transpose(values, (0, 3, 1, 2)).reshape(4 * levels, samples)
    hidden = jax.nn.relu(jnp.dot(weight_in, encoded, precision=lax.Precision.HIGHEST))
    mlp_out = jnp.dot(weight_out, hidden, precision=lax.Precision.HIGHEST)
    return (table_new, first_new, second_new, mlp_out)


def solution(mesh):
    in_specs = (
        P(None, ("table", "ray"), None, None),
        P(None, ("table", "ray"), None, None),
        P(None, ("table", "ray"), None, None),
        P(),
        P(None, ("table", "ray")),
        P(None, None, ("table", "ray")),
        P(None, None, ("table", "ray")),
        P(None, None, ("table", "ray")),
        P(),
        P(),
    )
    out_specs = (
        P(None, ("table", "ray"), None, None),
        P(None, ("table", "ray"), None, None),
        P(None, ("table", "ray"), None, None),
        P(None, ("table", "ray")),
    )
    return jax.shard_map(
        on_device, mesh=mesh, in_specs=in_specs, out_specs=out_specs, check_vma=False
    )
```

profile of v0, /device:TPU:0, one launch (start us, length us, event | category | flops | bytes accessed | tf_op | source)
XLA Modules:
  0.0 376.4 jit_solution(16789116876656948793)
XLA Ops:
  7.2 0.7 fusion.14
  8.0 0.7 fusion.16
  8.8 0.8 reshape.206
  10.1 0.8 reshape.207
  10.9 0.8 reshape.208
  12.1 11.2 %fusion = f32[2,16,128,512]{3,2,1,0:T(8,128)} fusion(f32[2,16,32,128]{2,1,3,0:T(8,128)S(1)} %bitcast.64, f32[2,16,32]{2,1,0:T(8,128)S(1)} %broadcast_in_dim.107, s32[2,16,32]{2,1,0:T(8,128)S(1)} %get-tuple-element.8, f32[2,16,32]{2,1,0:T(8,128)S(1)} %broadcast_in_dim.105, s32[2,16,32]{2,1,0:T(8,128)S(1)} %get-tuple-element.9, ...), kind=kOutput, calls=%fused_computation.2 | convolution fusion | flops 817364992 | bytes 8978432 | tf_op jit(solution)/shard_map/lrjc,lrje->lrce/dot_general | solution.py:44
  23.4 9.8 %reshape.209 = f32[2,16,8,4,4,512]{5,4,3,2,1,0:T(4,128)} reshape(f32[2,16,128,512]{3,2,1,0:T(8,128)} %fusion) | data formatting | bytes 16777216 | tf_op jit(solution)/shard_map/reshape | solution.py:77
  33.1 10.3 %copy.52 = f32[2,16,8,4,4,512]{5,4,3,1,0,2:T(4,128)} copy(f32[2,16,8,4,4,512]{5,4,3,2,1,0:T(4,128)} %reshape.209) | data formatting | bytes 16777216 | tf_op jit(solution)/shard_map/reshape | solution.py:77
  43.5 99.2 %all_to_all.10 = f32[2,8,16,4,4,512]{5,4,3,2,0,1:T(4,128)S(1)} all-to-all(f32[2,8,16,4,4,512]{5,4,3,2,0,1:T(4,128)} %bitcast.61), channel_id=1, replica_groups=mesh['table'=8,'ray'=16] {'table'}, dimensions={1} | all-to-all | bytes 16777216 | tf_op jit(solution)/shard_map/all_to_all | solution.py:79
  142.7 10.9 %copy.41 = f32[2,8,16,4,4,512]{5,1,4,3,0,2:T(8,128)} copy(f32[2,8,16,4,4,512]{5,4,3,2,0,1:T(4,128)S(1)} %all_to_all.10) | data formatting | bytes 16777216 | tf_op jit(solution)/shard_map/all_to_all | solution.py:79
  154.6 86.1 %reduce-scatter.4.cloned.1.call-done = f32[2,8,1,4,4,512]{5,1,4,3,0,2:T(8,128)} async-done(((f32[2,8,16,4,4,512]{5,1,4,3,0,2:T(8,128)}), f32[2,8,1,4,4,512]{5,1,4,3,0,2:T(8,128)}) %reduce-scatter.4.cloned.1.call-update) | async-done | bytes 524304
  240.7 1.4 copy.42
  242.4 0.7 fusion.5
  243.1 0.7 reshape.211
  243.9 4.5 %divide_subtract_fusion = (f32[2,64,4,512]{3,2,1,0:T(4,128)S(1)}, f32[2,64,4,512]{3,2,1,0:T(4,128)}, f32[2,64,4,512]{3,2,1,0:T(4,128)}) fusion(f32[2,64,4,512]{3,2,1,0:T(4,128)} %param.10, f32[2,64,4,512]{3,2,1,0:T(4,128)S(1)} %reshape.211, f32[2,64,4,512]{3,2,1,0:T(4,128)} %param.11, f32[2,64,4,512]{3,2,1,0:T(4,128)} %param.12), kind=kLoop, calls=%fused_computation.18 | loop fusion | flops 2883584 | bytes 7340032 | tf_op jit(solution)/shard_map/sub | solution.py:90
  248.4 0.7 reshape.212
  249.1 1.2 gather_fusion
  250.9 14.6 %all_to_all.11 = f32[2,8,1,4,4,512]{5,4,3,2,0,1:T(4,128)} all-to-all(f32[2,8,1,4,4,512]{5,4,3,2,0,1:T(4,128)S(1)} %copy_select_fusion), channel_id=1, replica_groups=mesh['table'=8,'ray'=16] {'table'}, dimensions={1} | all-to-all | bytes 1048576 | tf_op jit(solution)/shard_map/all_to_all | solution.py:94
  265.5 68.5 %all-gather.2.cloned.1.call-done = f32[2,8,16,4,4,512]{5,4,3,2,0,1:T(4,128)} async-done(((f32[2,8,1,4,4,512]{5,4,3,2,0,1:T(4,128)}), f32[2,8,16,4,4,512]{5,4,3,2,0,1:T(4,128)}) %all-gather.2.cloned.1.call-update) | async-done | bytes 8388624 | tf_op jit(solution)/shard_map/all_gather | solution.py:95
  334.0 10.3 %copy.46 = f32[2,16,8,4,4,512]{5,4,3,2,1,0:T(4,128)} copy(f32[2,16,8,4,4,512]{5,4,3,1,0,2:T(4,128)} %bitcast.63) | data formatting | bytes 16777216 | tf_op jit(solution)/shard_map/transpose | solution.py:96
  344.4 10.0 %reshape.213 = f32[2,16,128,512]{3,2,1,0:T(8,128)} reshape(f32[2,16,8,4,4,512]{5,4,3,2,1,0:T(4,128)} %copy.46) | data formatting | bytes 16777216 | tf_op jit(solution)/shard_map/reshape | solution.py:96
  354.4 12.6 %fusion.3 = f32[2,16,32,128]{3,2,1,0:T(8,128)S(1)} fusion(f32[2,16,128,512]{3,2,1,0:T(8,128)} %reshape.213, f32[2,16,32]{2,1,0:T(8,128)S(1)} %broadcast_in_dim.107, s32[2,16,32]{2,1,0:T(8,128)S(1)} %get-tuple-element.8, f32[2,16,32]{2,1,0:T(8,128)S(1)} %broadcast_in_dim.105, s32[2,16,32]{2,1,0:T(8,128)S(1)} %get-tuple-element.9, ...), kind=kOutput, calls=%fused_computation.21 | convolution fusion | flops 817364992 | bytes 8978432 | tf_op jit(solution)/shard_map/lrje,lrce->lrjc/dot_general | solution.py:99
  367.0 0.9 copy.47
  368.7 0.8 convolution_bitcast_fusion
  (41 shorter events, 3.6 us)
Async XLA Ops:
  7.2 146.7 %copy-start = (s32[8,2,128,4]{2,3,1,0:T(4,128)S(1)}, s32[8,2,128,4]{2,3,1,0:T(4,128)}, u32[]{:S(2)}) copy-start(s32[8,2,128,4]{2,3,1,0:T(4,128)} %param.13) | copy-start | bytes 98308
  7.2 233.5 %reduce-scatter.4.cloned.1.call-start = ((), (), s32[]{:S(2)}) async-start(), calls=%async_computation.4 | async-start | bytes 8912896
  153.6 180.4 %all-gather.2.cloned.1.call-start = ((), (), s32[]{:S(2)}) async-start(), calls=%async_computation.3 | async-start | bytes 8912896 | tf_op jit(solution)/shard_map/all_gather | solution.py:95
  248.4 1.9 copy-start.2
  367.0 1.4 copy-start.4
  367.0 2.5 copy-start.1
  368.0 0.7 copy-start.3
Sparse Core Ops, SparseCore 0:
  153.7 86.9 reduce-scatter.3
  265.6 68.3 all-gather.1
where the time goes:
time: 378 us; the launch traced here: 376 us
  waiting for transfers between devices  155 us (41%)
  blocking collectives  114 us (30%)
  local copies, waits for them, and re-layouts  60.9 us (16%)
  matrix products  25.7 us (7%)
  between operations  14.3 us (4%)
  other arithmetic  6.83 us (2%)
    all_to_all x1, blocking collectives, on_device(): lax.all_to_all(partial_value, 'table', split_axis=1, concat_axis=1, tiled...  99.2 us
    unnamed x3, waiting for transfers between devices  86.1 us
    all_gather x1, waiting for transfers between devices, on_device(): fetched = lax.all_gather(returned, 'ray', axis=2, tiled=True)  68.5 us
    reshape x2, local copies, waits for them, and re-layouts, on_device(): partial_value.reshape(levels, ray_size, table_size, slot_count, 4, block_...  20.1 us
    all_to_all x1, blocking collectives, on_device(): lax.all_to_all(picked, 'table', split_axis=1, concat_axis=1, tiled=True)  14.6 us
    dot_general x1, matrix products, on_device(): jnp.einsum('lrje,lrce->lrjc', spread, run_tables, precision=lax.Precision...  12.6 us
    dot_general x1, matrix products, block_partials(): jnp.einsum('lrjc,lrje->lrce', scaled, spread, precision=lax.Precision.HIG...  11.2 us
    all_to_all x1, local copies, waits for them, and re-layouts, on_device(): lax.all_to_all(partial_value, 'table', split_axis=1, concat_axis=1, tiled...  10.9 us
  transfers between devices with their start and end apart: 2, of which 2 were waited for; matrix products, arithmetic and copies ran while one was open for 0% of the time, Pallas kernels for 0%

commit v1 on v0

v1 whole, which is shorter than its diff:
```python
import jax
import jax.numpy as jnp
from jax import lax
from jax.experimental import pallas as pl
from jax.experimental.pallas import tpu as pltpu
from jax.sharding import PartitionSpec as P

beta_one = 0.9
beta_two = 0.99
learn_rate = 0.01
adam_eps = 1e-15

LANES = 128
RUN = 32
VMEM_LIMIT = 48 << 20


def block_transpose(pieces):
    group = lax.broadcasted_iota(jnp.int32, pieces[0].shape, 1) // RUN
    results = []
    for q in range(4):
        value = pieces[q]
        for p in range(4):
            if p != q:
                moved = pltpu.roll(pieces[p], (RUN * (p - q)) % LANES, 1)
                value = jnp.where(group == p, moved, value)
        results.append(value)
    return results


def split_two(value):
    high = value.astype(jnp.bfloat16)
    low = (value - high.astype(jnp.float32)).astype(jnp.bfloat16)
    return high, low


def pack_kernel(slot_ref, corners_ref, fractions_ref, cot_ref, out_ref):
    groups = [corners_ref[0].astype(jnp.float32), corners_ref[1].astype(jnp.float32)]
    for level in range(2):
        rows = [slot_ref[level : level + 1, :].astype(jnp.float32)]
        rows += [fractions_ref[d, level : level + 1, :] for d in range(3)]
        rows += [cot_ref[level]]
        groups.append(jnp.concatenate(rows, axis=0))
    for v in range(4):
        lanes = slice(v * LANES, (v + 1) * LANES)
        for p, value in enumerate(block_transpose([g[:, lanes] for g in groups])):
            out_ref[4 * v + p] = value


def grad_kernel(recv_ref, part_ref, high_ref, low_ref, cand_ref, corner_s, aux_s):
    for v in range(4):
        lanes = slice(v * LANES, (v + 1) * LANES)
        rows = block_transpose([recv_ref[4 * v + p] for p in range(4)])
        for level in range(2):
            corner_s[level, :, lanes] = rows[level].astype(jnp.int32)
            aux_s[level, :, lanes] = rows[2 + level]
    for level in range(2):
        aux = aux_s[level]
        sub = lax.broadcasted_iota(jnp.int32, (8, 512), 0)
        hat = None
        for d in range(3):
            f = jnp.broadcast_to(aux[1 + d : 2 + d], (8, 512))
            factor = jnp.where((sub >> d) & 1 == 1, f, 1.0 - f)
            hat = factor if hat is None else hat * factor
        slot = aux[0:1].astype(jnp.int32)
        cand = (slot // 64) * 4 + slot % 4
        cand_ref[level : level + 1, :] = cand
        for v in range(4):
            lanes = slice(v * LANES, (v + 1) * LANES)
            corner = corner_s[level, :, lanes]
            hat_v = hat[:, lanes]
            corner_b = [jnp.broadcast_to(corner[c : c + 1], (16, LANES)) for c in range(8)]
            hat_b = [jnp.broadcast_to(hat_v[c : c + 1], (16, LANES)) for c in range(8)]
            base = lax.broadcasted_iota(jnp.int32, (16, LANES), 0)

            def tile(step, carry):
                start = pl.multiple_of(step * 16, 16)
                entry = base + start
                total = jnp.where(corner_b[0] == entry, hat_b[0], 0.0)
                for c in range(1, 8):
                    total = total + jnp.where(corner_b[c] == entry, hat_b[c], 0.0)
                high, low = split_two(total)
                high_ref[level, pl.ds(start, 16), lanes] = high
                low_ref[level, pl.ds(start, 16), lanes] = low
                return carry

            lax.fori_loop(0, 32, tile, 0, unroll=4)
        cot = jnp.concatenate([aux[4:8]] * 32, axis=0)
        row = lax.broadcasted_iota(jnp.int32, (128, 512), 0) // 4
        scaled = jnp.where(cand == row, cot, 0.0)
        s_high, s_low = split_two(scaled)
        high = high_ref[level]
        contract = (((1,), (1,)), ((), ()))
        both = lax.dot_general(
            jnp.concatenate([s_high, s_low], axis=0), high, contract, preferred_element_type=jnp.float32
        )
        rest = lax.dot_general(s_high, low_ref[level], contract, preferred_element_type=jnp.float32)
        part = both[:128] + both[128:] + rest
        for t in range(8):
            part_ref[t, level] = part[16 * t : 16 * t + 16]


def adam_kernel(ids_ref, recv_ref, table_ref, m1_ref, m2_ref, tnew_ref, m1new_ref, m2new_ref, pick_ref, grad_s, *, ray):
    owner = lax.axis_index("table") * ray + lax.axis_index("ray")
    sub = lax.broadcasted_iota(jnp.int32, (8, LANES), 0) < 4
    grad_s[...] = jnp.zeros_like(grad_s)
    for g in range(8):
        for level in range(2):
            for pair in range(2):
                a = [recv_ref[g, level, 8 * pair : 8 * pair + 8, c * LANES : (c + 1) * LANES] for c in range(4)]
                for half in range(2):
                    row = (g * 2 + level) * 4 + 2 * pair + half
                    block = level * 64 + ids_ref[row, owner]
                    for k in range(2):
                        x, y = a[2 * k], a[2 * k + 1]
                        if half == 0:
                            value = jnp.where(sub, x, pltpu.roll(y, 4, 0))
                        else:
                            value = jnp.where(sub, pltpu.roll(x, 4, 0), y)
                        grad_s[block, 8 * k : 8 * k + 8, :] += value

    def update(step, carry):
        at = pl.ds(step * 4, 4)
        grad = grad_s[at]
        first = beta_one * m1_ref[at] + (1.0 - beta_one) * grad
        second = beta_two * m2_ref[at] + (1.0 - beta_two) * grad * grad
        m1new_ref[at] = first
        m2new_ref[at] = second
        tnew_ref[at] = table_ref[at] - learn_rate * first / (jnp.sqrt(second) + adam_eps)
        return carry

    lax.fori_loop(0, 32, update, 0)
    for g in range(8):
        for level in range(2):
            for pair in range(2):
                row = (g * 2 + level) * 4 + 2 * pair
                one = level * 64 + ids_ref[row, owner]
                two = level * 64 + ids_ref[row + 1, owner]
                for k in range(2):
                    x = tnew_ref[one, 8 * k : 8 * k + 8, :]
                    y = tnew_ref[two, 8 * k : 8 * k + 8, :]
                    pick_ref[g, level, 8 * pair : 8 * pair + 8, 2 * k * LANES : (2 * k + 1) * LANES] = jnp.where(
                        sub, x, pltpu.roll(y, 4, 0)
                    )
                    pick_ref[g, level, 8 * pair : 8 * pair + 8, (2 * k + 1) * LANES : (2 * k + 2) * LANES] = jnp.where(
                        sub, pltpu.roll(x, 4, 0), y
                    )


def lookup_kernel(recv_ref, high_ref, low_ref, cand_ref, win_ref, wout_ref, out_ref):
    rows = []
    for level in range(2):
        blocks = recv_ref[:, level].reshape(128, 512)
        b_high, b_low = split_two(blocks)
        both = jnp.dot(
            jnp.concatenate([b_high, b_low], axis=0), high_ref[level], preferred_element_type=jnp.float32
        )
        rest = jnp.dot(b_high, low_ref[level], preferred_element_type=jnp.float32)
        looked = both[:128] + both[128:] + rest
        row = lax.broadcasted_iota(jnp.int32, (128, 512), 0) // 4
        kept = jnp.where(cand_ref[level : level + 1, :] == row, looked, 0.0)
        folded = jnp.sum(kept.reshape(16, 8, 512), axis=0)
        rows.append(folded[:4] + folded[4:])
    encoded = jnp.concatenate(rows, axis=0)
    hidden = jnp.maximum(
        lax.dot_general(
            win_ref[...], encoded, (((0,), (0,)), ((), ())),
            precision=lax.Precision.HIGHEST, preferred_element_type=jnp.float32,
        ),
        0.0,
    )
    out = jnp.dot(wout_ref[...], hidden, precision=lax.Precision.HIGHEST, preferred_element_type=jnp.float32)
    low_lanes = lax.broadcasted_iota(jnp.int32, (8, LANES), 1) < RUN
    for v in range(4):
        upper = out[:8, v * LANES : (v + 1) * LANES]
        lower = out[8:, v * LANES : (v + 1) * LANES]
        for p in range(4):
            x = pltpu.roll(upper, (-RUN * p) % LANES, 1) if p else upper
            y = pltpu.roll(lower, (RUN - RUN * p) % LANES, 1) if p != 1 else lower
            out_ref[4 * v + p] = jnp.where(low_lanes, x, y)


def unpack_kernel(recv_ref, out_ref):
    group = lax.broadcasted_iota(jnp.int32, (8, LANES), 1) // RUN
    for v in range(4):
        upper = lower = None
        for p in range(4):
            piece = recv_ref[4 * v + p]
            x = pltpu.roll(piece, RUN * p, 1) if p else piece
            y = pltpu.roll(piece, (RUN * p - RUN) % LANES, 1) if p != 1 else piece
            upper = x if upper is None else jnp.where(group == p, x, upper)
            lower = y if lower is None else jnp.where(group == p, y, lower)
        out_ref[:8, v * LANES : (v + 1) * LANES] = upper
        out_ref[8:, v * LANES : (v + 1) * LANES] = lower


def call(kernel, outs, scratch=(), in_specs=None):
    vmem = pl.BlockSpec(memory_space=pltpu.VMEM)
    shapes = [jax.ShapeDtypeStruct(s, d) for s, d in outs]
    single = len(shapes) == 1
    extra = {} if in_specs is None else {"in_specs": in_specs}
    return pl.pallas_call(
        kernel,
        out_shape=shapes[0] if single else shapes,
        out_specs=vmem if single else [vmem] * len(shapes),
        scratch_shapes=list(scratch),
        compiler_params=pltpu.CompilerParams(vmem_limit_bytes=VMEM_LIMIT),
        **extra,
    )


def exchange(value, axis):
    return lax.all_to_all(value, axis, split_axis=0, concat_axis=0, tiled=True)


def rows_of(array):
    levels, blocks = array.shape[:2]
    return array.reshape(levels, blocks, 4, 4, LANES).transpose(0, 1, 3, 2, 4).reshape(levels * blocks, 16, LANES)


def rows_back(array, shape):
    levels, blocks = shape[:2]
    return array.reshape(levels, blocks, 4, 4, LANES).transpose(0, 1, 3, 2, 4).reshape(shape)


def on_device(
    table,
    moment1,
    moment2,
    block_ids,
    sample_slot,
    corners,
    fractions,
    feat_cot,
    weight_in,
    weight_out,
):
    f32, bf16, i32 = jnp.float32, jnp.bfloat16, jnp.int32
    ray = lax.axis_size("ray")
    packed = call(pack_kernel, [((16, 8, LANES), f32)])(
        sample_slot, corners, fractions.transpose(1, 0, 2), feat_cot
    )
    samples = exchange(packed, "ray")
    part, high, low, cand = call(
        grad_kernel,
        [((8, 2, 16, 512), f32), ((2, 512, 512), bf16), ((2, 512, 512), bf16), ((2, 512), i32)],
        [pltpu.VMEM((2, 8, 512), i32), pltpu.VMEM((2, 8, 512), f32)],
    )(samples)
    received = exchange(part, "table")
    ids = block_ids.transpose(0, 1, 3, 2).reshape(64, 128)
    vmem = pl.BlockSpec(memory_space=pltpu.VMEM)
    rows = (128, 16, LANES)

    def adam(*refs):
        adam_kernel(*refs, ray=ray)

    tnew, m1new, m2new, picked = call(
        adam,
        [(rows, f32), (rows, f32), (rows, f32), ((8, 2, 16, 512), f32)],
        [pltpu.VMEM(rows, f32)],
        [pl.BlockSpec(memory_space=pltpu.SMEM)] + [vmem] * 4,
    )(ids, received, rows_of(table), rows_of(moment1), rows_of(moment2))
    returned = exchange(picked, "table")
    sent = call(lookup_kernel, [((16, 8, LANES), f32)])(
        returned, high, low, cand, weight_in.T, weight_out
    )
    back = exchange(sent, "ray")
    mlp_out = call(unpack_kernel, [((16, 512), f32)])(back)
    shape = table.shape
    return (rows_back(tnew, shape), rows_back(m1new, shape), rows_back(m2new, shape), mlp_out)


def solution(mesh):
    in_specs = (
        P(None, ("table", "ray"), None, None),
        P(None, ("table", "ray"), None, None),
        P(None, ("table", "ray"), None, None),
        P(),
        P(None, ("table", "ray")),
        P(None, None, ("table", "ray")),
        P(None, None, ("table", "ray")),
        P(None, None, ("table", "ray")),
        P(),
        P(),
    )
    out_specs = (
        P(None, ("table", "ray"), None, None),
        P(None, ("table", "ray"), None, None),
        P(None, ("table", "ray"), None, None),
        P(None, ("table", "ray")),
    )
    return jax.shard_map(
        on_device, mesh=mesh, in_specs=in_specs, out_specs=out_specs, check_vma=False
    )
```

time: 378 us -> 70.7 us (0.19)
  waiting for transfers between devices: 155 us -> 0 us
  blocking collectives: 114 us -> 53.9 us
  local copies, waits for them, and re-layouts: 60.9 us -> 6.1 us
  matrix products: 25.7 us -> 0 us
  between operations: 14.3 us -> 0.69 us
  Pallas kernels: 0 us -> 9.48 us
  other arithmetic: 6.83 us -> 0 us
    unnamed x3 -> x0, waiting for transfers between devices: 86.1 us -> none
    all_gather x1 -> x0, waiting for transfers between devices: 68.5 us -> none  [on_device(): fetched = lax.all_gather(returned, 'ray', axis=2, tiled=True)]
    all_to_all x2 -> x4, blocking collectives: 114 us -> 53.9 us  [exchange(): return lax.all_to_all(value, axis, split_axis=0, concat_axis=0, tiled=True)]
    reshape x10 -> x0, local copies, waits for them, and re-layouts: 34.4 us -> none  [the longest x2 20.1 us: on_device(): partial_value.reshape(levels, ray_size, table_size, slot_count, 4, block_...]
    dot_general x5 -> x0, matrix products: 25.7 us -> none  [the longest x1 12.6 us: on_device(): jnp.einsum('lrje,lrce->lrjc', spread, run_tables, precision=lax.Precision...]
    all_to_all x1 -> x0, local copies, waits for them, and re-layouts: 10.9 us -> none  [on_device(): lax.all_to_all(partial_value, 'table', split_axis=1, concat_axis=1, tiled...]
    transpose x2 -> x0, local copies, waits for them, and re-layouts: 10.4 us -> none  [the longest x1 10.3 us: on_device(): jnp.transpose(fetched, (0, 2, 1, 3, 4, 5))]
    pallas_call x0 -> x5, Pallas kernels: none -> 9.48 us  [the longest x1 4.1 us: on_device(): call(adam, [(rows, f32), (rows, f32), (rows, f32), ((8, 2, 16, 512), f32)...]
  transfers between devices with their start and end apart: 2 -> 0, of which waited for: 2 -> 0; matrix products, arithmetic and copies ran while one was open for 0% -> 0% of each run, Pallas kernels for 0% -> 0%
where the time goes in v1:
time: 70.7 us; the launch traced here: 70.1 us
  blocking collectives  53.9 us (76%)
  Pallas kernels  9.48 us (13%)
  local copies, waits for them, and re-layouts  6.1 us (9%)
    all_to_all x4, blocking collectives, exchange(): return lax.all_to_all(value, axis, split_axis=0, concat_axis=0, tiled=True)  53.9 us
    unnamed x20, local copies, waits for them, and re-layouts  6.1 us
    pallas_call x1, Pallas kernels, on_device(): call(adam, [(rows, f32), (rows, f32), (rows, f32), ((8, 2, 16, 512), f32)...  4.1 us
    pallas_call x1, Pallas kernels, on_device(): call(grad_kernel, [((8, 2, 16, 512), f32), ((2, 512, 512), bf16), ((2, 51...  3.46 us

profile of v1, /device:TPU:0, one launch (start us, length us, event | category | flops | bytes accessed | tf_op | source)
XLA Modules:
  0.0 70.1 jit_solution(5377082091733558656)
XLA Ops:
  0.6 0.0 copy-start
  0.6 0.0 copy-start.4
  0.7 0.8 %copy-done.4 = s32[2,8,512]{2,1,0:T(8,128)S(1)} copy-done((s32[2,8,512]{2,1,0:T(8,128)S(1)}, s32[2,8,512]{2,1,0:T(8,128)}, u32[]{:S(2)}) %copy-start.4) | copy-done | bytes 32792
  1.5 0.0 copy-start.5
  1.5 0.7 %copy-done.5 = f32[2,4,512]{2,1,0:T(4,128)S(1)} copy-done((f32[2,4,512]{2,1,0:T(4,128)S(1)}, f32[2,4,512]{2,1,0:T(4,128)}, u32[]{:S(2)}) %copy-start.5) | copy-done | bytes 16408
  2.2 0.0 copy-start.6
  2.2 0.7 %copy-done.6 = f32[2,3,512]{2,0,1:T(2,128)S(1)} copy-done((f32[2,3,512]{2,0,1:T(2,128)S(1)}, f32[2,3,512]{2,0,1:T(2,128)}, u32[]{:S(2)}) %copy-start.6) | copy-done | bytes 12312
  2.9 0.7 copy-done.9
  3.6 0.1 shard_map.129
  3.7 15.5 %all_to_all.20.recv_ref = f32[16,8,128]{2,1,0:T(8,128)S(1)} all-to-all(f32[16,8,128]{2,1,0:T(8,128)S(1)} %shard_map.129), channel_id=1, replica_groups=mesh['table'=8,'ray'=16] {'ray'}, dimensions={0} | all-to-all | bytes 131072 | tf_op jit(solution)/shard_map/all_to_all | solution.py:213
  19.2 3.5 %shard_map.130 = (f32[8,2,16,512]{3,2,1,0:T(8,128)S(1)}, bf16[2,512,512]{2,1,0:T(8,128)(2,1)S(1)}, bf16[2,512,512]{2,1,0:T(8,128)(2,1)S(1)}, s32[2,512]{1,0:T(2,128)S(1)}) custom-call(f32[16,8,128]{2,1,0:T(8,128)S(1)} %all_to_all.20.recv_ref), custom_call_target="tpu_custom_call" | custom-call | tf_op jit(solution)/shard_map/pallas_call | solution.py:244
  22.7 0.0 copy-start.3
  22.7 14.6 %all_to_all.21.refs_1_ = f32[8,2,16,512]{3,2,1,0:T(8,128)S(1)} all-to-all(f32[8,2,16,512]{3,2,1,0:T(8,128)S(1)} %get-tuple-element.12), channel_id=1, replica_groups=mesh['table'=8,'ray'=16] {'table'}, dimensions={0} | all-to-all | bytes 1048576 | tf_op jit(solution)/shard_map/all_to_all | solution.py:213
  37.3 0.0 copy-done
  37.3 0.0 copy-done.3
  37.3 1.2 %copy-done.1 = f32[2,64,4,512]{3,2,1,0:T(4,128)S(1)} copy-done((f32[2,64,4,512]{3,2,1,0:T(4,128)S(1)}, f32[2,64,4,512]{3,2,1,0:T(4,128)}, u32[]{:S(2)}) %copy-start.1) | copy-done | bytes 1048600
  38.5 1.2 %copy-done.2 = f32[2,64,4,512]{3,2,1,0:T(4,128)S(1)} copy-done((f32[2,64,4,512]{3,2,1,0:T(4,128)S(1)}, f32[2,64,4,512]{3,2,1,0:T(4,128)}, u32[]{:S(2)}) %copy-start.2) | copy-done | bytes 1048600
  39.7 4.1 %shard_map.131 = (f32[128,16,128]{2,1,0:T(8,128)}, f32[128,16,128]{2,1,0:T(8,128)}, f32[128,16,128]{2,1,0:T(8,128)}, f32[8,2,16,512]{3,2,1,0:T(8,128)S(1)}) custom-call(s32[64,128]{1,0:T(8,128)S(1)} %bitcast.38, f32[8,2,16,512]{3,2,1,0:T(8,128)S(1)} %all_to_all.21.refs_1_, f32[128,16,128]{2,1,0:T(8,128)S(1)} %bitcast.35, f32[128,16,128]{2,1,0:T(8,128)S(1)} %bitcast.36, ...), custom_call_target="tpu_custom_call" | custom-call | tf_op jit(solution)/shard_map/pallas_call | solution.py:257
  43.8 12.9 %all_to_all.22.recv_ref = f32[8,2,16,512]{3,2,1,0:T(8,128)S(1)} all-to-all(f32[8,2,16,512]{3,2,1,0:T(8,128)S(1)} %get-tuple-element.16), channel_id=1, replica_groups=mesh['table'=8,'ray'=16] {'table'}, dimensions={0} | all-to-all | bytes 1048576 | tf_op jit(solution)/shard_map/all_to_all | solution.py:213
  56.7 0.0 copy-done.7
  56.7 0.7 copy-done.8
  57.4 1.1 %shard_map.132 = f32[16,8,128]{2,1,0:T(8,128)S(1)} custom-call(f32[8,2,16,512]{3,2,1,0:T(8,128)S(1)} %all_to_all.22.recv_ref, bf16[2,512,512]{2,1,0:T(8,128)(2,1)S(1)} %get-tuple-element.17.high_ref, bf16[2,512,512]{2,1,0:T(8,128)(2,1)S(1)} %get-tuple-element.18.low_ref, s32[2,512]{1,0:T(2,128)S(1)} %get-tuple-element.19.cand_ref, f32[8,64]{1,0:T(8,128)S(1)} %bitcast.40, ...), custom_call_target="tpu_custom_call" | custom-call | tf_op jit(solution)/shard_map/pallas_call | solution.py:264
  58.5 10.9 %all_to_all.23.recv_ref = f32[16,8,128]{2,1,0:T(8,128)S(1)} all-to-all(f32[16,8,128]{2,1,0:T(8,128)S(1)} %shard_map.132), channel_id=1, replica_groups=mesh['table'=8,'ray'=16] {'ray'}, dimensions={0} | all-to-all | bytes 131072 | tf_op jit(solution)/shard_map/all_to_all | solution.py:213
  69.4 0.7 %shard_map.133 = f32[16,512]{1,0:T(8,128)} custom-call(f32[16,8,128]{2,1,0:T(8,128)S(1)} %all_to_all.23.recv_ref), custom_call_target="tpu_custom_call" | custom-call | tf_op jit(solution)/shard_map/pallas_call | solution.py:268
  (5 shorter events, 0.0 us)
Async XLA Ops:
  0.6 36.7 %copy-start = (f32[2,64,4,512]{3,2,1,0:T(4,128)S(1)}, f32[2,64,4,512]{3,2,1,0:T(4,128)}, u32[]{:S(2)}) copy-start(f32[2,64,4,512]{3,2,1,0:T(4,128)} %param.10) | copy-start | bytes 3145732
  0.6 0.8 %copy-start.4 = (s32[2,8,512]{2,1,0:T(8,128)S(1)}, s32[2,8,512]{2,1,0:T(8,128)}, u32[]{:S(2)}) copy-start(s32[2,8,512]{2,1,0:T(8,128)} %corners_ref.1) | copy-start | bytes 98308
  1.5 0.7 %copy-start.5 = (f32[2,4,512]{2,1,0:T(4,128)S(1)}, f32[2,4,512]{2,1,0:T(4,128)}, u32[]{:S(2)}) copy-start(f32[2,4,512]{2,1,0:T(4,128)} %cot_ref.1) | copy-start | bytes 49156
  2.2 0.7 %copy-start.6 = (f32[2,3,512]{2,0,1:T(2,128)S(1)}, f32[2,3,512]{2,0,1:T(2,128)}, u32[]{:S(2)}) copy-start(f32[2,3,512]{2,0,1:T(2,128)} %param.16) | copy-start | bytes 36868
  2.9 0.7 copy-start.9
  22.7 14.6 %copy-start.3 = (s32[8,2,128,4]{2,3,1,0:T(4,128)S(1)}, s32[8,2,128,4]{2,3,1,0:T(4,128)}, u32[]{:S(2)}) copy-start(s32[8,2,128,4]{2,3,1,0:T(4,128)} %param.13) | copy-start | bytes 98308
  37.3 1.2 %copy-start.1 = (f32[2,64,4,512]{3,2,1,0:T(4,128)S(1)}, f32[2,64,4,512]{3,2,1,0:T(4,128)}, u32[]{:S(2)}) copy-start(f32[2,64,4,512]{3,2,1,0:T(4,128)} %param.11) | copy-start | bytes 3145732
  38.5 1.2 %copy-start.2 = (f32[2,64,4,512]{3,2,1,0:T(4,128)S(1)}, f32[2,64,4,512]{3,2,1,0:T(4,128)}, u32[]{:S(2)}) copy-start(f32[2,64,4,512]{3,2,1,0:T(4,128)} %param.12) | copy-start | bytes 3145732
  43.8 12.9 %copy-start.7 = (f32[16,64]{1,0:T(8,128)S(1)}, f32[16,64]{1,0:T(8,128)}, u32[]{:S(2)}) copy-start(f32[16,64]{1,0:T(8,128)} %wout_ref.1) | copy-start | bytes 12292
  56.7 0.7 copy-start.8

commit v2 on v1

--- a/solution.py
+++ b/solution.py
@@ -12,7 +12,7 @@
 
 LANES = 128
 RUN = 32
-VMEM_LIMIT = 48 << 20
+VMEM_LIMIT = 24 << 20
 
 
 def block_transpose(pieces):
@@ -34,7 +34,14 @@
     return high, low
 
 
-def pack_kernel(slot_ref, corners_ref, fractions_ref, cot_ref, out_ref):
+def pack_kernel(slot_hbm, corners_hbm, fractions_hbm, cot_hbm, out_ref, slot_ref, corners_ref, fractions_ref, cot_ref, sems):
+    sources = (slot_hbm, corners_hbm, fractions_hbm, cot_hbm)
+    targets = (slot_ref, corners_ref, fractions_ref, cot_ref)
+    copies = [pltpu.make_async_copy(x, y, sems.at[n]) for n, (x, y) in enumerate(zip(sources, targets))]
+    for copy in copies:
+        copy.start()
+    for copy in copies:
+        copy.wait()
     groups = [corners_ref[0].astype(jnp.float32), corners_ref[1].astype(jnp.float32)]
     for level in range(2):
         rows = [slot_ref[level : level + 1, :].astype(jnp.float32)]
@@ -47,7 +54,15 @@
             out_ref[4 * v + p] = value
 
 
-def grad_kernel(recv_ref, part_ref, high_ref, low_ref, cand_ref, corner_s, aux_s):
+def grad_kernel(
+    recv_ref, table_hbm, m1_hbm, m2_hbm, win_hbm, wout_hbm,
+    part_ref, high_ref, low_ref, cand_ref, table_ref, m1_ref, m2_ref, win_ref, wout_ref, corner_s, aux_s, sems,
+):
+    sources = (table_hbm, m1_hbm, m2_hbm, win_hbm, wout_hbm)
+    targets = (table_ref, m1_ref, m2_ref, win_ref, wout_ref)
+    copies = [pltpu.make_async_copy(x, y, sems.at[n]) for n, (x, y) in enumerate(zip(sources, targets))]
+    for copy in copies:
+        copy.start()
     for v in range(4):
         lanes = slice(v * LANES, (v + 1) * LANES)
         rows = block_transpose([recv_ref[4 * v + p] for p in range(4)])
@@ -98,53 +113,67 @@
         part = both[:128] + both[128:] + rest
         for t in range(8):
             part_ref[t, level] = part[16 * t : 16 * t + 16]
-
-
-def adam_kernel(ids_ref, recv_ref, table_ref, m1_ref, m2_ref, tnew_ref, m1new_ref, m2new_ref, pick_ref, grad_s, *, ray):
+    for copy in copies:
+        copy.wait()
+
+
+def moments(grad, m1, m2):
+    first = beta_one * m1 + (1.0 - beta_one) * grad
+    second = beta_two * m2 + (1.0 - beta_two) * grad * grad
+    return first, second
+
+
+def stepped(table, first, second):
+    return table - learn_rate * first / (jnp.sqrt(second) + adam_eps)
+
+
+def listed_kernel(ids_ref, recv_ref, table_ref, m1_ref, m2_ref, pick_ref, grad_ref, *, ray):
     owner = lax.axis_index("table") * ray + lax.axis_index("ray")
     sub = lax.broadcasted_iota(jnp.int32, (8, LANES), 0) < 4
-    grad_s[...] = jnp.zeros_like(grad_s)
+    grad_ref[...] = jnp.zeros_like(grad_ref)
+    blocks = {}
+    for g in range(8):
+        for level in range(2):
+            for slot in range(4):
+                blocks[g, level, slot] = level * 64 + ids_ref[(g * 2 + level) * 4 + slot, owner]
     for g in range(8):
         for level in range(2):
             for pair in range(2):
-                a = [recv_ref[g, level, 8 * pair : 8 * pair + 8, c * LANES : (c + 1) * LANES] for c in range(4)]
+                rows = slice(8 * pair, 8 * pair + 8)
+                a = [recv_ref[g, level, rows, c * LANES : (c + 1) * LANES] for c in range(4)]
                 for half in range(2):
-                    row = (g * 2 + level) * 4 + 2 * pair + half
-                    block = level * 64 + ids_ref[row, owner]
+                    block = blocks[g, level, 2 * pair + half]
                     for k in range(2):
                         x, y = a[2 * k], a[2 * k + 1]
                         if half == 0:
                             value = jnp.where(sub, x, pltpu.roll(y, 4, 0))
                         else:
                             value = jnp.where(sub, pltpu.roll(x, 4, 0), y)
-                        grad_s[block, 8 * k : 8 * k + 8, :] += value
-
-    def update(step, carry):
-        at = pl.ds(step * 4, 4)
-        grad = grad_s[at]
-        first = beta_one * m1_ref[at] + (1.0 - beta_one) * grad
-        second = beta_two * m2_ref[at] + (1.0 - beta_two) * grad * grad
-        m1new_ref[at] = first
-        m2new_ref[at] = second
-        tnew_ref[at] = table_ref[at] - learn_rate * first / (jnp.sqrt(second) + adam_eps)
-        return carry
-
-    lax.fori_loop(0, 32, update, 0)
+                        grad_ref[block, 8 * k : 8 * k + 8, :] += value
+
+    def new_rows(block, k):
+        rows = slice(8 * k, 8 * k + 8)
+        first, second = moments(grad_ref[block, rows], m1_ref[block, rows], m2_ref[block, rows])
+        return stepped(table_ref[block, rows], first, second)
+
     for g in range(8):
         for level in range(2):
             for pair in range(2):
-                row = (g * 2 + level) * 4 + 2 * pair
-                one = level * 64 + ids_ref[row, owner]
-                two = level * 64 + ids_ref[row + 1, owner]
+                rows = slice(8 * pair, 8 * pair + 8)
                 for k in range(2):
-                    x = tnew_ref[one, 8 * k : 8 * k + 8, :]
-                    y = tnew_ref[two, 8 * k : 8 * k + 8, :]
-                    pick_ref[g, level, 8 * pair : 8 * pair + 8, 2 * k * LANES : (2 * k + 1) * LANES] = jnp.where(
-                        sub, x, pltpu.roll(y, 4, 0)
-                    )
-                    pick_ref[g, level, 8 * pair : 8 * pair + 8, (2 * k + 1) * LANES : (2 * k + 2) * LANES] = jnp.where(
-                        sub, pltpu.roll(x, 4, 0), y
-                    )
+                    x = new_rows(blocks[g, level, 2 * pair], k)
+                    y = new_rows(blocks[g, level, 2 * pair + 1], k)
+                    left = slice(2 * k * LANES, (2 * k + 1) * LANES)
+                    right = slice((2 * k + 1) * LANES, (2 * k + 2) * LANES)
+                    pick_ref[g, level, rows, left] = jnp.where(sub, x, pltpu.roll(y, 4, 0))
+                    pick_ref[g, level, rows, right] = jnp.where(sub, pltpu.roll(x, 4, 0), y)
+
+
+def dense_kernel(grad_ref, table_ref, m1_ref, m2_ref, tnew_ref, m1new_ref, m2new_ref):
+    first, second = moments(grad_ref[...], m1_ref[...], m2_ref[...])
+    m1new_ref[...] = first
+    m2new_ref[...] = second
+    tnew_ref[...] = stepped(table_ref[...], first, second)
 
 
 def lookup_kernel(recv_ref, high_ref, low_ref, cand_ref, win_ref, wout_ref, out_ref):
@@ -194,11 +223,12 @@
         out_ref[8:, v * LANES : (v + 1) * LANES] = lower
 
 
-def call(kernel, outs, scratch=(), in_specs=None):
+def call(kernel, outs, scratch=(), in_specs=None, **extra):
     vmem = pl.BlockSpec(memory_space=pltpu.VMEM)
     shapes = [jax.ShapeDtypeStruct(s, d) for s, d in outs]
     single = len(shapes) == 1
-    extra = {} if in_specs is None else {"in_specs": in_specs}
+    if in_specs is not None:
+        extra["in_specs"] = in_specs
     return pl.pallas_call(
         kernel,
         out_shape=shapes[0] if single else shapes,
@@ -207,6 +237,10 @@
         compiler_params=pltpu.CompilerParams(vmem_limit_bytes=VMEM_LIMIT),
         **extra,
     )
+
+
+def in_hbm(*arrays):
+    return [pltpu.with_memory_space_constraint(array, pltpu.HBM) for array in arrays]
 
 
 def exchange(value, axis):
@@ -237,33 +271,62 @@
 ):
     f32, bf16, i32 = jnp.float32, jnp.bfloat16, jnp.int32
     ray = lax.axis_size("ray")
-    packed = call(pack_kernel, [((16, 8, LANES), f32)])(
-        sample_slot, corners, fractions.transpose(1, 0, 2), feat_cot
-    )
+    vmem = pl.BlockSpec(memory_space=pltpu.VMEM)
+    hbm = pl.BlockSpec(memory_space=pltpu.HBM)
+    packed = call(
+        pack_kernel,
+        [((16, 8, LANES), f32)],
+        [
+            pltpu.VMEM((2, 512), i32),
+            pltpu.VMEM((2, 8, 512), i32),
+            pltpu.VMEM((3, 2, 512), f32),
+            pltpu.VMEM((2, 4, 512), f32),
+            pltpu.SemaphoreType.DMA((4,)),
+        ],
+        [hbm] * 4,
+    )(*in_hbm(sample_slot, corners, fractions.transpose(1, 0, 2), feat_cot))
     samples = exchange(packed, "ray")
-    part, high, low, cand = call(
+    rows = (128, 16, LANES)
+    part, high, low, cand, table_v, m1_v, m2_v, win_v, wout_v = call(
         grad_kernel,
-        [((8, 2, 16, 512), f32), ((2, 512, 512), bf16), ((2, 512, 512), bf16), ((2, 512), i32)],
-        [pltpu.VMEM((2, 8, 512), i32), pltpu.VMEM((2, 8, 512), f32)],
-    )(samples)
+        [
+            ((8, 2, 16, 512), f32),
+            ((2, 512, 512), bf16),
+            ((2, 512, 512), bf16),
+            ((2, 512), i32),
+            (rows, f32),
+            (rows, f32),
+            (rows, f32),
+            ((8, 64), f32),
+            ((16, 64), f32),
+        ],
+        [pltpu.VMEM((2, 8, 512), i32), pltpu.VMEM((2, 8, 512), f32), pltpu.SemaphoreType.DMA((5,))],
+        [vmem] + [hbm] * 5,
+    )(samples, *in_hbm(rows_of(table), rows_of(moment1), rows_of(moment2), weight_in.T, weight_out))
     received = exchange(part, "table")
     ids = block_ids.transpose(0, 1, 3, 2).reshape(64, 128)
-    vmem = pl.BlockSpec(memory_space=pltpu.VMEM)
-    rows = (128, 16, LANES)
-
-    def adam(*refs):
-        adam_kernel(*refs, ray=ray)
-
-    tnew, m1new, m2new, picked = call(
-        adam,
-        [(rows, f32), (rows, f32), (rows, f32), ((8, 2, 16, 512), f32)],
-        [pltpu.VMEM(rows, f32)],
+
+    def listed(*refs):
+        listed_kernel(*refs, ray=ray)
+
+    picked, grad = call(
+        listed,
+        [((8, 2, 16, 512), f32), (rows, f32)],
+        (),
         [pl.BlockSpec(memory_space=pltpu.SMEM)] + [vmem] * 4,
-    )(ids, received, rows_of(table), rows_of(moment1), rows_of(moment2))
+    )(*in_hbm(ids), received, table_v, m1_v, m2_v)
     returned = exchange(picked, "table")
-    sent = call(lookup_kernel, [((16, 8, LANES), f32)])(
-        returned, high, low, cand, weight_in.T, weight_out
-    )
+    step = pl.BlockSpec((16, 16, LANES), lambda i: (i, 0, 0))
+    tnew, m1new, m2new = pl.pallas_call(
+        dense_kernel,
+        grid=(8,),
+        in_specs=[step] * 4,
+        out_specs=[step] * 3,
+        out_shape=[jax.ShapeDtypeStruct(rows, f32)] * 3,
+        compiler_params=pltpu.CompilerParams(vmem_limit_bytes=VMEM_LIMIT),
+        cost_estimate=pl.CostEstimate(flops=20 << 20, bytes_accessed=7 << 20, transcendentals=0),
+    )(grad, *in_hbm(rows_of(table), rows_of(moment1), rows_of(moment2)))
+    sent = call(lookup_kernel, [((16, 8, LANES), f32)])(returned, high, low, cand, win_v, wout_v)
     back = exchange(sent, "ray")
     mlp_out = call(unpack_kernel, [((16, 512), f32)])(back)
     shape = table.shape

time: 70.7 us -> 63.9 us (0.904)
  blocking collectives: 53.9 us -> 42.9 us
  local copies, waits for them, and re-layouts: 6.1 us -> 0 us
  Pallas kernels: 9.48 us -> 15 us
  starting transfers between devices: 0 us -> 3.49 us
  waiting for transfers between devices: 0 us -> 1.33 us
    all_to_all x4 -> x3, blocking collectives: 53.9 us -> 42.9 us  [exchange(): return lax.all_to_all(value, axis, split_axis=0, concat_axis=0, tiled=True)]
    unnamed x20 -> x0, local copies, waits for them, and re-layouts: 6.1 us -> none
    pallas_call x2 -> x3, Pallas kernels: 4.21 us -> 9.07 us  [the longest x1 6.28 us: on_device(): pl.pallas_call(dense_kernel, grid=(8,), in_specs=[step] * 4, out_specs=[s...]
    all_to_all x0 -> x1, starting transfers between devices: none -> 3.49 us  [exchange(): return lax.all_to_all(value, axis, split_axis=0, concat_axis=0, tiled=True)]
    all_to_all x0 -> x1, waiting for transfers between devices: none -> 1.33 us  [exchange(): return lax.all_to_all(value, axis, split_axis=0, concat_axis=0, tiled=True)]
  transfers between devices with their start and end apart: 0 -> 1, of which waited for: 0 -> 1; matrix products, arithmetic and copies ran while one was open for 0% -> 0% of each run, Pallas kernels for 0% -> 10%
where the time goes in v2:
time: 63.9 us; the launch traced here: 63.4 us
  blocking collectives  42.9 us (67%)
  Pallas kernels  15 us (23%)
  starting transfers between devices  3.49 us (5%)
  waiting for transfers between devices  1.33 us (2%)
  between operations  0.67 us (1%)
    all_to_all x3, blocking collectives, exchange(): return lax.all_to_all(value, axis, split_axis=0, concat_axis=0, tiled=True)  42.9 us
    pallas_call x1, Pallas kernels, on_device(): pl.pallas_call(dense_kernel, grid=(8,), in_specs=[step] * 4, out_specs=[s...  6.28 us
    pallas_call x1, Pallas kernels, on_device(): call(grad_kernel, [((8, 2, 16, 512), f32), ((2, 512, 512), bf16), ((2, 51...  3.53 us
    all_to_all x1, starting transfers between devices, exchange(): return lax.all_to_all(value, axis, split_axis=0, concat_axis=0, tiled=True)  3.49 us
    pallas_call x1, Pallas kernels, on_device(): call(listed, [((8, 2, 16, 512), f32), (rows, f32)], (), [pl.BlockSpec(mem...  1.86 us
    pallas_call x1, Pallas kernels, on_device(): call(lookup_kernel, [((16, 8, LANES), f32)])  1.71 us
    all_to_all x1, waiting for transfers between devices, exchange(): return lax.all_to_all(value, axis, split_axis=0, concat_axis=0, tiled=True)  1.33 us
  transfers between devices with their start and end apart: 1, of which 1 were waited for; matrix products, arithmetic and copies ran while one was open for 0% of the time, Pallas kernels for 10%

profile of v2, /device:TPU:0, one launch (start us, length us, event | category | flops | bytes accessed | tf_op | source)
XLA Modules:
  0.0 63.4 jit_solution(12305433292814938239)
XLA Ops:
  0.6 0.9 %shard_map.129 = f32[16,8,128]{2,1,0:T(8,128)S(1)} custom-call(s32[2,512]{1,0:T(2,128)} %slot_hbm.1, s32[2,8,512]{2,1,0:T(8,128)} %corners_hbm.1, f32[3,2,512]{2,1,0:T(2,128)} %bitcast.42, f32[2,4,512]{2,1,0:T(4,128)} %cot_hbm.1), custom_call_target="tpu_custom_call" | custom-call | tf_op jit(solution)/shard_map/pallas_call | solution.py:276
  1.6 15.5 %all_to_all.20.recv_ref = f32[16,8,128]{2,1,0:T(8,128)S(1)} all-to-all(f32[16,8,128]{2,1,0:T(8,128)S(1)} %shard_map.129), channel_id=1, replica_groups=mesh['table'=8,'ray'=16] {'ray'}, dimensions={0} | all-to-all | bytes 131072 | tf_op jit(solution)/shard_map/all_to_all | solution.py:247
  17.0 3.5 %shard_map.130 = (f32[8,2,16,512]{3,2,1,0:T(8,128)S(1)}, bf16[2,512,512]{2,1,0:T(8,128)(2,1)S(1)}, bf16[2,512,512]{2,1,0:T(8,128)(2,1)S(1)}, s32[2,512]{1,0:T(2,...) custom-call(f32[16,8,128]{2,1,0:T(8,128)S(1)} %all_to_all.20.recv_re, ...), custom_call_target="tpu_custom_call" | custom-call | tf_op jit(solution)/shard_map/pallas_call | solution.py:290
  20.6 14.6 %all_to_all.21.refs_1_ = f32[8,2,16,512]{3,2,1,0:T(8,128)S(1)} all-to-all(f32[8,2,16,512]{3,2,1,0:T(8,128)S(1)} %get-tuple-element.18), channel_id=1, replica_groups=mesh['table'=8,'ray'=16] {'table'}, dimensions={0} | all-to-all | bytes 1048576 | tf_op jit(solution)/shard_map/all_to_all | solution.py:247
  35.2 1.9 %shard_map.131 = (f32[8,2,16,512]{3,2,1,0:T(8,128)S(1)}, f32[128,16,128]{2,1,0:T(8,128)S(1)}) custom-call(s32[64,128]{1,0:T(8,128)} %bitcast.41, f32[8,2,16,512]{3,2,1,0:T(8,128)S(1)} %all_to_all.21.refs_1_, f32[128,16,128]{2,1,0:T(8,128)S(1)} %get-tuple-element.19.refs_2_, f32[128,16,128]{2,1,0:T(8,128)S(1)} %get-tuple-element.20.refs_3_, ...), custom_call_target="tpu_custom_call" | custom-call | tf_op jit(solution)/shard_map/pallas_call | solution.py:312
  37.1 12.8 %all_to_all.22.recv_ref = f32[8,2,16,512]{3,2,1,0:T(8,128)S(1)} all-to-all(f32[8,2,16,512]{3,2,1,0:T(8,128)S(1)} %get-tuple-element.26), channel_id=1, replica_groups=mesh['table'=8,'ray'=16] {'table'}, dimensions={0} | all-to-all | bytes 1048576 | tf_op jit(solution)/shard_map/all_to_all | solution.py:247
  49.8 1.7 %shard_map.133 = f32[16,8,128]{2,1,0:T(8,128)} custom-call(f32[8,2,16,512]{3,2,1,0:T(8,128)S(1)} %all_to_all.22.recv_ref, bf16[2,512,512]{2,1,0:T(8,128)(2,1)S(1)} %get-tuple-element.27.high_ref, bf16[2,512,512]{2,1,0:T(8,128)(2,1)S(1)} %get-tuple-element.28.low_ref, s32[2,512]{1,0:T(2,128)S(1)} %get-tuple-element.29.cand_ref, ...), custom_call_target="tpu_custom_call" | custom-call | tf_op jit(solution)/shard_map/pallas_call | solution.py:329
  51.5 3.5 %all-to-all-start.3 = ((f32[16,8,128]{2,1,0:T(8,128)}), f32[16,8,128]{2,1,0:T(8,128)S(1)}, u32[]{:S(2)}, u32[]{:S(2)}) async-start(f32[16,8,128]{2,1,0:T(8,128)} %shard_map.133), calls=%async_computation.3 | async-start | bytes 131072 | tf_op jit(solution)/shard_map/all_to_all | solution.py:247
  55.0 6.3 %shard_map.132 = (f32[128,16,128]{2,1,0:T(8,128)}, f32[128,16,128]{2,1,0:T(8,128)}, f32[128,16,128]{2,1,0:T(8,128)}) custom-call(f32[128,16,128]{2,1,0:T(8,128)S(1)} %get-tuple-element.22.grad_ref, f32[128,16,128]{2,1,0:T(8,128)} %bitcast.36, f32[128,16,128]{2,1,0:T(8,128)} %bitcast.38, f32[128,16,128]{2,1,0:T(8,128)} %bitcast.40), custom_call_target="tpu_custom_call" | custom-call | flops 20971520 | bytes 7340032 | tf_op jit(solution)/shard_map/pallas_call | solution.py:320
  61.3 1.3 %all-to-all-done.3.recv_ref = f32[16,8,128]{2,1,0:T(8,128)S(1)} async-done(((f32[16,8,128]{2,1,0:T(8,128)}), f32[16,8,128]{2,1,0:T(8,128)S(1)}, u32[]{:S(2)}, u32[]{:S(2)}) %all-to-all-start.3) | async-done | bytes 65568 | tf_op jit(solution)/shard_map/all_to_all | solution.py:247
  62.6 0.7 %shard_map.134 = f32[16,512]{1,0:T(8,128)} custom-call(f32[16,8,128]{2,1,0:T(8,128)S(1)} %all-to-all-done.3.recv_ref), custom_call_target="tpu_custom_call" | custom-call | tf_op jit(solution)/shard_map/pallas_call | solution.py:331
Async XLA Ops:
  51.5 11.1 %all-to-all-start.3 = ((f32[16,8,128]{2,1,0:T(8,128)}), f32[16,8,128]{2,1,0:T(8,128)S(1)}, u32[]{:S(2)}, u32[]{:S(2)}) async-start(f32[16,8,128]{2,1,0:T(8,128)} %shard_map.133), calls=%async_computation.3 | async-start | bytes 131072 | tf_op jit(solution)/shard_map/all_to_all | solution.py:247

commit v3 on v0

v3 whole, which is shorter than its diff:
```python
import jax
import jax.numpy as jnp
from jax import lax
from jax.experimental import pallas as pl
from jax.experimental.pallas import tpu as pltpu
from jax.sharding import PartitionSpec as P

beta_one = 0.9
beta_two = 0.99
learn_rate = 0.01
adam_eps = 1e-15

LANES = 128
RUN = 32
VMEM_LIMIT = 40 << 20
f32, bf16, i32 = jnp.float32, jnp.bfloat16, jnp.int32


def iota(shape, axis):
    return lax.broadcasted_iota(i32, shape, axis)


def lane_blocks(pieces):
    group = iota(pieces[0].shape, 1) // RUN
    results = []
    for q in range(4):
        value = pieces[q]
        for p in range(4):
            if p != q:
                moved = pltpu.roll(pieces[p], (RUN * (p - q)) % LANES, 1)
                value = jnp.where(group == p, moved, value)
        results.append(value)
    return results


def tile_blocks(value):
    shift = (iota((8, LANES), 0) // 2 - iota((8, LANES), 1) // RUN) & 3
    result = value
    for d in range(1, 4):
        moved = pltpu.roll(pltpu.roll(value, 2 * d, 0), LANES - RUN * d, 1)
        result = jnp.where(shift == d, moved, result)
    return result


def start_all(sources, targets, sems):
    copies = [pltpu.make_async_copy(x, y, sems.at[n]) for n, (x, y) in enumerate(zip(sources, targets))]
    for copy in copies:
        copy.start()
    return copies


def wait_all(copies):
    for copy in copies:
        copy.wait()


def pack_kernel(slot_hbm, corners_hbm, fractions_hbm, cot_hbm, out_ref, slot_ref, corners_ref, fractions_ref, cot_ref, sems):
    wait_all(
        start_all(
            (slot_hbm, corners_hbm, fractions_hbm, cot_hbm), (slot_ref, corners_ref, fractions_ref, cot_ref), sems
        )
    )
    groups = [corners_ref[0].astype(f32), corners_ref[1].astype(f32)]
    for level in range(2):
        rows = [slot_ref[level : level + 1, :].astype(f32)]
        rows += [fractions_ref[d, level : level + 1, :] for d in range(3)]
        rows += [cot_ref[level]]
        groups.append(jnp.concatenate(rows, axis=0))
    for v in range(4):
        lanes = slice(v * LANES, (v + 1) * LANES)
        for p, value in enumerate(lane_blocks([g[:, lanes] for g in groups])):
            for t in range(8):
                out_ref[16 * t + 4 * v + p] = value


def gather_lanes(value, index):
    return jnp.take_along_axis(value, index, axis=1, mode="promise_in_bounds")


def owner_kernel(
    ids_ref, recv_ref, table_hbm, m1_hbm, m2_hbm, win_hbm, wout_hbm,
    tnew_hbm, m1new_hbm, m2new_hbm, out_ref, win_ref, wout_ref,
    table_ref, m1_ref, m2_ref, grad_ref, corner_ref, aux_ref, back_ref, slots_ref, hot_ref, hat_ref, key_ref,
    found_ref, result_ref, sems,
):
    loads = start_all(
        (table_hbm, m1_hbm, m2_hbm, win_hbm, wout_hbm), (table_ref, m1_ref, m2_ref, win_ref, wout_ref), sems
    )
    mine = lax.axis_index("table")
    owner = mine * lax.axis_size("ray") + lax.axis_index("ray")
    sub = iota((8, LANES), 0)
    parity = sub // 4
    lane16 = iota((16, LANES), 1)

    grad_ref[...] = jnp.zeros_like(grad_ref)
    result_ref[...] = jnp.zeros_like(result_ref)

    def unpack(t, carry):
        for v in range(4):
            rows = lane_blocks([recv_ref[t * 16 + 4 * v + p] for p in range(4)])
            corner_ref[t, v] = rows[0]
            corner_ref[8 + t, v] = rows[1]
            aux_ref[t, v] = rows[2]
            aux_ref[8 + t, v] = rows[3]
        return carry

    lax.fori_loop(0, 8, unpack, 0, unroll=2)

    first_slot = (mine * 64).astype(f32)
    hits = []
    for v in range(4):
        slot = jnp.concatenate([aux_ref[lt, v, 0:1, :] for lt in range(16)], axis=0)
        hits.append(jnp.where((slot >= first_slot) & (slot < first_slot + 64.0), 1.0, 0.0))
    row, column = iota((LANES, 2 * LANES), 0), iota((LANES, 2 * LANES), 1)
    upper = jnp.where(row <= column, 1.0, 0.0).astype(bf16)
    counts = jnp.dot(jnp.concatenate(hits, axis=0).astype(bf16), upper, preferred_element_type=f32).astype(i32)
    through = [counts[16 * v : 16 * v + 16, :LANES] for v in range(4)]
    totals = [counts[16 * v : 16 * v + 16, LANES:] for v in range(4)]
    before = [jnp.zeros_like(totals[0])]
    for v in range(4):
        before.append(before[v] + totals[v])
    passes = (jnp.max(before[4]) + (LANES - 1)) // LANES

    def locate(step):
        for v in range(4):
            rank = before[v] + through[v] - 1 - step * LANES
            inside = (hits[v] > 0.5) & (rank >= 0) & (rank < LANES)
            slots_ref[v] = jnp.where(inside, rank, -1)
            wanted = lane16 + step * LANES - before[v]
            place = jnp.zeros_like(wanted)
            for jump in (64, 32, 16, 8, 4, 2, 1):
                probe = gather_lanes(through[v], place + (jump - 1))
                place = jnp.where(probe <= wanted, place + jump, place)
            back_ref[v] = jnp.where((wanted >= 0) & (wanted < totals[v]), place, -1)

    def compact(lt):
        corner = jnp.zeros((8, LANES), f32)
        aux = jnp.zeros((8, LANES), f32)
        for v in range(4):
            place = jnp.broadcast_to(back_ref[v, pl.ds(lt, 1), :], (8, LANES))
            index = jnp.maximum(place, 0)
            corner = jnp.where(place >= 0, gather_lanes(corner_ref[lt, v], index), corner)
            aux = jnp.where(place >= 0, gather_lanes(aux_ref[lt, v], index), aux)
        hat = None
        for d in range(3):
            f = jnp.broadcast_to(aux[1 + d : 2 + d], (8, LANES))
            factor = jnp.where((sub >> d) & 1 == 1, f, 1.0 - f)
            hat = factor if hat is None else hat * factor
        entry = corner.astype(i32)
        key = (aux[0:1].astype(i32) & 3) * 2 + ((entry >> 7) & 1)
        column = (entry & 127) | ((entry >> 8) << 7)
        hat_ref[lt] = hat
        key_ref[lt] = key
        entries = iota((256, LANES), 0)
        for c in range(8):
            hot = jnp.where(column[c : c + 1] == entries, 1.0, 0.0).astype(bf16)
            hot_ref[lt, :, c * LANES : (c + 1) * LANES] = hot
        return aux, hat, key

    def block_of(lt, slot):
        level, group = lt // 8, lt % 8
        return level * 64 + ids_ref[(group * 2 + level) * 4 + slot, owner]

    def accumulate(lt, carry):
        aux, hat, key = compact(lt)
        cot = jnp.where(sub < 4, pltpu.roll(aux, 4, 0), aux)
        columns = []
        for c in range(8):
            value = cot * hat[c : c + 1]
            high = value.astype(bf16).astype(f32)
            low = value - high
            masks = [jnp.broadcast_to(key[c : c + 1], (8, LANES)) == parity + 2 * i for i in range(4)]
            pieces = [jnp.where(m, high, 0.0) for m in masks] + [jnp.where(m, low, 0.0) for m in masks]
            columns.append(jnp.concatenate(pieces, axis=0).astype(bf16))
        both = lax.dot_general(
            jnp.concatenate(columns, axis=1), hot_ref[lt], (((1,), (1,)), ((), ())), preferred_element_type=f32
        )
        part = both[:32] + both[32:]
        for slot in range(4):
            block = block_of(lt, slot)
            for half in range(2):
                grad_ref[block, 8 * half : 8 * half + 8, :] += part[
                    8 * slot : 8 * slot + 8, half * LANES : (half + 1) * LANES
                ]
        return carry

    def gather_pass(step, carry):
        locate(step)
        lax.fori_loop(0, 16, accumulate, 0, unroll=2)
        return carry

    lax.fori_loop(0, passes, gather_pass, 0)
    wait_all(loads)

    def update(step, carry):
        at = pl.ds(step * 4, 4)
        grad = grad_ref[at]
        first = beta_one * m1_ref[at] + (1.0 - beta_one) * grad
        second = beta_two * m2_ref[at] + (1.0 - beta_two) * grad * grad
        m1_ref[at] = first
        m2_ref[at] = second
        table_ref[at] = table_ref[at] - learn_rate * first / (jnp.sqrt(second) + adam_eps)
        return carry

    lax.fori_loop(0, 32, update, 0)
    stores = start_all((table_ref, m1_ref, m2_ref), (tnew_hbm, m1new_hbm, m2new_hbm), sems)

    def look(lt, carry):
        blocks = [table_ref[block_of(lt, slot)] for slot in range(4)]
        rows = jnp.concatenate([jnp.concatenate([b[:8], b[8:]], axis=1) for b in blocks], axis=0)
        high = rows.astype(bf16)
        low = (rows - high.astype(f32)).astype(bf16)
        both = jnp.dot(jnp.concatenate([high, low], axis=0), hot_ref[lt], preferred_element_type=f32)
        seen = both[:32] + both[32:]
        hat, key = hat_ref[lt], key_ref[lt]
        total = jnp.zeros((8, LANES), f32)
        for c in range(8):
            own = jnp.broadcast_to(key[c : c + 1], (8, LANES))
            picked = jnp.zeros((8, LANES), f32)
            for i in range(4):
                picked = jnp.where(own == parity + 2 * i, seen[8 * i : 8 * i + 8, c * LANES : (c + 1) * LANES], picked)
            total = total + jnp.where((own & 1) == parity, picked, 0.0) * hat[c : c + 1]
        found_ref[lt] = total + pltpu.roll(total, 4, 0)
        return carry

    def spread(t, carry):
        value = jnp.where(sub < 4, found_ref[t], found_ref[8 + t])
        for v in range(4):
            zero = jnp.broadcast_to(slots_ref[v, pl.ds(t, 1), :], (8, LANES))
            one = jnp.broadcast_to(slots_ref[v, pl.ds(8 + t, 1), :], (8, LANES))
            place = jnp.where(sub < 4, zero, one)
            taken = gather_lanes(value, jnp.maximum(place, 0))
            result_ref[t * 4 + v] += jnp.where(place >= 0, taken, 0.0)
        return carry

    def look_pass(step, carry):
        @pl.when(passes > 1)
        def _():
            locate(step)

            def again(lt, inner):
                compact(lt)
                return inner

            lax.fori_loop(0, 16, again, 0)

        lax.fori_loop(0, 16, look, 0, unroll=2)
        lax.fori_loop(0, 8, spread, 0, unroll=2)
        return carry

    lax.fori_loop(0, passes, look_pass, 0)
    for m in range(32):
        out_ref[m] = tile_blocks(result_ref[m])
    wait_all(stores)


def network_kernel(recv_ref, win_ref, wout_ref, out_ref):
    columns = []
    for v in range(4):
        total = recv_ref[v]
        for t in range(1, 8):
            total = total + recv_ref[4 * t + v]
        columns.append(tile_blocks(total))
    encoded = jnp.concatenate(columns, axis=1)
    hidden = jnp.maximum(
        lax.dot_general(
            win_ref[...], encoded, (((0,), (0,)), ((), ())),
            precision=lax.Precision.HIGHEST, preferred_element_type=f32,
        ),
        0.0,
    )
    out_ref[...] = jnp.dot(wout_ref[...], hidden, precision=lax.Precision.HIGHEST, preferred_element_type=f32)


VMEM = pl.BlockSpec(memory_space=pltpu.VMEM)
HBM = pl.BlockSpec(memory_space=pltpu.HBM)
SMEM = pl.BlockSpec(memory_space=pltpu.SMEM)


def call(kernel, outs, in_specs, scratch=(), out_specs=None, **extra):
    return pl.pallas_call(
        kernel,
        out_shape=[jax.ShapeDtypeStruct(s, d) for s, d in outs],
        in_specs=in_specs,
        out_specs=[VMEM] * len(outs) if out_specs is None else out_specs,
        scratch_shapes=list(scratch),
        compiler_params=pltpu.CompilerParams(vmem_limit_bytes=VMEM_LIMIT),
        **extra,
    )


def in_hbm(*arrays):
    return [pltpu.with_memory_space_constraint(array, pltpu.HBM) for array in arrays]


def exchange(value):
    return lax.all_to_all(value, ("table", "ray"), split_axis=0, concat_axis=0, tiled=True)


def rows_of(array):
    levels, blocks = array.shape[:2]
    return array.reshape(levels, blocks, 4, 4, LANES).transpose(0, 1, 3, 2, 4).reshape(levels * blocks, 16, LANES)


def rows_back(array, shape):
    levels, blocks = shape[:2]
    return array.reshape(levels, blocks, 4, 4, LANES).transpose(0, 1, 3, 2, 4).reshape(shape)


def on_device(
    table,
    moment1,
    moment2,
    block_ids,
    sample_slot,
    corners,
    fractions,
    feat_cot,
    weight_in,
    weight_out,
):
    (packed,) = call(
        pack_kernel,
        [((128, 8, LANES), f32)],
        [HBM] * 4,
        [
            pltpu.VMEM((2, 512), i32),
            pltpu.VMEM((2, 8, 512), i32),
            pltpu.VMEM((3, 2, 512), f32),
            pltpu.VMEM((2, 4, 512), f32),
            pltpu.SemaphoreType.DMA((4,)),
        ],
    )(*in_hbm(sample_slot, corners, fractions.transpose(1, 0, 2), feat_cot))
    samples = exchange(packed)
    rows = (128, 16, LANES)
    ids = block_ids.transpose(0, 1, 3, 2).reshape(64, 128)
    tnew, m1new, m2new, found, win, wout = call(
        owner_kernel,
        [(rows, f32), (rows, f32), (rows, f32), ((32, 8, LANES), f32), ((8, 64), f32), ((16, 64), f32)],
        [SMEM, VMEM] + [HBM] * 5,
        [
            pltpu.VMEM(rows, f32),
            pltpu.VMEM(rows, f32),
            pltpu.VMEM(rows, f32),
            pltpu.VMEM(rows, f32),
            pltpu.VMEM((16, 4, 8, LANES), f32),
            pltpu.VMEM((16, 4, 8, LANES), f32),
            pltpu.VMEM((4, 16, LANES), i32),
            pltpu.VMEM((4, 16, LANES), i32),
            pltpu.VMEM((16, 256, 8 * LANES), bf16),
            pltpu.VMEM((16, 8, LANES), f32),
            pltpu.VMEM((16, 8, LANES), i32),
            pltpu.VMEM((16, 8, LANES), f32),
            pltpu.VMEM((32, 8, LANES), f32),
            pltpu.SemaphoreType.DMA((5,)),
        ],
        [HBM] * 3 + [VMEM] * 3,
    )(
        *in_hbm(ids),
        samples,
        *in_hbm(rows_of(table), rows_of(moment1), rows_of(moment2), weight_in.T, weight_out),
    )
    back = exchange(found.reshape(128, 2, LANES)).reshape(32, 8, LANES)
    (mlp_out,) = call(network_kernel, [((16, 512), f32)], [VMEM] * 3)(back, win, wout)
    shape = table.shape
    return (rows_back(tnew, shape), rows_back(m1new, shape), rows_back(m2new, shape), mlp_out)


def solution(mesh):
    in_specs = (
        P(None, ("table", "ray"), None, None),
        P(None, ("table", "ray"), None, None),
        P(None, ("table", "ray"), None, None),
        P(),
        P(None, ("table", "ray")),
        P(None, None, ("table", "ray")),
        P(None, None, ("table", "ray")),
        P(None, None, ("table", "ray")),
        P(),
        P(),
    )
    out_specs = (
        P(None, ("table", "ray"), None, None),
        P(None, ("table", "ray"), None, None),
        P(None, ("table", "ray"), None, None),
        P(None, ("table", "ray")),
    )
    return jax.shard_map(
        on_device, mesh=mesh, in_specs=in_specs, out_specs=out_specs, check_vma=False
    )
```

time: 378 us -> 54.6 us (0.14)
  waiting for transfers between devices: 155 us -> 0 us
  blocking collectives: 114 us -> 38.6 us
  local copies, waits for them, and re-layouts: 60.9 us -> 0 us
  matrix products: 25.7 us -> 0 us
  Pallas kernels: 0 us -> 14.4 us
  between operations: 14.3 us -> 0.65 us
  other arithmetic: 6.83 us -> 0 us
    unnamed x3 -> x0, waiting for transfers between devices: 86.1 us -> none
    all_to_all x2, blocking collectives: 114 us -> 38.6 us  [exchange(): lax.all_to_all(value, ('table', 'ray'), split_axis=0, concat_axis=0, tile...]
    all_gather x1 -> x0, waiting for transfers between devices: 68.5 us -> none  [on_device(): fetched = lax.all_gather(returned, 'ray', axis=2, tiled=True)]
    reshape x10 -> x0, local copies, waits for them, and re-layouts: 34.4 us -> none  [the longest x2 20.1 us: on_device(): partial_value.reshape(levels, ray_size, table_size, slot_count, 4, block_...]
    dot_general x5 -> x0, matrix products: 25.7 us -> none  [the longest x1 12.6 us: on_device(): jnp.einsum('lrje,lrce->lrjc', spread, run_tables, precision=lax.Precision...]
    pallas_call x0 -> x3, Pallas kernels: none -> 14.4 us  [the longest x1 12.3 us: on_device(): call(owner_kernel, [(rows, f32), (rows, f32), (rows, f32), ((32, 8, LANES...]
    all_to_all x1 -> x0, local copies, waits for them, and re-layouts: 10.9 us -> none  [on_device(): lax.all_to_all(partial_value, 'table', split_axis=1, concat_axis=1, tiled...]
    transpose x2 -> x0, local copies, waits for them, and re-layouts: 10.4 us -> none  [the longest x1 10.3 us: on_device(): jnp.transpose(fetched, (0, 2, 1, 3, 4, 5))]
  transfers between devices with their start and end apart: 2 -> 0, of which waited for: 2 -> 0; matrix products, arithmetic and copies ran while one was open for 0% -> 0% of each run, Pallas kernels for 0% -> 0%
where the time goes in v3:
time: 54.6 us; the launch traced here: 53.7 us
  blocking collectives  38.6 us (71%)
  Pallas kernels  14.4 us (26%)
  between operations  0.65 us (1%)
    all_to_all x2, blocking collectives, exchange(): lax.all_to_all(value, ('table', 'ray'), split_axis=0, concat_axis=0, tile...  38.6 us
    pallas_call x1, Pallas kernels, on_device(): call(owner_kernel, [(rows, f32), (rows, f32), (rows, f32), ((32, 8, LANES...  12.3 us
    pallas_call x1, Pallas kernels, on_device(): call(network_kernel, [((16, 512), f32)], [VMEM] * 3)(back, win, wout)  1.13 us

profile of v3, /device:TPU:0, one launch (start us, length us, event | category | flops | bytes accessed | tf_op | source)
XLA Modules:
  0.0 53.7 jit_solution(17385674556525877271)
XLA Ops:
  0.6 0.9 %shard_map.129 = f32[128,8,128]{2,1,0:T(8,128)S(1)} custom-call(s32[2,512]{1,0:T(2,128)} %slot_hbm.1, s32[2,8,512]{2,1,0:T(8,128)} %corners_hbm.1, f32[3,2,512]{2,1,0:T(2,128)} %bitcast.43, f32[2,4,512]{2,1,0:T(4,128)} %cot_hbm.1), custom_call_target="tpu_custom_call" | custom-call | tf_op jit(solution)/shard_map/pallas_call | solution.py:322
  1.6 24.6 %all_to_all.10.recv_ref = f32[128,8,128]{2,1,0:T(8,128)S(1)} all-to-all(f32[128,8,128]{2,1,0:T(8,128)S(1)} %shard_map.129), channel_id=1, replica_groups=mesh['table'=8,'ray'=16] {'table','ray'}, dimensions={0} | all-to-all | bytes 1048576 | tf_op jit(solution)/shard_map/all_to_all | solution.py:297
  26.1 12.3 %shard_map.130 = (f32[128,16,128]{2,1,0:T(8,128)}, f32[128,16,128]{2,1,0:T(8,128)}, f32[128,16,128]{2,1,0:T(8,128)}, f32[32,8,128]{2,1,0:T(8,128)S(1)}, f32[8,64]{1,0:T(8,128)S(1)}, /*index=5*/f32[16,64]{1,0:T(8,128)S(1)}) custom-call(s32[64,128]{1,0:T(8,128)} %bitcast.42, f32[128,8,128]{2,1,0:T(8,128)S(1)} %all_to_all.10.recv_ref, ...), custom_call_target="tpu_custom_call" | custom-call | tf_op jit(solution)/shard_map/pallas_call | solution.py:337
  38.5 14.0 %all_to_all.11 = f32[128,2,128]{2,1,0:T(2,128)S(1)} all-to-all(f32[128,2,128]{2,1,0:T(2,128)S(1)} %bitcast.38), channel_id=1, replica_groups=mesh['table'=8,'ray'=16] {'table','ray'}, dimensions={0} | all-to-all | bytes 262144 | tf_op jit(solution)/shard_map/all_to_all | solution.py:297
  52.5 1.1 %shard_map.131 = f32[16,512]{1,0:T(8,128)} custom-call(f32[32,8,128]{2,1,0:T(8,128)S(1)} %bitcast.37, f32[8,64]{1,0:T(8,128)S(1)} %get-tuple-element.14.win_ref, f32[16,64]{1,0:T(8,128)S(1)} %get-tuple-element.15.wout_ref), custom_call_target="tpu_custom_call" | custom-call | tf_op jit(solution)/shard_map/pallas_call | solution.py:364

commit v4 on v3

--- a/solution.py
+++ b/solution.py
@@ -21,16 +21,18 @@
 
 
 def lane_blocks(pieces):
-    group = iota(pieces[0].shape, 1) // RUN
-    results = []
-    for q in range(4):
-        value = pieces[q]
-        for p in range(4):
-            if p != q:
-                moved = pltpu.roll(pieces[p], (RUN * (p - q)) % LANES, 1)
-                value = jnp.where(group == p, moved, value)
-        results.append(value)
-    return results
+    lane = iota(pieces[0].shape, 1)
+    for width in (2 * RUN, RUN):
+        low = (lane & width) == 0
+        step = width // RUN
+        results = list(pieces)
+        for one in range(4):
+            if not one & step:
+                x, y = pieces[one], pieces[one + step]
+                results[one] = jnp.where(low, x, pltpu.roll(y, width, 1))
+                results[one + step] = jnp.where(low, pltpu.roll(x, LANES - width, 1), y)
+        pieces = results
+    return pieces
 
 
 def tile_blocks(value):
@@ -80,7 +82,7 @@
 def owner_kernel(
     ids_ref, recv_ref, table_hbm, m1_hbm, m2_hbm, win_hbm, wout_hbm,
     tnew_hbm, m1new_hbm, m2new_hbm, out_ref, win_ref, wout_ref,
-    table_ref, m1_ref, m2_ref, grad_ref, corner_ref, aux_ref, back_ref, slots_ref, hot_ref, hat_ref, key_ref,
+    table_ref, m1_ref, m2_ref, grad_ref, corner_ref, aux_ref, back_ref, slots_ref, hat_ref, key_ref, column_ref, cot_ref,
     found_ref, result_ref, sems,
 ):
     loads = start_all(
@@ -104,7 +106,7 @@
             aux_ref[8 + t, v] = rows[3]
         return carry
 
-    lax.fori_loop(0, 8, unpack, 0, unroll=2)
+    lax.fori_loop(0, 8, unpack, 0, unroll=8)
 
     first_slot = (mine * 64).astype(f32)
     hits = []
@@ -133,7 +135,12 @@
                 place = jnp.where(probe <= wanted, place + jump, place)
             back_ref[v] = jnp.where((wanted >= 0) & (wanted < totals[v]), place, -1)
 
-    def compact(lt):
+    entries = [(iota((16, LANES), 0) + 16 * i).astype(f32).astype(bf16) for i in range(8)]
+    owns = [((iota((16, LANES), 0) & 7) // 4 + 2 * i).astype(f32).astype(bf16) for i in range(8)]
+    one = jnp.ones((16, LANES), bf16)
+    none = jnp.zeros((16, LANES), bf16)
+
+    def compact(lt, carry):
         corner = jnp.zeros((8, LANES), f32)
         aux = jnp.zeros((8, LANES), f32)
         for v in range(4):
@@ -147,46 +154,46 @@
             factor = jnp.where((sub >> d) & 1 == 1, f, 1.0 - f)
             hat = factor if hat is None else hat * factor
         entry = corner.astype(i32)
-        key = (aux[0:1].astype(i32) & 3) * 2 + ((entry >> 7) & 1)
-        column = (entry & 127) | ((entry >> 8) << 7)
         hat_ref[lt] = hat
-        key_ref[lt] = key
-        entries = iota((256, LANES), 0)
+        key_ref[lt] = ((aux[0:1].astype(i32) & 3) * 4 + (entry >> 7)).astype(f32)
+        column_ref[lt] = (entry & 127).astype(f32)
+        cot_ref[lt] = jnp.where(sub < 4, pltpu.roll(aux, 4, 0), aux)
+        return carry
+
+    def hot_rows(lt):
+        pieces = []
         for c in range(8):
-            hot = jnp.where(column[c : c + 1] == entries, 1.0, 0.0).astype(bf16)
-            hot_ref[lt, :, c * LANES : (c + 1) * LANES] = hot
-        return aux, hat, key
+            wanted = jnp.broadcast_to(column_ref[lt, c : c + 1, :], (16, LANES)).astype(bf16)
+            pieces.append(jnp.concatenate([jnp.where(wanted == entries[i], one, none) for i in range(8)], axis=0))
+        return jnp.concatenate(pieces, axis=1)
 
     def block_of(lt, slot):
         level, group = lt // 8, lt % 8
         return level * 64 + ids_ref[(group * 2 + level) * 4 + slot, owner]
 
     def accumulate(lt, carry):
-        aux, hat, key = compact(lt)
-        cot = jnp.where(sub < 4, pltpu.roll(aux, 4, 0), aux)
+        cot = cot_ref[lt]
         columns = []
         for c in range(8):
-            value = cot * hat[c : c + 1]
+            value = cot * hat_ref[lt, c : c + 1, :]
             high = value.astype(bf16).astype(f32)
-            low = value - high
-            masks = [jnp.broadcast_to(key[c : c + 1], (8, LANES)) == parity + 2 * i for i in range(4)]
-            pieces = [jnp.where(m, high, 0.0) for m in masks] + [jnp.where(m, low, 0.0) for m in masks]
-            columns.append(jnp.concatenate(pieces, axis=0).astype(bf16))
-        both = lax.dot_general(
-            jnp.concatenate(columns, axis=1), hot_ref[lt], (((1,), (1,)), ((), ())), preferred_element_type=f32
+            both = jnp.concatenate([high, value - high], axis=0).astype(bf16)
+            key = jnp.broadcast_to(key_ref[lt, c : c + 1, :], (16, LANES)).astype(bf16)
+            columns.append(jnp.concatenate([jnp.where(key == owns[i], both, none) for i in range(8)], axis=0))
+        sums = lax.dot_general(
+            jnp.concatenate(columns, axis=1), hot_rows(lt), (((1,), (1,)), ((), ())), preferred_element_type=f32
         )
-        part = both[:32] + both[32:]
         for slot in range(4):
             block = block_of(lt, slot)
             for half in range(2):
-                grad_ref[block, 8 * half : 8 * half + 8, :] += part[
-                    8 * slot : 8 * slot + 8, half * LANES : (half + 1) * LANES
-                ]
+                at = 32 * slot + 16 * half
+                grad_ref[block, 8 * half : 8 * half + 8, :] += sums[at : at + 8] + sums[at + 8 : at + 16]
         return carry
 
     def gather_pass(step, carry):
         locate(step)
-        lax.fori_loop(0, 16, accumulate, 0, unroll=2)
+        lax.fori_loop(0, 16, compact, 0, unroll=4)
+        lax.fori_loop(0, 16, accumulate, 0, unroll=4)
         return carry
 
     lax.fori_loop(0, passes, gather_pass, 0)
@@ -206,20 +213,21 @@
     stores = start_all((table_ref, m1_ref, m2_ref), (tnew_hbm, m1new_hbm, m2new_hbm), sems)
 
     def look(lt, carry):
-        blocks = [table_ref[block_of(lt, slot)] for slot in range(4)]
-        rows = jnp.concatenate([jnp.concatenate([b[:8], b[8:]], axis=1) for b in blocks], axis=0)
+        rows = jnp.concatenate([table_ref[block_of(lt, slot)] for slot in range(4)], axis=0)
         high = rows.astype(bf16)
         low = (rows - high.astype(f32)).astype(bf16)
-        both = jnp.dot(jnp.concatenate([high, low], axis=0), hot_ref[lt], preferred_element_type=f32)
-        seen = both[:32] + both[32:]
-        hat, key = hat_ref[lt], key_ref[lt]
+        hot = hot_rows(lt)
+        seen = jnp.dot(
+            jnp.concatenate([high, low], axis=1), jnp.concatenate([hot, hot], axis=0), preferred_element_type=f32
+        )
         total = jnp.zeros((8, LANES), f32)
         for c in range(8):
-            own = jnp.broadcast_to(key[c : c + 1], (8, LANES))
+            own = jnp.broadcast_to(key_ref[lt, c : c + 1, :], (8, LANES))
             picked = jnp.zeros((8, LANES), f32)
-            for i in range(4):
-                picked = jnp.where(own == parity + 2 * i, seen[8 * i : 8 * i + 8, c * LANES : (c + 1) * LANES], picked)
-            total = total + jnp.where((own & 1) == parity, picked, 0.0) * hat[c : c + 1]
+            for i in range(8):
+                mask = own == (parity + 2 * i).astype(f32)
+                picked = jnp.where(mask, seen[8 * i : 8 * i + 8, c * LANES : (c + 1) * LANES], picked)
+            total = total + picked * hat_ref[lt, c : c + 1, :]
         found_ref[lt] = total + pltpu.roll(total, 4, 0)
         return carry
 
@@ -237,14 +245,9 @@
         @pl.when(passes > 1)
         def _():
             locate(step)
-
-            def again(lt, inner):
-                compact(lt)
-                return inner
-
-            lax.fori_loop(0, 16, again, 0)
-
-        lax.fori_loop(0, 16, look, 0, unroll=2)
+            lax.fori_loop(0, 16, compact, 0)
+
+        lax.fori_loop(0, 16, look, 0, unroll=4)
         lax.fori_loop(0, 8, spread, 0, unroll=2)
         return carry
 
@@ -347,9 +350,10 @@
             pltpu.VMEM((16, 4, 8, LANES), f32),
             pltpu.VMEM((4, 16, LANES), i32),
             pltpu.VMEM((4, 16, LANES), i32),
-            pltpu.VMEM((16, 256, 8 * LANES), bf16),
-            pltpu.VMEM((16, 8, LANES), f32),
-            pltpu.VMEM((16, 8, LANES), i32),
+            pltpu.VMEM((16, 8, LANES), f32),
+            pltpu.VMEM((16, 8, LANES), f32),
+            pltpu.VMEM((16, 8, LANES), f32),
+            pltpu.VMEM((16, 8, LANES), f32),
             pltpu.VMEM((16, 8, LANES), f32),
             pltpu.VMEM((32, 8, LANES), f32),
             pltpu.SemaphoreType.DMA((5,)),

time: 54.6 us -> 51.4 us (0.941)
  Pallas kernels: 14.4 us -> 11.2 us
    pallas_call x1, Pallas kernels: 12.3 us -> 9.07 us  [on_device(): call(owner_kernel, [(rows, f32), (rows, f32), (rows, f32), ((32, 8, LANES...]
where the time goes in v4:
time: 51.4 us; the launch traced here: 50.5 us
  blocking collectives  38.6 us (75%)
  Pallas kernels  11.2 us (22%)
  between operations  0.65 us (1%)
    all_to_all x2, blocking collectives, exchange(): lax.all_to_all(value, ('table', 'ray'), split_axis=0, concat_axis=0, tile...  38.6 us
    pallas_call x1, Pallas kernels, on_device(): call(owner_kernel, [(rows, f32), (rows, f32), (rows, f32), ((32, 8, LANES...  9.07 us
    pallas_call x1, Pallas kernels, on_device(): call(network_kernel, [((16, 512), f32)], [VMEM] * 3)(back, win, wout)  1.14 us

profile of v4, /device:TPU:0, one launch (start us, length us, event | category | flops | bytes accessed | tf_op | source)
XLA Modules:
  0.0 50.5 jit_solution(3506060801349294352)
XLA Ops:
  0.6 1.0 %shard_map.129 = f32[128,8,128]{2,1,0:T(8,128)S(1)} custom-call(s32[2,512]{1,0:T(2,128)} %slot_hbm.1, s32[2,8,512]{2,1,0:T(8,128)} %corners_hbm.1, f32[3,2,512]{2,1,0:T(2,128)} %bitcast.43, f32[2,4,512]{2,1,0:T(4,128)} %cot_hbm.1), custom_call_target="tpu_custom_call" | custom-call | tf_op jit(solution)/shard_map/pallas_call | solution.py:325
  1.6 24.6 %all_to_all.10.recv_ref = f32[128,8,128]{2,1,0:T(8,128)S(1)} all-to-all(f32[128,8,128]{2,1,0:T(8,128)S(1)} %shard_map.129), channel_id=1, replica_groups=mesh['table'=8,'ray'=16] {'table','ray'}, dimensions={0} | all-to-all | bytes 1048576 | tf_op jit(solution)/shard_map/all_to_all | solution.py:300
  26.2 9.1 %shard_map.130 = (f32[128,16,128]{2,1,0:T(8,128)}, f32[128,16,128]{2,1,0:T(8,128)}, f32[128,16,128]{2,1,0:T(8,128)}, f32[32,8,128]{2,1,0:T(8,128)S(1)}, f32[8,64]{1,0:T(8,128)S(1)}, /*index=5*/f32[16,64]{1,0:T(8,128)S(1)}) custom-call(s32[64,128]{1,0:T(8,128)} %bitcast.42, f32[128,8,128]{2,1,0:T(8,128)S(1)} %all_to_all.10.recv_ref, ...), custom_call_target="tpu_custom_call" | custom-call | tf_op jit(solution)/shard_map/pallas_call | solution.py:340
  35.3 14.0 %all_to_all.11 = f32[128,2,128]{2,1,0:T(2,128)S(1)} all-to-all(f32[128,2,128]{2,1,0:T(2,128)S(1)} %bitcast.38), channel_id=1, replica_groups=mesh['table'=8,'ray'=16] {'table','ray'}, dimensions={0} | all-to-all | bytes 262144 | tf_op jit(solution)/shard_map/all_to_all | solution.py:300
  49.3 1.1 %shard_map.131 = f32[16,512]{1,0:T(8,128)} custom-call(f32[32,8,128]{2,1,0:T(8,128)S(1)} %bitcast.37, f32[8,64]{1,0:T(8,128)S(1)} %get-tuple-element.14.win_ref, f32[16,64]{1,0:T(8,128)S(1)} %get-tuple-element.15.wout_ref), custom_call_target="tpu_custom_call" | custom-call | tf_op jit(solution)/shard_map/pallas_call | solution.py:368

commit v5 on v4

--- a/solution.py
+++ b/solution.py
@@ -12,7 +12,7 @@
 
 LANES = 128
 RUN = 32
-VMEM_LIMIT = 40 << 20
+VMEM_LIMIT = 16 << 20
 f32, bf16, i32 = jnp.float32, jnp.bfloat16, jnp.int32
 
 
@@ -80,14 +80,12 @@
 
 
 def owner_kernel(
-    ids_ref, recv_ref, table_hbm, m1_hbm, m2_hbm, win_hbm, wout_hbm,
-    tnew_hbm, m1new_hbm, m2new_hbm, out_ref, win_ref, wout_ref,
-    table_ref, m1_ref, m2_ref, grad_ref, corner_ref, aux_ref, back_ref, slots_ref, hat_ref, key_ref, column_ref, cot_ref,
+    ids_ref, recv_ref, table_ref, m1_hbm, m2_hbm,
+    tnew_ref, m1new_ref, m2new_ref, out_ref,
+    grad_ref, corner_ref, aux_ref, back_ref, slots_ref, hat_ref, key_ref, column_ref, cot_ref,
     found_ref, result_ref, sems,
 ):
-    loads = start_all(
-        (table_hbm, m1_hbm, m2_hbm, win_hbm, wout_hbm), (table_ref, m1_ref, m2_ref, win_ref, wout_ref), sems
-    )
+    loads = start_all((m1_hbm, m2_hbm), (m1new_ref, m2new_ref), sems)
     mine = lax.axis_index("table")
     owner = mine * lax.axis_size("ray") + lax.axis_index("ray")
     sub = iota((8, LANES), 0)
@@ -197,23 +195,23 @@
         return carry
 
     lax.fori_loop(0, passes, gather_pass, 0)
+
     wait_all(loads)
 
     def update(step, carry):
         at = pl.ds(step * 4, 4)
         grad = grad_ref[at]
-        first = beta_one * m1_ref[at] + (1.0 - beta_one) * grad
-        second = beta_two * m2_ref[at] + (1.0 - beta_two) * grad * grad
-        m1_ref[at] = first
-        m2_ref[at] = second
-        table_ref[at] = table_ref[at] - learn_rate * first / (jnp.sqrt(second) + adam_eps)
+        first = beta_one * m1new_ref[at] + (1.0 - beta_one) * grad
+        second = beta_two * m2new_ref[at] + (1.0 - beta_two) * grad * grad
+        m1new_ref[at] = first
+        m2new_ref[at] = second
+        tnew_ref[at] = table_ref[at] - learn_rate * first / (jnp.sqrt(second) + adam_eps)
         return carry
 
     lax.fori_loop(0, 32, update, 0)
-    stores = start_all((table_ref, m1_ref, m2_ref), (tnew_hbm, m1new_hbm, m2new_hbm), sems)
 
     def look(lt, carry):
-        rows = jnp.concatenate([table_ref[block_of(lt, slot)] for slot in range(4)], axis=0)
+        rows = jnp.concatenate([tnew_ref[block_of(lt, slot)] for slot in range(4)], axis=0)
         high = rows.astype(bf16)
         low = (rows - high.astype(f32)).astype(bf16)
         hot = hot_rows(lt)
@@ -254,7 +252,6 @@
     lax.fori_loop(0, passes, look_pass, 0)
     for m in range(32):
         out_ref[m] = tile_blocks(result_ref[m])
-    wait_all(stores)
 
 
 def network_kernel(recv_ref, win_ref, wout_ref, out_ref):
@@ -283,7 +280,7 @@
 def call(kernel, outs, in_specs, scratch=(), out_specs=None, **extra):
     return pl.pallas_call(
         kernel,
-        out_shape=[jax.ShapeDtypeStruct(s, d) for s, d in outs],
+        out_shape=[jax.ShapeDtypeStruct(*o) if isinstance(o, tuple) else o for o in outs],
         in_specs=in_specs,
         out_specs=[VMEM] * len(outs) if out_specs is None else out_specs,
         scratch_shapes=list(scratch),
@@ -337,14 +334,11 @@
     samples = exchange(packed)
     rows = (128, 16, LANES)
     ids = block_ids.transpose(0, 1, 3, 2).reshape(64, 128)
-    tnew, m1new, m2new, found, win, wout = call(
+    tnew, m1new, m2new, found = call(
         owner_kernel,
-        [(rows, f32), (rows, f32), (rows, f32), ((32, 8, LANES), f32), ((8, 64), f32), ((16, 64), f32)],
-        [SMEM, VMEM] + [HBM] * 5,
+        [pltpu.VMEM(rows, f32)] * 3 + [((32, 8, LANES), f32)],
+        [SMEM, VMEM, VMEM, HBM, HBM],
         [
-            pltpu.VMEM(rows, f32),
-            pltpu.VMEM(rows, f32),
-            pltpu.VMEM(rows, f32),
             pltpu.VMEM(rows, f32),
             pltpu.VMEM((16, 4, 8, LANES), f32),
             pltpu.VMEM((16, 4, 8, LANES), f32),
@@ -356,16 +350,11 @@
             pltpu.VMEM((16, 8, LANES), f32),
             pltpu.VMEM((16, 8, LANES), f32),
             pltpu.VMEM((32, 8, LANES), f32),
-            pltpu.SemaphoreType.DMA((5,)),
+            pltpu.SemaphoreType.DMA((2,)),
         ],
-        [HBM] * 3 + [VMEM] * 3,
-    )(
-        *in_hbm(ids),
-        samples,
-        *in_hbm(rows_of(table), rows_of(moment1), rows_of(moment2), weight_in.T, weight_out),
-    )
+    )(*in_hbm(ids), samples, rows_of(table), *in_hbm(rows_of(moment1), rows_of(moment2)))
     back = exchange(found.reshape(128, 2, LANES)).reshape(32, 8, LANES)
-    (mlp_out,) = call(network_kernel, [((16, 512), f32)], [VMEM] * 3)(back, win, wout)
+    (mlp_out,) = call(network_kernel, [((16, 512), f32)], [VMEM] * 3)(back, weight_in.T, weight_out)
     shape = table.shape
     return (rows_back(tnew, shape), rows_back(m1new, shape), rows_back(m2new, shape), mlp_out)
 

time: 51.4 us -> 52.2 us (1.016)
  blocking collectives: 38.6 us -> 24.6 us
  waiting for transfers between devices: 0 us -> 6.67 us
  starting transfers between devices: 0 us -> 4.61 us
  local copies, waits for them, and re-layouts: 0 us -> 2.92 us
  Pallas kernels: 11.2 us -> 11.9 us
    all_to_all x2 -> x1, blocking collectives: 38.6 us -> 24.6 us  [exchange(): lax.all_to_all(value, ('table', 'ray'), split_axis=0, concat_axis=0, tile...]
    all_to_all x0 -> x1, waiting for transfers between devices: none -> 6.67 us  [exchange(): lax.all_to_all(value, ('table', 'ray'), split_axis=0, concat_axis=0, tile...]
    all_to_all x0 -> x1, starting transfers between devices: none -> 4.61 us  [exchange(): lax.all_to_all(value, ('table', 'ray'), split_axis=0, concat_axis=0, tile...]
    unnamed x0 -> x9, local copies, waits for them, and re-layouts: none -> 2.92 us
    pallas_call x2, Pallas kernels: 10.2 us -> 10.8 us  [the longest x1 9.66 us: on_device(): call(owner_kernel, [pltpu.VMEM(rows, f32)] * 3 + [((32, 8, LANES), f32)],...]
  transfers between devices with their start and end apart: 0 -> 1, of which waited for: 0 -> 1; matrix products, arithmetic and copies ran while one was open for 0% -> 6% of each run, Pallas kernels for 0% -> 0%
where the time goes in v5:
time: 52.2 us; the launch traced here: 51.3 us
  blocking collectives  24.6 us (47%)
  Pallas kernels  11.9 us (23%)
  waiting for transfers between devices  6.67 us (13%)
  starting transfers between devices  4.61 us (9%)
  local copies, waits for them, and re-layouts  2.92 us (6%)
  between operations  0.67 us (1%)
    all_to_all x1, blocking collectives, exchange(): lax.all_to_all(value, ('table', 'ray'), split_axis=0, concat_axis=0, tile...  24.6 us
    pallas_call x1, Pallas kernels, on_device(): call(owner_kernel, [pltpu.VMEM(rows, f32)] * 3 + [((32, 8, LANES), f32)],...  9.66 us
    all_to_all x1, waiting for transfers between devices, exchange(): lax.all_to_all(value, ('table', 'ray'), split_axis=0, concat_axis=0, tile...  6.67 us
    all_to_all x1, starting transfers between devices, exchange(): lax.all_to_all(value, ('table', 'ray'), split_axis=0, concat_axis=0, tile...  4.61 us
    unnamed x9, local copies, waits for them, and re-layouts  2.92 us
    pallas_call x1, Pallas kernels, on_device(): call(network_kernel, [((16, 512), f32)], [VMEM] * 3)  1.13 us
    pallas_call x1, Pallas kernels, on_device(): call(pack_kernel, [((128, 8, LANES), f32)], [HBM] * 4, [pltpu.VMEM((2, 51...  1.08 us
  transfers between devices with their start and end apart: 1, of which 1 were waited for; matrix products, arithmetic and copies ran while one was open for 6% of the time, Pallas kernels for 0%

profile of v5, /device:TPU:0, one launch (start us, length us, event | category | flops | bytes accessed | tf_op | source)
XLA Modules:
  0.0 51.3 jit_solution(13434451133469436480)
XLA Ops:
  0.6 0.0 copy-start
  0.6 1.1 %shard_map.129 = f32[128,8,128]{2,1,0:T(8,128)S(1)} custom-call(s32[2,512]{1,0:T(2,128)} %slot_hbm.1, s32[2,8,512]{2,1,0:T(8,128)} %corners_hbm.1, f32[3,2,512]{2,1,0:T(2,128)} %bitcast.46, f32[2,4,512]{2,1,0:T(4,128)} %cot_hbm.1), custom_call_target="tpu_custom_call" | custom-call | tf_op jit(solution)/shard_map/pallas_call | solution.py:322
  1.7 24.6 %all_to_all.10.recv_ref = f32[128,8,128]{2,1,0:T(8,128)S(1)} all-to-all(f32[128,8,128]{2,1,0:T(8,128)S(1)} %shard_map.129), channel_id=1, replica_groups=mesh['table'=8,'ray'=16] {'table','ray'}, dimensions={0} | all-to-all | bytes 1048576 | tf_op jit(solution)/shard_map/all_to_all | solution.py:297
  26.3 0.0 copy-done
  26.3 9.7 %shard_map.130 = (f32[128,16,128]{2,1,0:T(8,128)S(1)}, f32[128,16,128]{2,1,0:T(8,128)S(1)}, f32[128,16,128]{2,1,0:T(8,128)S(1)}, f32[32,8,128]{2,1,0:T(8,128)}) custom-call(s32[64,128]{1,0:T(8,128)} %bitcast.45, f32[128,8,128]{2,1,0:T(8,128)S(1)} %all_to_all.10.recv_ref, f32[128,16,128]{2,1,0:T(8,128)S(1)} %bitcast.40, f32[128,16,128]{2,1,0:T(8,128)} %bitcast.43, ...), custom_call_target="tpu_custom_call" | custom-call | tf_op jit(solution)/shard_map/pallas_call | solution.py:337
  36.0 4.6 %all-to-all-start.1 = ((f32[128,2,128]{2,1,0:T(2,128)}), f32[128,2,128]{2,1,0:T(2,128)S(1)}, u32[]{:S(2)}, u32[]{:S(2)}) async-start(f32[128,2,128]{2,1,0:T(2,128)} %bitcast.21), calls=%async_computation.1 | async-start | bytes 262144 | tf_op jit(solution)/shard_map/all_to_all | solution.py:297
  40.6 1.0 %copy.20 = f32[2,64,4,512]{3,2,1,0:T(4,128)} copy(f32[2,64,4,512]{3,2,1,0:T(4,128)S(1)} %bitcast.39) | data formatting | bytes 2097152
  41.6 1.0 %copy.21 = f32[2,64,4,512]{3,2,1,0:T(4,128)} copy(f32[2,64,4,512]{3,2,1,0:T(4,128)S(1)} %bitcast.38) | data formatting | bytes 2097152
  42.5 0.0 copy-start.1
  42.5 0.0 copy-start.2
  42.5 1.0 %copy.22 = f32[2,64,4,512]{3,2,1,0:T(4,128)} copy(f32[2,64,4,512]{3,2,1,0:T(4,128)S(1)} %bitcast.37) | data formatting | bytes 2097152
  43.5 6.7 %all-to-all-done.1 = f32[128,2,128]{2,1,0:T(2,128)S(1)} async-done(((f32[128,2,128]{2,1,0:T(2,128)}), f32[128,2,128]{2,1,0:T(2,128)S(1)}, u32[]{:S(2)}, u32[]{:S(2)}) %all-to-all-start.1) | async-done | bytes 131104 | tf_op jit(solution)/shard_map/all_to_all | solution.py:297
  50.2 0.0 copy-done.1
  50.2 0.0 copy-done.2
  50.2 1.1 %shard_map.131 = f32[16,512]{1,0:T(8,128)} custom-call(f32[32,8,128]{2,1,0:T(8,128)S(1)} %bitcast.41, f32[8,64]{1,0:T(8,128)S(1)} %bitcast.42, f32[16,64]{1,0:T(8,128)S(1)} %copy-done.1), custom_call_target="tpu_custom_call" | custom-call | tf_op jit(solution)/shard_map/pallas_call | solution.py:357
Async XLA Ops:
  0.6 25.7 %copy-start = (f32[2,64,4,512]{3,2,1,0:T(4,128)S(1)}, f32[2,64,4,512]{3,2,1,0:T(4,128)}, u32[]{:S(2)}) copy-start(f32[2,64,4,512]{3,2,1,0:T(4,128)} %param.10) | copy-start | bytes 3145732
  36.0 14.2 %all-to-all-start.1 = ((f32[128,2,128]{2,1,0:T(2,128)}), f32[128,2,128]{2,1,0:T(2,128)S(1)}, u32[]{:S(2)}, u32[]{:S(2)}) async-start(f32[128,2,128]{2,1,0:T(2,128)} %bitcast.21), calls=%async_computation.1 | async-start | bytes 262144 | tf_op jit(solution)/shard_map/all_to_all | solution.py:297
  42.5 7.6 %copy-start.1 = (f32[16,64]{1,0:T(8,128)S(1)}, f32[16,64]{1,0:T(8,128)}, u32[]{:S(2)}) copy-start(f32[16,64]{1,0:T(8,128)} %wout_ref.1) | copy-start | bytes 12292
  42.5 7.6 %copy-start.2 = (f32[64,8]{0,1:T(8,128)S(1)}, f32[64,8]{0,1:T(8,128)}, u32[]{:S(2)}) copy-start(f32[64,8]{0,1:T(8,128)} %param.18) | copy-start | bytes 6148

commit v6 on v5

--- a/solution.py
+++ b/solution.py
@@ -80,17 +80,16 @@
 
 
 def owner_kernel(
-    ids_ref, recv_ref, table_ref, m1_hbm, m2_hbm,
+    ids_hbm, recv_ref, table_ref, m1_hbm, m2_hbm,
     tnew_ref, m1new_ref, m2new_ref, out_ref,
-    grad_ref, corner_ref, aux_ref, back_ref, slots_ref, hat_ref, key_ref, column_ref, cot_ref,
+    ids_ref, grad_ref, corner_ref, aux_ref, slots_ref, hat_ref, key_ref, column_ref, cot_ref,
     found_ref, result_ref, sems,
 ):
-    loads = start_all((m1_hbm, m2_hbm), (m1new_ref, m2new_ref), sems)
+    loads = start_all((ids_hbm, m1_hbm, m2_hbm), (ids_ref, m1new_ref, m2new_ref), sems)
     mine = lax.axis_index("table")
     owner = mine * lax.axis_size("ray") + lax.axis_index("ray")
     sub = iota((8, LANES), 0)
     parity = sub // 4
-    lane16 = iota((16, LANES), 1)
 
     grad_ref[...] = jnp.zeros_like(grad_ref)
     result_ref[...] = jnp.zeros_like(result_ref)
@@ -126,12 +125,6 @@
             rank = before[v] + through[v] - 1 - step * LANES
             inside = (hits[v] > 0.5) & (rank >= 0) & (rank < LANES)
             slots_ref[v] = jnp.where(inside, rank, -1)
-            wanted = lane16 + step * LANES - before[v]
-            place = jnp.zeros_like(wanted)
-            for jump in (64, 32, 16, 8, 4, 2, 1):
-                probe = gather_lanes(through[v], place + (jump - 1))
-                place = jnp.where(probe <= wanted, place + jump, place)
-            back_ref[v] = jnp.where((wanted >= 0) & (wanted < totals[v]), place, -1)
 
     entries = [(iota((16, LANES), 0) + 16 * i).astype(f32).astype(bf16) for i in range(8)]
     owns = [((iota((16, LANES), 0) & 7) // 4 + 2 * i).astype(f32).astype(bf16) for i in range(8)]
@@ -139,13 +132,18 @@
     none = jnp.zeros((16, LANES), bf16)
 
     def compact(lt, carry):
-        corner = jnp.zeros((8, LANES), f32)
-        aux = jnp.zeros((8, LANES), f32)
+        high, low, chosen = [], [], []
         for v in range(4):
-            place = jnp.broadcast_to(back_ref[v, pl.ds(lt, 1), :], (8, LANES))
-            index = jnp.maximum(place, 0)
-            corner = jnp.where(place >= 0, gather_lanes(corner_ref[lt, v], index), corner)
-            aux = jnp.where(place >= 0, gather_lanes(aux_ref[lt, v], index), aux)
+            piece = jnp.concatenate([corner_ref[lt, v], aux_ref[lt, v]], axis=0)
+            high.append(piece.astype(bf16))
+            low.append((piece - high[v].astype(f32)).astype(bf16))
+            slot = jnp.broadcast_to(slots_ref[v, pl.ds(lt, 1), :].astype(f32), (16, LANES)).astype(bf16)
+            chosen.append(jnp.concatenate([jnp.where(slot == entries[i], one, none) for i in range(8)], axis=0))
+        rows = jnp.concatenate([jnp.concatenate(high, axis=1), jnp.concatenate(low, axis=1)], axis=0)
+        both = lax.dot_general(
+            rows, jnp.concatenate(chosen, axis=1), (((1,), (1,)), ((), ())), preferred_element_type=f32
+        )
+        corner, aux = both[:8] + both[16:24], both[8:16] + both[24:]
         hat = None
         for d in range(3):
             f = jnp.broadcast_to(aux[1 + d : 2 + d], (8, LANES))
@@ -188,15 +186,19 @@
                 grad_ref[block, 8 * half : 8 * half + 8, :] += sums[at : at + 8] + sums[at + 8 : at + 16]
         return carry
 
+    locate(0)
+    lax.fori_loop(0, 16, compact, 0, unroll=4)
+    loads[0].wait()
+    lax.fori_loop(0, 16, accumulate, 0, unroll=4)
+
     def gather_pass(step, carry):
         locate(step)
-        lax.fori_loop(0, 16, compact, 0, unroll=4)
-        lax.fori_loop(0, 16, accumulate, 0, unroll=4)
-        return carry
-
-    lax.fori_loop(0, passes, gather_pass, 0)
-
-    wait_all(loads)
+        lax.fori_loop(0, 16, compact, 0)
+        lax.fori_loop(0, 16, accumulate, 0)
+        return carry
+
+    lax.fori_loop(1, passes, gather_pass, 0)
+    wait_all(loads[1:])
 
     def update(step, carry):
         at = pl.ds(step * 4, 4)
@@ -240,16 +242,20 @@
         return carry
 
     def look_pass(step, carry):
-        @pl.when(passes > 1)
-        def _():
-            locate(step)
-            lax.fori_loop(0, 16, compact, 0)
-
-        lax.fori_loop(0, 16, look, 0, unroll=4)
-        lax.fori_loop(0, 8, spread, 0, unroll=2)
-        return carry
-
-    lax.fori_loop(0, passes, look_pass, 0)
+        locate(step)
+        lax.fori_loop(0, 16, compact, 0)
+        lax.fori_loop(0, 16, look, 0)
+        lax.fori_loop(0, 8, spread, 0)
+        return carry
+
+    @pl.when(passes > 1)
+    def _():
+        locate(0)
+        lax.fori_loop(0, 16, compact, 0)
+
+    lax.fori_loop(0, 16, look, 0, unroll=4)
+    lax.fori_loop(0, 8, spread, 0, unroll=2)
+    lax.fori_loop(1, passes, look_pass, 0)
     for m in range(32):
         out_ref[m] = tile_blocks(result_ref[m])
 
@@ -274,7 +280,6 @@
 
 VMEM = pl.BlockSpec(memory_space=pltpu.VMEM)
 HBM = pl.BlockSpec(memory_space=pltpu.HBM)
-SMEM = pl.BlockSpec(memory_space=pltpu.SMEM)
 
 
 def call(kernel, outs, in_specs, scratch=(), out_specs=None, **extra):
@@ -337,20 +342,20 @@
     tnew, m1new, m2new, found = call(
         owner_kernel,
         [pltpu.VMEM(rows, f32)] * 3 + [((32, 8, LANES), f32)],
-        [SMEM, VMEM, VMEM, HBM, HBM],
+        [HBM, VMEM, VMEM, HBM, HBM],
         [
+            pltpu.SMEM((64, LANES), i32),
             pltpu.VMEM(rows, f32),
             pltpu.VMEM((16, 4, 8, LANES), f32),
             pltpu.VMEM((16, 4, 8, LANES), f32),
             pltpu.VMEM((4, 16, LANES), i32),
-            pltpu.VMEM((4, 16, LANES), i32),
             pltpu.VMEM((16, 8, LANES), f32),
             pltpu.VMEM((16, 8, LANES), f32),
             pltpu.VMEM((16, 8, LANES), f32),
             pltpu.VMEM((16, 8, LANES), f32),
             pltpu.VMEM((16, 8, LANES), f32),
             pltpu.VMEM((32, 8, LANES), f32),
-            pltpu.SemaphoreType.DMA((2,)),
+            pltpu.SemaphoreType.DMA((3,)),
         ],
     )(*in_hbm(ids), samples, rows_of(table), *in_hbm(rows_of(moment1), rows_of(moment2)))
     back = exchange(found.reshape(128, 2, LANES)).reshape(32, 8, LANES)

time: 52.2 us -> 51 us (0.977)
  Pallas kernels: 11.9 us -> 10.7 us
    pallas_call x1, Pallas kernels: 9.66 us -> 8.53 us  [on_device(): call(owner_kernel, [pltpu.VMEM(rows, f32)] * 3 + [((32, 8, LANES), f32)],...]
where the time goes in v6:
time: 51 us; the launch traced here: 50.2 us
  blocking collectives  24.6 us (48%)
  Pallas kernels  10.7 us (21%)
  waiting for transfers between devices  6.67 us (13%)
  starting transfers between devices  4.61 us (9%)
  local copies, waits for them, and re-layouts  2.92 us (6%)
  between operations  0.67 us (1%)
    all_to_all x1, blocking collectives, exchange(): lax.all_to_all(value, ('table', 'ray'), split_axis=0, concat_axis=0, tile...  24.6 us
    pallas_call x1, Pallas kernels, on_device(): call(owner_kernel, [pltpu.VMEM(rows, f32)] * 3 + [((32, 8, LANES), f32)],...  8.53 us
    all_to_all x1, waiting for transfers between devices, exchange(): lax.all_to_all(value, ('table', 'ray'), split_axis=0, concat_axis=0, tile...  6.67 us
    all_to_all x1, starting transfers between devices, exchange(): lax.all_to_all(value, ('table', 'ray'), split_axis=0, concat_axis=0, tile...  4.61 us
    unnamed x9, local copies, waits for them, and re-layouts  2.92 us
    pallas_call x1, Pallas kernels, on_device(): call(network_kernel, [((16, 512), f32)], [VMEM] * 3)  1.13 us
    pallas_call x1, Pallas kernels, on_device(): call(pack_kernel, [((128, 8, LANES), f32)], [HBM] * 4, [pltpu.VMEM((2, 51...  1.08 us
  transfers between devices with their start and end apart: 1, of which 1 were waited for; matrix products, arithmetic and copies ran while one was open for 6% of the time, Pallas kernels for 0%

profile of v6, /device:TPU:0, one launch (start us, length us, event | category | flops | bytes accessed | tf_op | source)
XLA Modules:
  0.0 50.2 jit_solution(1871038058898552938)
XLA Ops:
  0.6 0.0 copy-start
  0.6 1.1 %shard_map.129 = f32[128,8,128]{2,1,0:T(8,128)S(1)} custom-call(s32[2,512]{1,0:T(2,128)} %slot_hbm.1, s32[2,8,512]{2,1,0:T(8,128)} %corners_hbm.1, f32[3,2,512]{2,1,0:T(2,128)} %bitcast.46, f32[2,4,512]{2,1,0:T(4,128)} %cot_hbm.1), custom_call_target="tpu_custom_call" | custom-call | tf_op jit(solution)/shard_map/pallas_call | solution.py:327
  1.7 24.6 %all_to_all.10.recv_ref = f32[128,8,128]{2,1,0:T(8,128)S(1)} all-to-all(f32[128,8,128]{2,1,0:T(8,128)S(1)} %shard_map.129), channel_id=1, replica_groups=mesh['table'=8,'ray'=16] {'table','ray'}, dimensions={0} | all-to-all | bytes 1048576 | tf_op jit(solution)/shard_map/all_to_all | solution.py:302
  26.3 0.0 copy-done
  26.3 8.5 %shard_map.130 = (f32[128,16,128]{2,1,0:T(8,128)S(1)}, f32[128,16,128]{2,1,0:T(8,128)S(1)}, f32[128,16,128]{2,1,0:T(8,128)S(1)}, f32[32,8,128]{2,1,0:T(8,128)}) custom-call(s32[64,128]{1,0:T(8,128)} %bitcast.45, f32[128,8,128]{2,1,0:T(8,128)S(1)} %all_to_all.10.recv_ref, f32[128,16,128]{2,1,0:T(8,128)S(1)} %bitcast.40, f32[128,16,128]{2,1,0:T(8,128)} %bitcast.43, ...), custom_call_target="tpu_custom_call" | custom-call | tf_op jit(solution)/shard_map/pallas_call | solution.py:342
  34.8 4.6 %all-to-all-start.1 = ((f32[128,2,128]{2,1,0:T(2,128)}), f32[128,2,128]{2,1,0:T(2,128)S(1)}, u32[]{:S(2)}, u32[]{:S(2)}) async-start(f32[128,2,128]{2,1,0:T(2,128)} %bitcast.21), calls=%async_computation.1 | async-start | bytes 262144 | tf_op jit(solution)/shard_map/all_to_all | solution.py:302
  39.4 1.0 %copy.20 = f32[2,64,4,512]{3,2,1,0:T(4,128)} copy(f32[2,64,4,512]{3,2,1,0:T(4,128)S(1)} %bitcast.39) | data formatting | bytes 2097152
  40.4 1.0 %copy.21 = f32[2,64,4,512]{3,2,1,0:T(4,128)} copy(f32[2,64,4,512]{3,2,1,0:T(4,128)S(1)} %bitcast.38) | data formatting | bytes 2097152
  41.4 0.0 copy-start.1
  41.4 0.0 copy-start.2
  41.4 1.0 %copy.22 = f32[2,64,4,512]{3,2,1,0:T(4,128)} copy(f32[2,64,4,512]{3,2,1,0:T(4,128)S(1)} %bitcast.37) | data formatting | bytes 2097152
  42.4 6.7 %all-to-all-done.1 = f32[128,2,128]{2,1,0:T(2,128)S(1)} async-done(((f32[128,2,128]{2,1,0:T(2,128)}), f32[128,2,128]{2,1,0:T(2,128)S(1)}, u32[]{:S(2)}, u32[]{:S(2)}) %all-to-all-start.1) | async-done | bytes 131104 | tf_op jit(solution)/shard_map/all_to_all | solution.py:302
  49.0 0.0 copy-done.1
  49.0 0.0 copy-done.2
  49.0 1.1 %shard_map.131 = f32[16,512]{1,0:T(8,128)} custom-call(f32[32,8,128]{2,1,0:T(8,128)S(1)} %bitcast.41, f32[8,64]{1,0:T(8,128)S(1)} %bitcast.42, f32[16,64]{1,0:T(8,128)S(1)} %copy-done.1), custom_call_target="tpu_custom_call" | custom-call | tf_op jit(solution)/shard_map/pallas_call | solution.py:362
Async XLA Ops:
  0.6 25.7 %copy-start = (f32[2,64,4,512]{3,2,1,0:T(4,128)S(1)}, f32[2,64,4,512]{3,2,1,0:T(4,128)}, u32[]{:S(2)}) copy-start(f32[2,64,4,512]{3,2,1,0:T(4,128)} %param.10) | copy-start | bytes 3145732
  34.8 14.2 %all-to-all-start.1 = ((f32[128,2,128]{2,1,0:T(2,128)}), f32[128,2,128]{2,1,0:T(2,128)S(1)}, u32[]{:S(2)}, u32[]{:S(2)}) async-start(f32[128,2,128]{2,1,0:T(2,128)} %bitcast.21), calls=%async_computation.1 | async-start | bytes 262144 | tf_op jit(solution)/shard_map/all_to_all | solution.py:302
  41.4 7.6 %copy-start.1 = (f32[16,64]{1,0:T(8,128)S(1)}, f32[16,64]{1,0:T(8,128)}, u32[]{:S(2)}) copy-start(f32[16,64]{1,0:T(8,128)} %wout_ref.1) | copy-start | bytes 12292
  41.4 7.6 %copy-start.2 = (f32[64,8]{0,1:T(8,128)S(1)}, f32[64,8]{0,1:T(8,128)}, u32[]{:S(2)}) copy-start(f32[64,8]{0,1:T(8,128)} %param.18) | copy-start | bytes 6148

commit v7 on v6

v7 whole, which is shorter than its diff:
```python
import jax
import jax.numpy as jnp
from jax import lax
from jax.experimental import pallas as pl
from jax.experimental.pallas import tpu as pltpu
from jax.sharding import PartitionSpec as P

beta_one = 0.9
beta_two = 0.99
learn_rate = 0.01
adam_eps = 1e-15

LANES = 128
RUN = 32
VMEM_LIMIT = 16 << 20
f32, bf16, i32 = jnp.float32, jnp.bfloat16, jnp.int32


def iota(shape, axis):
    return lax.broadcasted_iota(i32, shape, axis)


def lane_blocks(pieces):
    lane = iota(pieces[0].shape, 1)
    for width in (2 * RUN, RUN):
        low = (lane & width) == 0
        step = width // RUN
        results = list(pieces)
        for one in range(4):
            if not one & step:
                x, y = pieces[one], pieces[one + step]
                results[one] = jnp.where(low, x, pltpu.roll(y, width, 1))
                results[one + step] = jnp.where(low, pltpu.roll(x, LANES - width, 1), y)
        pieces = results
    return pieces


def tile_blocks(value):
    shift = (iota((8, LANES), 0) // 2 - iota((8, LANES), 1) // RUN) & 3
    result = value
    for d in range(1, 4):
        moved = pltpu.roll(pltpu.roll(value, 2 * d, 0), LANES - RUN * d, 1)
        result = jnp.where(shift == d, moved, result)
    return result


def start_all(sources, targets, sems):
    copies = [pltpu.make_async_copy(x, y, sems.at[n]) for n, (x, y) in enumerate(zip(sources, targets))]
    for copy in copies:
        copy.start()
    return copies


def wait_all(copies):
    for copy in copies:
        copy.wait()


def pack_kernel(slot_hbm, corners_hbm, fractions_hbm, cot_hbm, out_ref, slot_ref, corners_ref, fractions_ref, cot_ref, sems):
    wait_all(
        start_all(
            (slot_hbm, corners_hbm, fractions_hbm, cot_hbm), (slot_ref, corners_ref, fractions_ref, cot_ref), sems
        )
    )
    groups = [corners_ref[0].astype(f32), corners_ref[1].astype(f32)]
    for level in range(2):
        rows = [slot_ref[level : level + 1, :].astype(f32)]
        rows += [fractions_ref[d, level : level + 1, :] for d in range(3)]
        rows += [cot_ref[level]]
        groups.append(jnp.concatenate(rows, axis=0))
    for v in range(4):
        lanes = slice(v * LANES, (v + 1) * LANES)
        for p, value in enumerate(lane_blocks([g[:, lanes] for g in groups])):
            for t in range(4):
                out_ref[16 * t + 4 * v + p] = value


def gather_lanes(value, index):
    return jnp.take_along_axis(value, index, axis=1, mode="promise_in_bounds")


class Half:
    def __init__(self, recv_ref, corner_ref, aux_ref, slots_ref, hat_ref, key_ref, column_ref, cot_ref):
        self.recv_ref, self.corner_ref, self.aux_ref, self.slots_ref = recv_ref, corner_ref, aux_ref, slots_ref
        self.hat_ref, self.key_ref, self.column_ref, self.cot_ref = hat_ref, key_ref, column_ref, cot_ref
        self.entries = [(iota((16, LANES), 0) + 16 * i).astype(f32).astype(bf16) for i in range(8)]
        self.owns = [((iota((16, LANES), 0) & 7) // 4 + 2 * i).astype(f32).astype(bf16) for i in range(8)]
        self.one = jnp.ones((16, LANES), bf16)
        self.none = jnp.zeros((16, LANES), bf16)
        self.sub = iota((8, LANES), 0)

    def count(self, unroll):
        def unpack(t, carry):
            for v in range(4):
                rows = lane_blocks([self.recv_ref[t * 16 + 4 * v + p] for p in range(4)])
                self.corner_ref[t, v] = rows[0]
                self.corner_ref[4 + t, v] = rows[1]
                self.aux_ref[t, v] = rows[2]
                self.aux_ref[4 + t, v] = rows[3]
            return carry

        lax.fori_loop(0, 4, unpack, 0, unroll=unroll)
        first_slot = (lax.axis_index("table") * 64).astype(f32)
        self.hits = []
        for v in range(4):
            slot = jnp.concatenate([self.aux_ref[lt, v, 0:1, :] for lt in range(8)], axis=0)
            self.hits.append(jnp.where((slot >= first_slot) & (slot < first_slot + 64.0), 1.0, 0.0))
        row, column = iota((LANES, 2 * LANES), 0), iota((LANES, 2 * LANES), 1)
        upper = jnp.where(row <= column, 1.0, 0.0).astype(bf16)
        hits = jnp.concatenate(self.hits, axis=0).astype(bf16)
        counts = jnp.dot(hits, upper, preferred_element_type=f32).astype(i32)
        self.through = [counts[8 * v : 8 * v + 8, :LANES] for v in range(4)]
        self.before = [jnp.zeros((8, LANES), i32)]
        for v in range(4):
            self.before.append(self.before[v] + counts[8 * v : 8 * v + 8, LANES:])
        self.total = self.before[4]

    def gather(self, step, unroll):
        for v in range(4):
            rank = self.before[v] + self.through[v] - 1 - step * LANES
            inside = (self.hits[v] > 0.5) & (rank >= 0) & (rank < LANES)
            self.slots_ref[v] = jnp.where(inside, rank, -1)
        lax.fori_loop(0, 8, self.compact, 0, unroll=unroll)

    def compact(self, lt, carry):
        high, low, chosen = [], [], []
        for v in range(4):
            piece = jnp.concatenate([self.corner_ref[lt, v], self.aux_ref[lt, v]], axis=0)
            high.append(piece.astype(bf16))
            low.append((piece - high[v].astype(f32)).astype(bf16))
            slot = jnp.broadcast_to(self.slots_ref[v, pl.ds(lt, 1), :].astype(f32), (16, LANES)).astype(bf16)
            chosen.append(
                jnp.concatenate([jnp.where(slot == self.entries[i], self.one, self.none) for i in range(8)], axis=0)
            )
        rows = jnp.concatenate([jnp.concatenate(high, axis=1), jnp.concatenate(low, axis=1)], axis=0)
        both = lax.dot_general(
            rows, jnp.concatenate(chosen, axis=1), (((1,), (1,)), ((), ())), preferred_element_type=f32
        )
        corner, aux = both[:8] + both[16:24], both[8:16] + both[24:]
        hat = None
        for d in range(3):
            f = jnp.broadcast_to(aux[1 + d : 2 + d], (8, LANES))
            factor = jnp.where((self.sub >> d) & 1 == 1, f, 1.0 - f)
            hat = factor if hat is None else hat * factor
        entry = corner.astype(i32)
        self.hat_ref[lt] = hat
        self.key_ref[lt] = ((aux[0:1].astype(i32) & 3) * 4 + (entry >> 7)).astype(f32)
        self.column_ref[lt] = (entry & 127).astype(f32)
        self.cot_ref[lt] = jnp.where(self.sub < 4, pltpu.roll(aux, 4, 0), aux)
        return carry

    def hot_rows(self, lt):
        pieces = []
        for c in range(8):
            wanted = jnp.broadcast_to(self.column_ref[lt, c : c + 1, :], (16, LANES)).astype(bf16)
            pieces.append(
                jnp.concatenate([jnp.where(wanted == self.entries[i], self.one, self.none) for i in range(8)], axis=0)
            )
        return jnp.concatenate(pieces, axis=1)

    def accumulate(self, grad_ref, blocks):
        def one_group(lt, carry):
            cot = self.cot_ref[lt]
            columns = []
            for c in range(8):
                value = cot * self.hat_ref[lt, c : c + 1, :]
                high = value.astype(bf16).astype(f32)
                both = jnp.concatenate([high, value - high], axis=0).astype(bf16)
                key = jnp.broadcast_to(self.key_ref[lt, c : c + 1, :], (16, LANES)).astype(bf16)
                columns.append(
                    jnp.concatenate([jnp.where(key == self.owns[i], both, self.none) for i in range(8)], axis=0)
                )
            sums = lax.dot_general(
                jnp.concatenate(columns, axis=1), self.hot_rows(lt), (((1,), (1,)), ((), ())),
                preferred_element_type=f32,
            )
            for slot in range(4):
                block = blocks(lt, slot)
                for half in range(2):
                    at = 32 * slot + 16 * half
                    grad_ref[block, 8 * half : 8 * half + 8, :] += sums[at : at + 8] + sums[at + 8 : at + 16]
            return carry

        return one_group

    def look(self, table_ref, found_ref, blocks):
        parity = self.sub // 4

        def one_group(lt, carry):
            rows = jnp.concatenate([table_ref[blocks(lt, slot)] for slot in range(4)], axis=0)
            high = rows.astype(bf16)
            low = (rows - high.astype(f32)).astype(bf16)
            hot = self.hot_rows(lt)
            seen = jnp.dot(
                jnp.concatenate([high, low], axis=1), jnp.concatenate([hot, hot], axis=0), preferred_element_type=f32
            )
            total = jnp.zeros((8, LANES), f32)
            for c in range(8):
                own = jnp.broadcast_to(self.key_ref[lt, c : c + 1, :], (8, LANES))
                picked = jnp.zeros((8, LANES), f32)
                for i in range(8):
                    mask = own == (parity + 2 * i).astype(f32)
                    picked = jnp.where(mask, seen[8 * i : 8 * i + 8, c * LANES : (c + 1) * LANES], picked)
                total = total + picked * self.hat_ref[lt, c : c + 1, :]
            found_ref[lt] = total + pltpu.roll(total, 4, 0)
            return carry

        return one_group

    def spread(self, found_ref, result_ref):
        def one_group(t, carry):
            value = jnp.where(self.sub < 4, found_ref[t], found_ref[4 + t])
            for v in range(4):
                zero = jnp.broadcast_to(self.slots_ref[v, pl.ds(t, 1), :], (8, LANES))
                one = jnp.broadcast_to(self.slots_ref[v, pl.ds(4 + t, 1), :], (8, LANES))
                place = jnp.where(self.sub < 4, zero, one)
                taken = gather_lanes(value, jnp.maximum(place, 0))
                result_ref[t * 4 + v] += jnp.where(place >= 0, taken, 0.0)
            return carry

        return one_group


def passes_of(total):
    return (jnp.max(total) + (LANES - 1)) // LANES


def block_finder(ids_ref, other):
    mine = lax.axis_index("table")
    owner = mine * lax.axis_size("ray") + lax.axis_index("ray")
    parity = (mine + other) % 2

    def blocks(lt, slot):
        level, group = lt // 4, 2 * (lt % 4) + parity
        return level * 64 + ids_ref[(group * 2 + level) * 4 + slot, owner]

    return blocks


def gradients(half, grad_ref, blocks, ready):
    half.count(4)
    half.gather(0, 4)
    ready()
    step = half.accumulate(grad_ref, blocks)
    lax.fori_loop(0, 8, step, 0, unroll=4)
    passes = passes_of(half.total)

    def again(number, carry):
        half.gather(number, 1)
        return lax.fori_loop(0, 8, step, carry)

    lax.fori_loop(1, passes, again, 0)

    @pl.when(passes > 1)
    def _():
        half.gather(0, 1)

    return passes


def first_kernel(
    ids_hbm, recv_ref, m1_hbm, m2_hbm,
    grad_ref, slots_ref, hat_ref, key_ref, column_ref, total_ref, m1_ref, m2_ref,
    ids_ref, corner_ref, aux_ref, cot_ref, sems,
):
    loads = start_all((ids_hbm, m1_hbm, m2_hbm), (ids_ref, m1_ref, m2_ref), sems)
    grad_ref[...] = jnp.zeros_like(grad_ref)
    half = Half(recv_ref, corner_ref, aux_ref, slots_ref, hat_ref, key_ref, column_ref, cot_ref)
    gradients(half, grad_ref, block_finder(ids_ref, 0), loads[0].wait)
    total_ref[...] = half.total
    wait_all(loads[1:])


def second_kernel(
    ids_hbm, recv_ref, before_ref, table_ref, m1_ref, m2_ref,
    tnew_ref, m1new_ref, m2new_ref, out_ref,
    ids_ref, grad_ref, corner_ref, aux_ref, slots_ref, hat_ref, key_ref, column_ref, cot_ref,
    found_ref, result_ref, sem,
):
    (load,) = start_all((ids_hbm,), (ids_ref,), sem)
    grad_ref[...] = before_ref[...]
    result_ref[...] = jnp.zeros_like(result_ref)
    half = Half(recv_ref, corner_ref, aux_ref, slots_ref, hat_ref, key_ref, column_ref, cot_ref)
    blocks = block_finder(ids_ref, 1)
    passes = gradients(half, grad_ref, blocks, load.wait)

    def update(step, carry):
        at = pl.ds(step * 4, 4)
        grad = grad_ref[at]
        first = beta_one * m1_ref[at] + (1.0 - beta_one) * grad
        second = beta_two * m2_ref[at] + (1.0 - beta_two) * grad * grad
        m1new_ref[at] = first
        m2new_ref[at] = second
        tnew_ref[at] = table_ref[at] - learn_rate * first / (jnp.sqrt(second) + adam_eps)
        return carry

    lax.fori_loop(0, 32, update, 0)
    look, spread = half.look(tnew_ref, found_ref, blocks), half.spread(found_ref, result_ref)
    lax.fori_loop(0, 8, look, 0, unroll=4)
    lax.fori_loop(0, 4, spread, 0, unroll=2)

    def again(number, carry):
        half.gather(number, 1)
        lax.fori_loop(0, 8, look, 0)
        return lax.fori_loop(0, 4, spread, carry)

    lax.fori_loop(1, passes, again, 0)
    for m in range(16):
        out_ref[m] = tile_blocks(result_ref[m])


def third_kernel(
    ids_hbm, recv_ref, tnew_ref, slots_ref, hat_ref, key_ref, column_ref, total_ref,
    out_ref,
    ids_ref, corner_ref, aux_ref, slots_s, hat_s, key_s, column_s, cot_s, found_ref, result_ref, sem,
):
    (load,) = start_all((ids_hbm,), (ids_ref,), sem)
    result_ref[...] = jnp.zeros_like(result_ref)
    half = Half(recv_ref, corner_ref, aux_ref, slots_ref, hat_ref, key_ref, column_ref, cot_s)
    blocks = block_finder(ids_ref, 0)
    load.wait()
    lax.fori_loop(0, 8, half.look(tnew_ref, found_ref, blocks), 0, unroll=4)
    lax.fori_loop(0, 4, half.spread(found_ref, result_ref), 0, unroll=2)
    passes = passes_of(total_ref[...])

    @pl.when(passes > 1)
    def _():
        more = Half(recv_ref, corner_ref, aux_ref, slots_s, hat_s, key_s, column_s, cot_s)
        more.count(1)
        look, spread = more.look(tnew_ref, found_ref, blocks), more.spread(found_ref, result_ref)

        def again(number, carry):
            more.gather(number, 1)
            lax.fori_loop(0, 8, look, 0)
            return lax.fori_loop(0, 4, spread, carry)

        lax.fori_loop(1, passes, again, 0)

    for m in range(16):
        out_ref[m] = tile_blocks(result_ref[m])


def network_kernel(recv_ref, win_ref, wout_ref, out_ref):
    columns = []
    for v in range(4):
        total = recv_ref[v]
        for t in range(1, 4):
            total = total + recv_ref[4 * t + v]
        columns.append(tile_blocks(total))
    encoded = jnp.concatenate(columns, axis=1)
    hidden = jnp.maximum(
        lax.dot_general(
            win_ref[...], encoded, (((0,), (0,)), ((), ())),
            precision=lax.Precision.HIGHEST, preferred_element_type=f32,
        ),
        0.0,
    )
    out_ref[...] = jnp.dot(wout_ref[...], hidden, precision=lax.Precision.HIGHEST, preferred_element_type=f32)


VMEM = pl.BlockSpec(memory_space=pltpu.VMEM)
HBM = pl.BlockSpec(memory_space=pltpu.HBM)


def call(kernel, outs, in_specs, scratch=(), out_specs=None, **extra):
    return pl.pallas_call(
        kernel,
        out_shape=[jax.ShapeDtypeStruct(*o) if isinstance(o, tuple) else o for o in outs],
        in_specs=in_specs,
        out_specs=[VMEM] * len(outs) if out_specs is None else out_specs,
        scratch_shapes=list(scratch),
        compiler_params=pltpu.CompilerParams(vmem_limit_bytes=VMEM_LIMIT),
        **extra,
    )


def in_hbm(*arrays):
    return [pltpu.with_memory_space_constraint(array, pltpu.HBM) for array in arrays]


def exchange(value):
    tables, rays = lax.axis_size("table"), lax.axis_size("ray")
    groups = [[t * rays + r for t in range(core, tables, 2) for r in range(rays)] for core in range(2)]
    return lax.all_to_all(
        value, ("table", "ray"), split_axis=0, concat_axis=0, tiled=True, axis_index_groups=groups
    )


def swap_cores(value):
    return lax.ppermute(value, "table", [(t, t ^ 1) for t in range(lax.axis_size("table"))])


def rows_of(array):
    levels, blocks = array.shape[:2]
    return array.reshape(levels, blocks, 4, 4, LANES).transpose(0, 1, 3, 2, 4).reshape(levels * blocks, 16, LANES)


def rows_back(array, shape):
    levels, blocks = shape[:2]
    return array.reshape(levels, blocks, 4, 4, LANES).transpose(0, 1, 3, 2, 4).reshape(shape)


def on_device(
    table,
    moment1,
    moment2,
    block_ids,
    sample_slot,
    corners,
    fractions,
    feat_cot,
    weight_in,
    weight_out,
):
    (packed,) = call(
        pack_kernel,
        [((64, 8, LANES), f32)],
        [HBM] * 4,
        [
            pltpu.VMEM((2, 512), i32),
            pltpu.VMEM((2, 8, 512), i32),
            pltpu.VMEM((3, 2, 512), f32),
            pltpu.VMEM((2, 4, 512), f32),
            pltpu.SemaphoreType.DMA((4,)),
        ],
    )(*in_hbm(sample_slot, corners, fractions.transpose(1, 0, 2), feat_cot))
    samples = exchange(packed)
    others = swap_cores(samples)
    rows = (128, 16, LANES)
    (ids,) = in_hbm(block_ids.transpose(0, 1, 3, 2).reshape(64, 128))
    tile = pltpu.VMEM((8, 8, LANES), f32)
    lists = pltpu.VMEM((4, 8, LANES), i32)
    full = pltpu.VMEM(rows, f32)
    data = pltpu.VMEM((8, 4, 8, LANES), f32)
    wide = pltpu.VMEM((16, 8, LANES), f32)
    id_table = pltpu.SMEM((64, LANES), i32)
    grad, slots, hat, key, column, total, m1, m2 = call(
        first_kernel,
        [full, lists, tile, tile, tile, pltpu.VMEM((8, LANES), i32), full, full],
        [HBM, VMEM, HBM, HBM],
        [id_table, data, data, tile, pltpu.SemaphoreType.DMA((3,))],
        cost_estimate=pl.CostEstimate(flops=1 << 30, bytes_accessed=4 << 20, transcendentals=0),
    )(ids, samples, *in_hbm(rows_of(moment1), rows_of(moment2)))
    tnew, m1new, m2new, found_other = call(
        second_kernel,
        [full, full, full, ((16, 8, LANES), f32)],
        [HBM] + [VMEM] * 5,
        [id_table, full, data, data, lists, tile, tile, tile, tile, tile, wide, pltpu.SemaphoreType.DMA((1,))],
    )(ids, others, grad, rows_of(table), m1, m2)
    partner = swap_cores(found_other)
    (found_own,) = call(
        third_kernel,
        [((16, 8, LANES), f32)],
        [HBM] + [VMEM] * 7,
        [id_table, data, data, lists, tile, tile, tile, tile, tile, wide, pltpu.SemaphoreType.DMA((1,))],
        cost_estimate=pl.CostEstimate(flops=1 << 30, bytes_accessed=4 << 20, transcendentals=0),
    )(ids, samples, tnew, slots, hat, key, column, total)
    found = found_own + partner
    back = exchange(found.reshape(64, 2, LANES)).reshape(16, 8, LANES)
    (mlp_out,) = call(network_kernel, [((16, 512), f32)], [VMEM] * 3)(back, weight_in.T, weight_out)
    shape = table.shape
    return (rows_back(tnew, shape), rows_back(m1new, shape), rows_back(m2new, shape), mlp_out)


def solution(mesh):
    in_specs = (
        P(None, ("table", "ray"), None, None),
        P(None, ("table", "ray"), None, None),
        P(None, ("table", "ray"), None, None),
        P(),
        P(None, ("table", "ray")),
        P(None, None, ("table", "ray")),
        P(None, None, ("table", "ray")),
        P(None, None, ("table", "ray")),
        P(),
        P(),
    )
    out_specs = (
        P(None, ("table", "ray"), None, None),
        P(None, ("table", "ray"), None, None),
        P(None, ("table", "ray"), None, None),
        P(None, ("table", "ray")),
    )
    return jax.shard_map(
        on_device, mesh=mesh, in_specs=in_specs, out_specs=out_specs, check_vma=False
    )
```

time: 51 us -> 50.8 us (level)
  blocking collectives: 24.6 us -> 21.9 us
  Pallas kernels: 10.7 us -> 12 us
  starting transfers between devices: 4.61 us -> 5.48 us
  other arithmetic: 0 us -> 0.64 us
    all_to_all x1, blocking collectives: 24.6 us -> 21.9 us  [exchange(): lax.all_to_all(value, ('table', 'ray'), split_axis=0, concat_axis=0, tile...]
    pallas_call x2 -> x4, Pallas kernels: 9.61 us -> 10.9 us  [the longest x1 4.82 us: on_device(): call(second_kernel, [full, full, full, ((16, 8, LANES), f32)], [HBM] + [V...]
    add x0 -> x1, other arithmetic: none -> 0.64 us  [on_device(): found = found_own + partner]
    ppermute x0 -> x2, starting transfers between devices: none -> 0.59 us  [swap_cores(): lax.ppermute(value, 'table', [(t, t ^ 1) for t in range(lax.axis_size('ta...]
  transfers between devices with their start and end apart: 1 -> 3, of which waited for: 1 -> 1; matrix products, arithmetic and copies ran while one was open for 6% -> 6% of each run, Pallas kernels for 0% -> 10%
where the time goes in v7:
time: 50.8 us; the launch traced here: 50.4 us
  blocking collectives  21.9 us (43%)
  Pallas kernels  12 us (24%)
  waiting for transfers between devices  6.68 us (13%)
  starting transfers between devices  5.48 us (11%)
  local copies, waits for them, and re-layouts  2.92 us (6%)
  between operations  0.7 us (1%)
  other arithmetic  0.64 us (1%)
    all_to_all x1, blocking collectives, exchange(): lax.all_to_all(value, ('table', 'ray'), split_axis=0, concat_axis=0, tile...  21.9 us
    all_to_all x1, waiting for transfers between devices, exchange(): lax.all_to_all(value, ('table', 'ray'), split_axis=0, concat_axis=0, tile...  6.68 us
    all_to_all x1, starting transfers between devices, exchange(): lax.all_to_all(value, ('table', 'ray'), split_axis=0, concat_axis=0, tile...  4.89 us
    pallas_call x1, Pallas kernels, on_device(): call(second_kernel, [full, full, full, ((16, 8, LANES), f32)], [HBM] + [V...  4.82 us
    unnamed x9, local copies, waits for them, and re-layouts  2.92 us
    pallas_call x1, Pallas kernels, on_device(): call(third_kernel, [((16, 8, LANES), f32)], [HBM] + [VMEM] * 7, [id_table...  2.64 us
    pallas_call x1, Pallas kernels, on_device(): call(first_kernel, [full, lists, tile, tile, tile, pltpu.VMEM((8, LANES),...  2.47 us
    pallas_call x1, Pallas kernels, on_device(): call(network_kernel, [((16, 512), f32)], [VMEM] * 3)  1.13 us
  transfers between devices with their start and end apart: 3, of which 1 were waited for; matrix products, arithmetic and copies ran while one was open for 6% of the time, Pallas kernels for 10%

profile of v7, /device:TPU:0, one launch (start us, length us, event | category | flops | bytes accessed | tf_op | source)
XLA Modules:
  0.0 50.4 jit_solution(12671501865877642437)
XLA Ops:
  0.6 1.0 %shard_map.129 = f32[64,8,128]{2,1,0:T(8,128)S(1)} custom-call(s32[2,512]{1,0:T(2,128)} %slot_hbm.1, s32[2,8,512]{2,1,0:T(8,128)} %corners_hbm.1, f32[3,2,512]{2,1,0:T(2,128)} %bitcast.46, f32[2,4,512]{2,1,0:T(4,128)} %cot_hbm.1), custom_call_target="tpu_custom_call" | custom-call | tf_op jit(solution)/shard_map/pallas_call | solution.py:415
  1.6 21.9 %all_to_all.10.recv_ref = f32[64,8,128]{2,1,0:T(8,128)S(1)} all-to-all(f32[64,8,128]{2,1,0:T(8,128)S(1)} %shard_map.129), channel_id=1, replica_groups={{0,1,2,3,4,5,6,7,8,9,10,11,12,13,14,15,32,33,34,35,36,37,38,39,40,41,42..., dimensions={0} | all-to-all | bytes 524288 | tf_op jit(solution)/shard_map/all_to_all | solution.py:384
  23.5 0.0 collective-permute-start
  23.5 0.0 copy-start
  23.5 2.5 %shard_map.130 = (f32[128,16,128]{2,1,0:T(8,128)S(1)}, s32[4,8,128]{2,1,0:T(8,128)S(1)}, f32[8,8,128]{2,1,0:T(8,128)S(1)}, f32[8,8,128]{2,1,0:T(8,128)S(1)}, f32...) custom-call(s32[64,128]{1,0:T(8,128)} %bitcast.43, ...), custom_call_target="tpu_custom_call" | custom-call | flops 1073741824 | bytes 4194304 | tf_op jit(solution)/shard_map/pallas_call | solution.py:437
  26.0 0.0 collective-permute-done.recv_ref
  26.0 0.0 copy-done
  26.0 4.8 %shard_map.131 = (f32[128,16,128]{2,1,0:T(8,128)S(1)}, f32[128,16,128]{2,1,0:T(8,128)S(1)}, f32[128,16,128]{2,1,0:T(8,128)S(1)}, f32[16,8,128]{2,1,0:T(8,128)S(1)}) custom-call(s32[64,128]{1,0:T(8,128)} %bitcast.44, f32[64,8,128]{2,1,0:T(8,128)S(1)} %collective-permute-done.recv_ref, f32[128,16,128]{2,1,0:T(8,128)S(1)} %get-tuple-element.16.before_ref, ...), custom_call_target="tpu_custom_call" | custom-call | tf_op jit(solution)/shard_map/pallas_call | solution.py:444
  30.8 0.6 %collective-permute-start.1 = (f32[16,8,128]{2,1,0:T(8,128)S(1)}, f32[16,8,128]{2,1,0:T(8,128)S(1)}, u32[]{:S(2)}, u32[]{:S(2)}) collective-permute-start(f32[16,8,128]{2,1,0:T(8,128)S(1)} %get-tuple-element.27), channel_id=1, source_target_pairs={{0,16},{16,0},{32,48},{48,32},{64,80},{80,64},{96,112},{112,96},{1... | collective-permute-start | bytes 196616 | tf_op jit(solution)/shard_map/ppermute | solution.py:390
  31.4 2.6 %shard_map.132 = f32[16,8,128]{2,1,0:T(8,128)S(1)} custom-call(s32[64,128]{1,0:T(8,128)} %bitcast.45, f32[64,8,128]{2,1,0:T(8,128)S(1)} %all_to_all.10.recv_ref, f32[128,16,128]{2,1,0:T(8,128)S(1)} %get-tuple-element.19.tnew_ref, s32[4,8,128]{2,1,0:T(8,128)S(1)} %get-tuple-element.22.slots_ref, f32[8,8,128]{2,1,0:T(8,128)S(1)} %get-tuple-element.23.hat_ref, ...), custom_call_target="tpu_custom_call" | custom-call | flops 1073741824 | bytes 4194304 | tf_op jit(solution)/shard_map/pallas_call | solution.py:451
  34.1 0.0 collective-permute-done.1
  34.1 0.6 %add.3 = f32[16,8,128]{2,1,0:T(8,128)} add(f32[16,8,128]{2,1,0:T(8,128)S(1)} %shard_map.132, f32[16,8,128]{2,1,0:T(8,128)S(1)} %collective-permute-done.1) | non-fusion elementwise | flops 16384 | bytes 196608 | tf_op jit(solution)/shard_map/add | solution.py:458
  34.7 4.9 %all-to-all-start.1 = ((f32[64,2,128]{2,1,0:T(2,128)}), f32[64,2,128]{2,1,0:T(2,128)S(1)}, u32[]{:S(2)}, u32[]{:S(2)}) async-start(f32[64,2,128]{2,1,0:T(2,128)} %bitcast.22), calls=%async_computation.1 | async-start | bytes 131072 | tf_op jit(solution)/shard_map/all_to_all | solution.py:384
  39.6 1.0 %copy.21 = f32[2,64,4,512]{3,2,1,0:T(4,128)} copy(f32[2,64,4,512]{3,2,1,0:T(4,128)S(1)} %bitcast.39) | data formatting | bytes 2097152
  40.6 1.0 %copy.22 = f32[2,64,4,512]{3,2,1,0:T(4,128)} copy(f32[2,64,4,512]{3,2,1,0:T(4,128)S(1)} %bitcast.38) | data formatting | bytes 2097152
  41.6 0.0 copy-start.1
  41.6 0.0 copy-start.2
  41.6 1.0 %copy.20 = f32[2,64,4,512]{3,2,1,0:T(4,128)} copy(f32[2,64,4,512]{3,2,1,0:T(4,128)S(1)} %bitcast.37) | data formatting | bytes 2097152
  42.5 6.7 %all-to-all-done.1 = f32[64,2,128]{2,1,0:T(2,128)S(1)} async-done(((f32[64,2,128]{2,1,0:T(2,128)}), f32[64,2,128]{2,1,0:T(2,128)S(1)}, u32[]{:S(2)}, u32[]{:S(2)}) %all-to-all-start.1) | async-done | bytes 65568 | tf_op jit(solution)/shard_map/all_to_all | solution.py:384
  49.2 0.0 copy-done.1
  49.2 0.0 copy-done.2
  49.2 1.1 %shard_map.133 = f32[16,512]{1,0:T(8,128)} custom-call(f32[16,8,128]{2,1,0:T(8,128)S(1)} %bitcast.41, f32[8,64]{1,0:T(8,128)S(1)} %bitcast.42, f32[16,64]{1,0:T(8,128)S(1)} %copy-done.1), custom_call_target="tpu_custom_call" | custom-call | tf_op jit(solution)/shard_map/pallas_call | solution.py:460
Async XLA Ops:
  23.5 2.5 %collective-permute-start = (f32[64,8,128]{2,1,0:T(8,128)S(1)}, f32[64,8,128]{2,1,0:T(8,128)S(1)}, u32[]{:S(2)}, u32[]{:S(2)}) collective-permute-start(f32[64,8,128]{2,1,0:T(8,128)S(1)} %all_to_all.10.recv_ref), channel_id=1, source_target_pairs={{0,16},{16,0},{32,48},{48,32},{64,80},{80,64},{96,112},{112,96},{1... | collective-permute-start | bytes 786440 | tf_op jit(solution)/shard_map/ppermute | solution.py:390
  23.5 2.5 %copy-start = (f32[2,64,4,512]{3,2,1,0:T(4,128)S(1)}, f32[2,64,4,512]{3,2,1,0:T(4,128)}, u32[]{:S(2)}) copy-start(f32[2,64,4,512]{3,2,1,0:T(4,128)} %param.10) | copy-start | bytes 3145732
  30.8 3.2 %collective-permute-start.1 = (f32[16,8,128]{2,1,0:T(8,128)S(1)}, f32[16,8,128]{2,1,0:T(8,128)S(1)}, u32[]{:S(2)}, u32[]{:S(2)}) collective-permute-start(f32[16,8,128]{2,1,0:T(8,128)S(1)} %get-tuple-element.27), channel_id=1, source_target_pairs={{0,16},{16,0},{32,48},{48,32},{64,80},{80,64},{96,112},{112,96},{1... | collective-permute-start | bytes 196616 | tf_op jit(solution)/shard_map/ppermute | solution.py:390
  34.7 14.5 %all-to-all-start.1 = ((f32[64,2,128]{2,1,0:T(2,128)}), f32[64,2,128]{2,1,0:T(2,128)S(1)}, u32[]{:S(2)}, u32[]{:S(2)}) async-start(f32[64,2,128]{2,1,0:T(2,128)} %bitcast.22), calls=%async_computation.1 | async-start | bytes 131072 | tf_op jit(solution)/shard_map/all_to_all | solution.py:384
  41.6 7.7 %copy-start.1 = (f32[16,64]{1,0:T(8,128)S(1)}, f32[16,64]{1,0:T(8,128)}, u32[]{:S(2)}) copy-start(f32[16,64]{1,0:T(8,128)} %wout_ref.1) | copy-start | bytes 12292
  41.6 7.7 %copy-start.2 = (f32[64,8]{0,1:T(8,128)S(1)}, f32[64,8]{0,1:T(8,128)}, u32[]{:S(2)}) copy-start(f32[64,8]{0,1:T(8,128)} %param.18) | copy-start | bytes 6148

commit v8 on v7

--- a/solution.py
+++ b/solution.py
@@ -272,7 +272,8 @@
 
 
 def second_kernel(
-    ids_hbm, recv_ref, before_ref, table_ref, m1_ref, m2_ref,
+    ids_hbm, recv_ref, own_recv_ref, before_ref, table_ref, m1_ref, m2_ref,
+    own_slots_ref, own_hat_ref, own_key_ref, own_column_ref, own_total_ref,
     tnew_ref, m1new_ref, m2new_ref, out_ref,
     ids_ref, grad_ref, corner_ref, aux_ref, slots_ref, hat_ref, key_ref, column_ref, cot_ref,
     found_ref, result_ref, sem,
@@ -280,8 +281,9 @@
     (load,) = start_all((ids_hbm,), (ids_ref,), sem)
     grad_ref[...] = before_ref[...]
     result_ref[...] = jnp.zeros_like(result_ref)
-    half = Half(recv_ref, corner_ref, aux_ref, slots_ref, hat_ref, key_ref, column_ref, cot_ref)
-    blocks = block_finder(ids_ref, 1)
+    spare = (corner_ref, aux_ref, slots_ref, hat_ref, key_ref, column_ref, cot_ref)
+    half = Half(recv_ref, *spare)
+    blocks, own_blocks = block_finder(ids_ref, 1), block_finder(ids_ref, 0)
     passes = gradients(half, grad_ref, blocks, load.wait)
 
     def update(step, carry):
@@ -295,56 +297,43 @@
         return carry
 
     lax.fori_loop(0, 32, update, 0)
-    look, spread = half.look(tnew_ref, found_ref, blocks), half.spread(found_ref, result_ref)
-    lax.fori_loop(0, 8, look, 0, unroll=4)
-    lax.fori_loop(0, 4, spread, 0, unroll=2)
-
-    def again(number, carry):
-        half.gather(number, 1)
-        lax.fori_loop(0, 8, look, 0)
-        return lax.fori_loop(0, 4, spread, carry)
-
-    lax.fori_loop(1, passes, again, 0)
-    for m in range(16):
-        out_ref[m] = tile_blocks(result_ref[m])
-
-
-def third_kernel(
-    ids_hbm, recv_ref, tnew_ref, slots_ref, hat_ref, key_ref, column_ref, total_ref,
-    out_ref,
-    ids_ref, corner_ref, aux_ref, slots_s, hat_s, key_s, column_s, cot_s, found_ref, result_ref, sem,
-):
-    (load,) = start_all((ids_hbm,), (ids_ref,), sem)
-    result_ref[...] = jnp.zeros_like(result_ref)
-    half = Half(recv_ref, corner_ref, aux_ref, slots_ref, hat_ref, key_ref, column_ref, cot_s)
-    blocks = block_finder(ids_ref, 0)
-    load.wait()
-    lax.fori_loop(0, 8, half.look(tnew_ref, found_ref, blocks), 0, unroll=4)
-    lax.fori_loop(0, 4, half.spread(found_ref, result_ref), 0, unroll=2)
-    passes = passes_of(total_ref[...])
-
-    @pl.when(passes > 1)
-    def _():
-        more = Half(recv_ref, corner_ref, aux_ref, slots_s, hat_s, key_s, column_s, cot_s)
-        more.count(1)
-        look, spread = more.look(tnew_ref, found_ref, blocks), more.spread(found_ref, result_ref)
+    own = Half(own_recv_ref, corner_ref, aux_ref, own_slots_ref, own_hat_ref, own_key_ref, own_column_ref, cot_ref)
+    results = [result_ref.at[pl.ds(0, 16)], result_ref.at[pl.ds(16, 16)]]
+    for part, finder, result in ((own, own_blocks, results[0]), (half, blocks, results[1])):
+        lax.fori_loop(0, 8, part.look(tnew_ref, found_ref, finder), 0, unroll=4)
+        lax.fori_loop(0, 4, part.spread(found_ref, result), 0, unroll=2)
+
+    def more_passes(part, finder, result, count):
+        look, spread = part.look(tnew_ref, found_ref, finder), part.spread(found_ref, result)
 
         def again(number, carry):
-            more.gather(number, 1)
+            part.gather(number, 1)
             lax.fori_loop(0, 8, look, 0)
             return lax.fori_loop(0, 4, spread, carry)
 
-        lax.fori_loop(1, passes, again, 0)
-
-    for m in range(16):
-        out_ref[m] = tile_blocks(result_ref[m])
+        lax.fori_loop(1, count, again, 0)
+
+    more_passes(half, blocks, results[1], passes)
+    own_passes = passes_of(own_total_ref[...])
+
+    @pl.when(own_passes > 1)
+    def _():
+        again = Half(own_recv_ref, *spare)
+        again.count(1)
+        more_passes(again, own_blocks, results[0], own_passes)
+
+    core = lax.axis_index("table") % 2
+    for h in range(4):
+        for v in range(4):
+            out_ref[(2 * h + core) * 4 + v] = tile_blocks(result_ref[4 * h + v])
+            out_ref[(2 * h + 1 - core) * 4 + v] = tile_blocks(result_ref[16 + 4 * h + v])
 
 
 def network_kernel(recv_ref, win_ref, wout_ref, out_ref):
     columns = []
     for v in range(4):
         total = recv_ref[v]
-        for t in range(1, 4):
+        for t in range(1, 8):
             total = total + recv_ref[4 * t + v]
         columns.append(tile_blocks(total))
     encoded = jnp.concatenate(columns, axis=1)
@@ -378,12 +367,15 @@
     return [pltpu.with_memory_space_constraint(array, pltpu.HBM) for array in arrays]
 
 
-def exchange(value):
-    tables, rays = lax.axis_size("table"), lax.axis_size("ray")
-    groups = [[t * rays + r for t in range(core, tables, 2) for r in range(rays)] for core in range(2)]
+def exchange(value, groups=None):
     return lax.all_to_all(
         value, ("table", "ray"), split_axis=0, concat_axis=0, tiled=True, axis_index_groups=groups
     )
+
+
+def same_core():
+    tables, rays = lax.axis_size("table"), lax.axis_size("ray")
+    return [[t * rays + r for t in range(core, tables, 2) for r in range(rays)] for core in range(2)]
 
 
 def swap_cores(value):
@@ -424,7 +416,7 @@
             pltpu.SemaphoreType.DMA((4,)),
         ],
     )(*in_hbm(sample_slot, corners, fractions.transpose(1, 0, 2), feat_cot))
-    samples = exchange(packed)
+    samples = exchange(packed, same_core())
     others = swap_cores(samples)
     rows = (128, 16, LANES)
     (ids,) = in_hbm(block_ids.transpose(0, 1, 3, 2).reshape(64, 128))
@@ -432,7 +424,6 @@
     lists = pltpu.VMEM((4, 8, LANES), i32)
     full = pltpu.VMEM(rows, f32)
     data = pltpu.VMEM((8, 4, 8, LANES), f32)
-    wide = pltpu.VMEM((16, 8, LANES), f32)
     id_table = pltpu.SMEM((64, LANES), i32)
     grad, slots, hat, key, column, total, m1, m2 = call(
         first_kernel,
@@ -441,22 +432,17 @@
         [id_table, data, data, tile, pltpu.SemaphoreType.DMA((3,))],
         cost_estimate=pl.CostEstimate(flops=1 << 30, bytes_accessed=4 << 20, transcendentals=0),
     )(ids, samples, *in_hbm(rows_of(moment1), rows_of(moment2)))
-    tnew, m1new, m2new, found_other = call(
+    tnew, m1new, m2new, found = call(
         second_kernel,
-        [full, full, full, ((16, 8, LANES), f32)],
-        [HBM] + [VMEM] * 5,
-        [id_table, full, data, data, lists, tile, tile, tile, tile, tile, wide, pltpu.SemaphoreType.DMA((1,))],
-    )(ids, others, grad, rows_of(table), m1, m2)
-    partner = swap_cores(found_other)
-    (found_own,) = call(
-        third_kernel,
-        [((16, 8, LANES), f32)],
-        [HBM] + [VMEM] * 7,
-        [id_table, data, data, lists, tile, tile, tile, tile, tile, wide, pltpu.SemaphoreType.DMA((1,))],
-        cost_estimate=pl.CostEstimate(flops=1 << 30, bytes_accessed=4 << 20, transcendentals=0),
-    )(ids, samples, tnew, slots, hat, key, column, total)
-    found = found_own + partner
-    back = exchange(found.reshape(64, 2, LANES)).reshape(16, 8, LANES)
+        [full, full, full, ((32, 8, LANES), f32)],
+        [HBM] + [VMEM] * 11,
+        [
+            id_table, full, data, data, lists, tile, tile, tile, tile, tile,
+            pltpu.VMEM((32, 8, LANES), f32),
+            pltpu.SemaphoreType.DMA((1,)),
+        ],
+    )(ids, others, samples, grad, rows_of(table), m1, m2, slots, hat, key, column, total)
+    back = exchange(found.reshape(128, 2, LANES)).reshape(32, 8, LANES)
     (mlp_out,) = call(network_kernel, [((16, 512), f32)], [VMEM] * 3)(back, weight_in.T, weight_out)
     shape = table.shape
     return (rows_back(tnew, shape), rows_back(m1new, shape), rows_back(m2new, shape), mlp_out)

time: 50.8 us -> 49.3 us (0.970); the launches traced: 50.4 us -> 48.3 us
  starting transfers between devices: 5.48 us -> 4.67 us
  other arithmetic: 0.64 us -> 0 us
    add x1 -> x0, other arithmetic: 0.64 us -> none  [on_device(): found = found_own + partner]
    ppermute x2 -> x1, starting transfers between devices: 0.59 us -> 0.01 us  [swap_cores(): lax.ppermute(value, 'table', [(t, t ^ 1) for t in range(lax.axis_size('ta...]
    pallas_call x2 -> x1, Pallas kernels: 7.46 us -> 6.92 us  [on_device(): call(second_kernel, [full, full, full, ((32, 8, LANES), f32)], [HBM] + [V...]
  transfers between devices with their start and end apart: 3 -> 2, of which waited for: 1 -> 1; matrix products, arithmetic and copies ran while one was open for 6% -> 6% of each run, Pallas kernels for 10% -> 5%
where the time goes in v8:
time: 49.3 us; the launch traced here: 48.3 us
  blocking collectives  21.9 us (44%)
  Pallas kernels  11.5 us (23%)
  waiting for transfers between devices  6.67 us (14%)
  starting transfers between devices  4.67 us (9%)
  local copies, waits for them, and re-layouts  2.92 us (6%)
  between operations  0.69 us (1%)
    all_to_all x1, blocking collectives, exchange(): lax.all_to_all(value, ('table', 'ray'), split_axis=0, concat_axis=0, tile...  21.9 us
    pallas_call x1, Pallas kernels, on_device(): call(second_kernel, [full, full, full, ((32, 8, LANES), f32)], [HBM] + [V...  6.92 us
    all_to_all x1, waiting for transfers between devices, exchange(): lax.all_to_all(value, ('table', 'ray'), split_axis=0, concat_axis=0, tile...  6.67 us
    all_to_all x1, starting transfers between devices, exchange(): lax.all_to_all(value, ('table', 'ray'), split_axis=0, concat_axis=0, tile...  4.66 us
    unnamed x9, local copies, waits for them, and re-layouts  2.92 us
    pallas_call x1, Pallas kernels, on_device(): call(first_kernel, [full, lists, tile, tile, tile, pltpu.VMEM((8, LANES),...  2.47 us
    pallas_call x1, Pallas kernels, on_device(): call(network_kernel, [((16, 512), f32)], [VMEM] * 3)  1.13 us
  transfers between devices with their start and end apart: 2, of which 1 were waited for; matrix products, arithmetic and copies ran while one was open for 6% of the time, Pallas kernels for 5%

profile of v8, /device:TPU:0, one launch (start us, length us, event | category | flops | bytes accessed | tf_op | source)
XLA Modules:
  0.0 48.3 jit_solution(11002280060720440268)
XLA Ops:
  0.6 1.0 %shard_map.129 = f32[64,8,128]{2,1,0:T(8,128)S(1)} custom-call(s32[2,512]{1,0:T(2,128)} %slot_hbm.1, s32[2,8,512]{2,1,0:T(8,128)} %corners_hbm.1, f32[3,2,512]{2,1,0:T(2,128)} %bitcast.45, f32[2,4,512]{2,1,0:T(4,128)} %cot_hbm.1), custom_call_target="tpu_custom_call" | custom-call | tf_op jit(solution)/shard_map/pallas_call | solution.py:407
  1.6 21.9 %all_to_all.10.recv_ref.own_recv_ref = f32[64,8,128]{2,1,0:T(8,128)S(1)} all-to-all(f32[64,8,128]{2,1,0:T(8,128)S(1)} %shard_map.129), channel_id=1, replica_groups={{0,1,2,3,4,5,6,7,8,9,10,11,12,13,14,15,32,33,34,35,36,37,38,39,40,41,42..., dimensions={0} | all-to-all | bytes 524288 | tf_op jit(solution)/shard_map/all_to_all | solution.py:371
  23.5 0.0 collective-permute-start
  23.5 0.0 copy-start
  23.5 2.5 %shard_map.130 = (f32[128,16,128]{2,1,0:T(8,128)S(1)}, s32[4,8,128]{2,1,0:T(8,128)S(1)}, f32[8,8,128]{2,1,0:T(8,128)S(1)}, f32[8,8,128]{2,1,0:T(8,128)S(1)}, f32...) custom-call(s32[64,128]{1,0:T(8,128)} %bitcast.43, ...), custom_call_target="tpu_custom_call" | custom-call | flops 1073741824 | bytes 4194304 | tf_op jit(solution)/shard_map/pallas_call | solution.py:428
  26.0 0.0 collective-permute-done.recv_ref
  26.0 0.0 copy-done
  26.0 6.9 %shard_map.131 = (f32[128,16,128]{2,1,0:T(8,128)S(1)}, f32[128,16,128]{2,1,0:T(8,128)S(1)}, f32[128,16,128]{2,1,0:T(8,128)S(1)}, f32[32,8,128]{2,1,0:T(8,128)}) custom-call(s32[64,128]{1,0:T(8,128)} %bitcast.44, f32[64,8,128]{2,1,0:T(8,128)S(1)} %collective-permute-done.recv_ref, f32[64,8,128]{2,1,0:T(8,128)S(1)} %all_to_all.10.recv_ref.own_recv_ref, ...), custom_call_target="tpu_custom_call" | custom-call | tf_op jit(solution)/shard_map/pallas_call | solution.py:435
  32.9 4.7 %all-to-all-start.1 = ((f32[128,2,128]{2,1,0:T(2,128)}), f32[128,2,128]{2,1,0:T(2,128)S(1)}, u32[]{:S(2)}, u32[]{:S(2)}) async-start(f32[128,2,128]{2,1,0:T(2,128)} %bitcast.22), calls=%async_computation.1 | async-start | bytes 262144 | tf_op jit(solution)/shard_map/all_to_all | solution.py:371
  37.6 1.0 %copy.20 = f32[2,64,4,512]{3,2,1,0:T(4,128)} copy(f32[2,64,4,512]{3,2,1,0:T(4,128)S(1)} %bitcast.39) | data formatting | bytes 2097152
  38.6 1.0 %copy.21 = f32[2,64,4,512]{3,2,1,0:T(4,128)} copy(f32[2,64,4,512]{3,2,1,0:T(4,128)S(1)} %bitcast.38) | data formatting | bytes 2097152
  39.6 0.0 copy-start.1
  39.6 0.0 copy-start.2
  39.6 1.0 %copy.22 = f32[2,64,4,512]{3,2,1,0:T(4,128)} copy(f32[2,64,4,512]{3,2,1,0:T(4,128)S(1)} %bitcast.37) | data formatting | bytes 2097152
  40.5 6.7 %all-to-all-done.1 = f32[128,2,128]{2,1,0:T(2,128)S(1)} async-done(((f32[128,2,128]{2,1,0:T(2,128)}), f32[128,2,128]{2,1,0:T(2,128)S(1)}, u32[]{:S(2)}, u32[]{:S(2)}) %all-to-all-start.1) | async-done | bytes 131104 | tf_op jit(solution)/shard_map/all_to_all | solution.py:371
  47.2 0.0 copy-done.1
  47.2 0.0 copy-done.2
  47.2 1.1 %shard_map.132 = f32[16,512]{1,0:T(8,128)} custom-call(f32[32,8,128]{2,1,0:T(8,128)S(1)} %bitcast.41, f32[8,64]{1,0:T(8,128)S(1)} %bitcast.42, f32[16,64]{1,0:T(8,128)S(1)} %copy-done.1), custom_call_target="tpu_custom_call" | custom-call | tf_op jit(solution)/shard_map/pallas_call | solution.py:446
Async XLA Ops:
  23.5 2.5 %collective-permute-start = (f32[64,8,128]{2,1,0:T(8,128)S(1)}, f32[64,8,128]{2,1,0:T(8,128)S(1)}, u32[]{:S(2)}, u32[]{:S(2)}) collective-permute-start(f32[64,8,128]{2,1,0:T(8,128)S(1)} %all_to_all.10.recv_ref.own_recv_ref), channel_id=1, source_target_pairs={{0,16},{16,0},{32,48},{48,32},{64,80},{80,64},{96,112},{112,96},{1... | collective-permute-start | bytes 786440 | tf_op jit(solution)/shard_map/ppermute | solution.py:382
  23.5 2.5 %copy-start = (f32[2,64,4,512]{3,2,1,0:T(4,128)S(1)}, f32[2,64,4,512]{3,2,1,0:T(4,128)}, u32[]{:S(2)}) copy-start(f32[2,64,4,512]{3,2,1,0:T(4,128)} %param.10) | copy-start | bytes 3145732
  32.9 14.3 %all-to-all-start.1 = ((f32[128,2,128]{2,1,0:T(2,128)}), f32[128,2,128]{2,1,0:T(2,128)S(1)}, u32[]{:S(2)}, u32[]{:S(2)}) async-start(f32[128,2,128]{2,1,0:T(2,128)} %bitcast.22), calls=%async_computation.1 | async-start | bytes 262144 | tf_op jit(solution)/shard_map/all_to_all | solution.py:371
  39.6 7.6 %copy-start.1 = (f32[16,64]{1,0:T(8,128)S(1)}, f32[16,64]{1,0:T(8,128)}, u32[]{:S(2)}) copy-start(f32[16,64]{1,0:T(8,128)} %wout_ref.1) | copy-start | bytes 12292
  39.6 7.6 %copy-start.2 = (f32[64,8]{0,1:T(8,128)S(1)}, f32[64,8]{0,1:T(8,128)}, u32[]{:S(2)}) copy-start(f32[64,8]{0,1:T(8,128)} %param.18) | copy-start | bytes 6148

commit v9 on v8

--- a/solution.py
+++ b/solution.py
@@ -13,6 +13,7 @@
 LANES = 128
 RUN = 32
 VMEM_LIMIT = 16 << 20
+DEEP = 4
 f32, bf16, i32 = jnp.float32, jnp.bfloat16, jnp.int32
 
 
@@ -44,6 +45,11 @@
     return result
 
 
+def each(count, step):
+    for number in range(count):
+        step(number, 0)
+
+
 def start_all(sources, targets, sems):
     copies = [pltpu.make_async_copy(x, y, sems.at[n]) for n, (x, y) in enumerate(zip(sources, targets))]
     for copy in copies:
@@ -99,7 +105,10 @@
                 self.aux_ref[4 + t, v] = rows[3]
             return carry
 
-        lax.fori_loop(0, 4, unpack, 0, unroll=unroll)
+        if unroll:
+            each(4, unpack)
+        else:
+            lax.fori_loop(0, 4, unpack, 0)
         first_slot = (lax.axis_index("table") * 64).astype(f32)
         self.hits = []
         for v in range(4):
@@ -120,7 +129,10 @@
             rank = self.before[v] + self.through[v] - 1 - step * LANES
             inside = (self.hits[v] > 0.5) & (rank >= 0) & (rank < LANES)
             self.slots_ref[v] = jnp.where(inside, rank, -1)
-        lax.fori_loop(0, 8, self.compact, 0, unroll=unroll)
+        if unroll:
+            each(8, self.compact)
+        else:
+            lax.fori_loop(0, 8, self.compact, 0)
 
     def compact(self, lt, carry):
         high, low, chosen = [], [], []
@@ -149,9 +161,9 @@
         self.cot_ref[lt] = jnp.where(self.sub < 4, pltpu.roll(aux, 4, 0), aux)
         return carry
 
-    def hot_rows(self, lt):
+    def hot_rows(self, lt, corners=range(8)):
         pieces = []
-        for c in range(8):
+        for c in corners:
             wanted = jnp.broadcast_to(self.column_ref[lt, c : c + 1, :], (16, LANES)).astype(bf16)
             pieces.append(
                 jnp.concatenate([jnp.where(wanted == self.entries[i], self.one, self.none) for i in range(8)], axis=0)
@@ -190,10 +202,12 @@
             rows = jnp.concatenate([table_ref[blocks(lt, slot)] for slot in range(4)], axis=0)
             high = rows.astype(bf16)
             low = (rows - high.astype(f32)).astype(bf16)
-            hot = self.hot_rows(lt)
+            deep, tall = self.hot_rows(lt, range(DEEP)), self.hot_rows(lt, range(DEEP, 8))
             seen = jnp.dot(
-                jnp.concatenate([high, low], axis=1), jnp.concatenate([hot, hot], axis=0), preferred_element_type=f32
+                jnp.concatenate([high, low], axis=1), jnp.concatenate([deep, deep], axis=0), preferred_element_type=f32
             )
+            both = jnp.dot(jnp.concatenate([high, low], axis=0), tall, preferred_element_type=f32)
+            seen = jnp.concatenate([seen, both[:64] + both[64:]], axis=1)
             total = jnp.zeros((8, LANES), f32)
             for c in range(8):
                 own = jnp.broadcast_to(self.key_ref[lt, c : c + 1, :], (8, LANES))
@@ -238,22 +252,22 @@
 
 
 def gradients(half, grad_ref, blocks, ready):
-    half.count(4)
-    half.gather(0, 4)
+    half.count(True)
+    half.gather(0, True)
     ready()
     step = half.accumulate(grad_ref, blocks)
-    lax.fori_loop(0, 8, step, 0, unroll=4)
+    each(8, step)
     passes = passes_of(half.total)
 
     def again(number, carry):
-        half.gather(number, 1)
+        half.gather(number, False)
         return lax.fori_loop(0, 8, step, carry)
 
     lax.fori_loop(1, passes, again, 0)
 
     @pl.when(passes > 1)
     def _():
-        half.gather(0, 1)
+        half.gather(0, False)
 
     return passes
 
@@ -300,14 +314,14 @@
     own = Half(own_recv_ref, corner_ref, aux_ref, own_slots_ref, own_hat_ref, own_key_ref, own_column_ref, cot_ref)
     results = [result_ref.at[pl.ds(0, 16)], result_ref.at[pl.ds(16, 16)]]
     for part, finder, result in ((own, own_blocks, results[0]), (half, blocks, results[1])):
-        lax.fori_loop(0, 8, part.look(tnew_ref, found_ref, finder), 0, unroll=4)
-        lax.fori_loop(0, 4, part.spread(found_ref, result), 0, unroll=2)
+        each(8, part.look(tnew_ref, found_ref, finder))
+        each(4, part.spread(found_ref, result))
 
     def more_passes(part, finder, result, count):
         look, spread = part.look(tnew_ref, found_ref, finder), part.spread(found_ref, result)
 
         def again(number, carry):
-            part.gather(number, 1)
+            part.gather(number, False)
             lax.fori_loop(0, 8, look, 0)
             return lax.fori_loop(0, 4, spread, carry)
 
@@ -319,7 +333,7 @@
     @pl.when(own_passes > 1)
     def _():
         again = Half(own_recv_ref, *spare)
-        again.count(1)
+        again.count(False)
         more_passes(again, own_blocks, results[0], own_passes)
 
     core = lax.axis_index("table") % 2

time: 49.3 us -> 47.6 us (0.966)
  the two profiles are of different devices: /device:TPU:0 before, /device:TPU:1 now
where the time goes in v9:
time: 47.6 us; the launch traced here: 47.3 us
  blocking collectives  21.2 us (45%)
  Pallas kernels  9.85 us (21%)
  waiting for transfers between devices  6.94 us (15%)
  starting transfers between devices  5.72 us (12%)
  local copies, waits for them, and re-layouts  2.92 us (6%)
  between operations  0.69 us (1%)
    all_to_all x1, blocking collectives, exchange(): lax.all_to_all(value, ('table', 'ray'), split_axis=0, concat_axis=0, tile...  21.2 us
    all_to_all x1, waiting for transfers between devices, exchange(): lax.all_to_all(value, ('table', 'ray'), split_axis=0, concat_axis=0, tile...  6.94 us
    pallas_call x1, Pallas kernels, on_device(): call(second_kernel, [full, full, full, ((32, 8, LANES), f32)], [HBM] + [V...  5.47 us
    all_to_all x1, starting transfers between devices, exchange(): lax.all_to_all(value, ('table', 'ray'), split_axis=0, concat_axis=0, tile...  3.61 us
    unnamed x9, local copies, waits for them, and re-layouts  2.92 us
    pallas_call x1, Pallas kernels, on_device(): call(first_kernel, [full, lists, tile, tile, tile, pltpu.VMEM((8, LANES),...  2.27 us
    ppermute x1, starting transfers between devices, swap_cores(): lax.ppermute(value, 'table', [(t, t ^ 1) for t in range(lax.axis_size('ta...  2.11 us
    pallas_call x1, Pallas kernels, on_device(): call(network_kernel, [((16, 512), f32)], [VMEM] * 3)  1.14 us
  transfers between devices with their start and end apart: 2, of which 1 were waited for; matrix products, arithmetic and copies ran while one was open for 6% of the time, Pallas kernels for 5%

profile of v9, /device:TPU:1, one launch (start us, length us, event | category | flops | bytes accessed | tf_op | source)
XLA Modules:
  0.0 47.3 jit_solution(2053649533628681533)
XLA Ops:
  0.6 1.0 %shard_map.129 = f32[64,8,128]{2,1,0:T(8,128)S(1)} custom-call(s32[2,512]{1,0:T(2,128)} %slot_hbm.1, s32[2,8,512]{2,1,0:T(8,128)} %corners_hbm.1, f32[3,2,512]{2,1,0:T(2,128)} %bitcast.45, f32[2,4,512]{2,1,0:T(4,128)} %cot_hbm.1), custom_call_target="tpu_custom_call" | custom-call | tf_op jit(solution)/shard_map/pallas_call | solution.py:421
  1.6 21.2 %all_to_all.10.recv_ref.own_recv_ref = f32[64,8,128]{2,1,0:T(8,128)S(1)} all-to-all(f32[64,8,128]{2,1,0:T(8,128)S(1)} %shard_map.129), channel_id=1, replica_groups={{0,1,2,3,4,5,6,7,8,9,10,11,12,13,14,15,32,33,34,35,36,37,38,39,40,41,42..., dimensions={0} | all-to-all | bytes 524288 | tf_op jit(solution)/shard_map/all_to_all | solution.py:385
  22.8 2.1 %collective-permute-start = (f32[64,8,128]{2,1,0:T(8,128)S(1)}, f32[64,8,128]{2,1,0:T(8,128)S(1)}, u32[]{:S(2)}, u32[]{:S(2)}) collective-permute-start(f32[64,8,128]{2,1,0:T(8,128)S(1)} %all_to_all.10.recv_ref.own_recv_ref), channel_id=1, source_target_pairs={{0,16},{16,0},{32,48},{48,32},{64,80},{80,64},{96,112},{112,96},{1... | collective-permute-start | bytes 786440 | tf_op jit(solution)/shard_map/ppermute | solution.py:396
  24.9 0.0 copy-start
  24.9 2.3 %shard_map.130 = (f32[128,16,128]{2,1,0:T(8,128)S(1)}, s32[4,8,128]{2,1,0:T(8,128)S(1)}, f32[8,8,128]{2,1,0:T(8,128)S(1)}, f32[8,8,128]{2,1,0:T(8,128)S(1)}, f32...) custom-call(s32[64,128]{1,0:T(8,128)} %bitcast.43, ...), custom_call_target="tpu_custom_call" | custom-call | flops 1073741824 | bytes 4194304 | tf_op jit(solution)/shard_map/pallas_call | solution.py:442
  27.2 0.0 collective-permute-done.recv_ref
  27.2 0.0 copy-done
  27.2 5.5 %shard_map.131 = (f32[128,16,128]{2,1,0:T(8,128)S(1)}, f32[128,16,128]{2,1,0:T(8,128)S(1)}, f32[128,16,128]{2,1,0:T(8,128)S(1)}, f32[32,8,128]{2,1,0:T(8,128)}) custom-call(s32[64,128]{1,0:T(8,128)} %bitcast.44, f32[64,8,128]{2,1,0:T(8,128)S(1)} %collective-permute-done.recv_ref, f32[64,8,128]{2,1,0:T(8,128)S(1)} %all_to_all.10.recv_ref.own_recv_ref, ...), custom_call_target="tpu_custom_call" | custom-call | tf_op jit(solution)/shard_map/pallas_call | solution.py:449
  32.7 3.6 %all-to-all-start.1 = ((f32[128,2,128]{2,1,0:T(2,128)}), f32[128,2,128]{2,1,0:T(2,128)S(1)}, u32[]{:S(2)}, u32[]{:S(2)}) async-start(f32[128,2,128]{2,1,0:T(2,128)} %bitcast.22), calls=%async_computation.1 | async-start | bytes 262144 | tf_op jit(solution)/shard_map/all_to_all | solution.py:385
  36.3 1.0 %copy.20 = f32[2,64,4,512]{3,2,1,0:T(4,128)} copy(f32[2,64,4,512]{3,2,1,0:T(4,128)S(1)} %bitcast.39) | data formatting | bytes 2097152
  37.3 1.0 %copy.21 = f32[2,64,4,512]{3,2,1,0:T(4,128)} copy(f32[2,64,4,512]{3,2,1,0:T(4,128)S(1)} %bitcast.38) | data formatting | bytes 2097152
  38.2 0.0 copy-start.1
  38.2 0.0 copy-start.2
  38.2 1.0 %copy.22 = f32[2,64,4,512]{3,2,1,0:T(4,128)} copy(f32[2,64,4,512]{3,2,1,0:T(4,128)S(1)} %bitcast.37) | data formatting | bytes 2097152
  39.2 6.9 %all-to-all-done.1 = f32[128,2,128]{2,1,0:T(2,128)S(1)} async-done(((f32[128,2,128]{2,1,0:T(2,128)}), f32[128,2,128]{2,1,0:T(2,128)S(1)}, u32[]{:S(2)}, u32[]{:S(2)}) %all-to-all-start.1) | async-done | bytes 131104 | tf_op jit(solution)/shard_map/all_to_all | solution.py:385
  46.1 0.0 copy-done.1
  46.1 0.0 copy-done.2
  46.1 1.1 %shard_map.132 = f32[16,512]{1,0:T(8,128)} custom-call(f32[32,8,128]{2,1,0:T(8,128)S(1)} %bitcast.41, f32[8,64]{1,0:T(8,128)S(1)} %bitcast.42, f32[16,64]{1,0:T(8,128)S(1)} %copy-done.1), custom_call_target="tpu_custom_call" | custom-call | tf_op jit(solution)/shard_map/pallas_call | solution.py:460
Async XLA Ops:
  22.8 4.4 %collective-permute-start = (f32[64,8,128]{2,1,0:T(8,128)S(1)}, f32[64,8,128]{2,1,0:T(8,128)S(1)}, u32[]{:S(2)}, u32[]{:S(2)}) collective-permute-start(f32[64,8,128]{2,1,0:T(8,128)S(1)} %all_to_all.10.recv_ref.own_recv_ref), channel_id=1, source_target_pairs={{0,16},{16,0},{32,48},{48,32},{64,80},{80,64},{96,112},{112,96},{1... | collective-permute-start | bytes 786440 | tf_op jit(solution)/shard_map/ppermute | solution.py:396
  24.9 2.3 %copy-start = (f32[2,64,4,512]{3,2,1,0:T(4,128)S(1)}, f32[2,64,4,512]{3,2,1,0:T(4,128)}, u32[]{:S(2)}) copy-start(f32[2,64,4,512]{3,2,1,0:T(4,128)} %param.10) | copy-start | bytes 3145732
  32.7 13.5 %all-to-all-start.1 = ((f32[128,2,128]{2,1,0:T(2,128)}), f32[128,2,128]{2,1,0:T(2,128)S(1)}, u32[]{:S(2)}, u32[]{:S(2)}) async-start(f32[128,2,128]{2,1,0:T(2,128)} %bitcast.22), calls=%async_computation.1 | async-start | bytes 262144 | tf_op jit(solution)/shard_map/all_to_all | solution.py:385
  38.2 7.9 %copy-start.1 = (f32[16,64]{1,0:T(8,128)S(1)}, f32[16,64]{1,0:T(8,128)}, u32[]{:S(2)}) copy-start(f32[16,64]{1,0:T(8,128)} %wout_ref.1) | copy-start | bytes 12292
  38.2 7.9 %copy-start.2 = (f32[64,8]{0,1:T(8,128)S(1)}, f32[64,8]{0,1:T(8,128)}, u32[]{:S(2)}) copy-start(f32[64,8]{0,1:T(8,128)} %param.18) | copy-start | bytes 6148

commit v10 on v9

--- a/solution.py
+++ b/solution.py
@@ -43,6 +43,11 @@
         moved = pltpu.roll(pltpu.roll(value, 2 * d, 0), LANES - RUN * d, 1)
         result = jnp.where(shift == d, moved, result)
     return result
+
+
+def split_two(value):
+    high = value.astype(bf16).astype(f32)
+    return high, value - high
 
 
 def each(count, step):
@@ -273,11 +278,11 @@
 
 
 def first_kernel(
-    ids_hbm, recv_ref, m1_hbm, m2_hbm,
-    grad_ref, slots_ref, hat_ref, key_ref, column_ref, total_ref, m1_ref, m2_ref,
+    ids_hbm, recv_ref, m1_hbm,
+    grad_ref, slots_ref, hat_ref, key_ref, column_ref, total_ref, m1_ref,
     ids_ref, corner_ref, aux_ref, cot_ref, sems,
 ):
-    loads = start_all((ids_hbm, m1_hbm, m2_hbm), (ids_ref, m1_ref, m2_ref), sems)
+    loads = start_all((ids_hbm, m1_hbm), (ids_ref, m1_ref), sems)
     grad_ref[...] = jnp.zeros_like(grad_ref)
     half = Half(recv_ref, corner_ref, aux_ref, slots_ref, hat_ref, key_ref, column_ref, cot_ref)
     gradients(half, grad_ref, block_finder(ids_ref, 0), loads[0].wait)
@@ -286,25 +291,26 @@
 
 
 def second_kernel(
-    ids_hbm, recv_ref, own_recv_ref, before_ref, table_ref, m1_ref, m2_ref,
+    ids_hbm, m2_hbm, recv_ref, own_recv_ref, before_ref, table_ref, m1_ref,
     own_slots_ref, own_hat_ref, own_key_ref, own_column_ref, own_total_ref,
     tnew_ref, m1new_ref, m2new_ref, out_ref,
     ids_ref, grad_ref, corner_ref, aux_ref, slots_ref, hat_ref, key_ref, column_ref, cot_ref,
-    found_ref, result_ref, sem,
+    found_ref, result_ref, sems,
 ):
-    (load,) = start_all((ids_hbm,), (ids_ref,), sem)
+    loads = start_all((ids_hbm, m2_hbm), (ids_ref, m2new_ref), sems)
     grad_ref[...] = before_ref[...]
     result_ref[...] = jnp.zeros_like(result_ref)
     spare = (corner_ref, aux_ref, slots_ref, hat_ref, key_ref, column_ref, cot_ref)
     half = Half(recv_ref, *spare)
     blocks, own_blocks = block_finder(ids_ref, 1), block_finder(ids_ref, 0)
-    passes = gradients(half, grad_ref, blocks, load.wait)
+    passes = gradients(half, grad_ref, blocks, loads[0].wait)
+    loads[1].wait()
 
     def update(step, carry):
         at = pl.ds(step * 4, 4)
         grad = grad_ref[at]
         first = beta_one * m1_ref[at] + (1.0 - beta_one) * grad
-        second = beta_two * m2_ref[at] + (1.0 - beta_two) * grad * grad
+        second = beta_two * m2new_ref[at] + (1.0 - beta_two) * grad * grad
         m1new_ref[at] = first
         m2new_ref[at] = second
         tnew_ref[at] = table_ref[at] - learn_rate * first / (jnp.sqrt(second) + adam_eps)
@@ -351,14 +357,20 @@
             total = total + recv_ref[4 * t + v]
         columns.append(tile_blocks(total))
     encoded = jnp.concatenate(columns, axis=1)
-    hidden = jnp.maximum(
-        lax.dot_general(
-            win_ref[...], encoded, (((0,), (0,)), ((), ())),
-            precision=lax.Precision.HIGHEST, preferred_element_type=f32,
-        ),
-        0.0,
-    )
-    out_ref[...] = jnp.dot(wout_ref[...], hidden, precision=lax.Precision.HIGHEST, preferred_element_type=f32)
+    w_high, w_low = split_two(win_ref[...])
+    e_high, e_low = split_two(encoded)
+    hidden = lax.dot_general(
+        jnp.concatenate([w_high, w_low, w_high], axis=0).astype(bf16),
+        jnp.concatenate([e_high, e_high, e_low], axis=0).astype(bf16),
+        (((0,), (0,)), ((), ())), preferred_element_type=f32,
+    )
+    h_high, h_low = split_two(jnp.maximum(hidden, 0.0))
+    w_high, w_low = split_two(wout_ref[...])
+    both = jnp.dot(
+        jnp.concatenate([w_high, w_low], axis=0).astype(bf16), h_high.astype(bf16), preferred_element_type=f32
+    )
+    rest = jnp.dot(w_high.astype(bf16), h_low.astype(bf16), preferred_element_type=f32)
+    out_ref[...] = both[:16] + both[16:] + rest
 
 
 VMEM = pl.BlockSpec(memory_space=pltpu.VMEM)
@@ -439,23 +451,23 @@
     full = pltpu.VMEM(rows, f32)
     data = pltpu.VMEM((8, 4, 8, LANES), f32)
     id_table = pltpu.SMEM((64, LANES), i32)
-    grad, slots, hat, key, column, total, m1, m2 = call(
+    grad, slots, hat, key, column, total, m1 = call(
         first_kernel,
-        [full, lists, tile, tile, tile, pltpu.VMEM((8, LANES), i32), full, full],
-        [HBM, VMEM, HBM, HBM],
-        [id_table, data, data, tile, pltpu.SemaphoreType.DMA((3,))],
+        [full, lists, tile, tile, tile, pltpu.VMEM((8, LANES), i32), full],
+        [HBM, VMEM, HBM],
+        [id_table, data, data, tile, pltpu.SemaphoreType.DMA((2,))],
         cost_estimate=pl.CostEstimate(flops=1 << 30, bytes_accessed=4 << 20, transcendentals=0),
-    )(ids, samples, *in_hbm(rows_of(moment1), rows_of(moment2)))
+    )(ids, samples, *in_hbm(rows_of(moment1)))
     tnew, m1new, m2new, found = call(
         second_kernel,
         [full, full, full, ((32, 8, LANES), f32)],
-        [HBM] + [VMEM] * 11,
+        [HBM, HBM] + [VMEM] * 10,
         [
             id_table, full, data, data, lists, tile, tile, tile, tile, tile,
             pltpu.VMEM((32, 8, LANES), f32),
-            pltpu.SemaphoreType.DMA((1,)),
+            pltpu.SemaphoreType.DMA((2,)),
         ],
-    )(ids, others, samples, grad, rows_of(table), m1, m2, slots, hat, key, column, total)
+    )(ids, *in_hbm(rows_of(moment2)), others, samples, grad, rows_of(table), m1, slots, hat, key, column, total)
     back = exchange(found.reshape(128, 2, LANES)).reshape(32, 8, LANES)
     (mlp_out,) = call(network_kernel, [((16, 512), f32)], [VMEM] * 3)(back, weight_in.T, weight_out)
     shape = table.shape

time: 47.6 us -> 46.9 us (0.985)
  the two profiles are of different devices: /device:TPU:1 before, /device:TPU:0 now
where the time goes in v10:
time: 46.9 us; the launch traced here: 46 us
  blocking collectives  21.9 us (47%)
  Pallas kernels  9.18 us (20%)
  waiting for transfers between devices  6.67 us (14%)
  starting transfers between devices  4.66 us (10%)
  local copies, waits for them, and re-layouts  2.92 us (6%)
  between operations  0.69 us (1%)
    all_to_all x1, blocking collectives, exchange(): lax.all_to_all(value, ('table', 'ray'), split_axis=0, concat_axis=0, tile...  21.9 us
    all_to_all x1, waiting for transfers between devices, exchange(): lax.all_to_all(value, ('table', 'ray'), split_axis=0, concat_axis=0, tile...  6.67 us
    pallas_call x1, Pallas kernels, on_device(): call(second_kernel, [full, full, full, ((32, 8, LANES), f32)], [HBM, HBM]...  5.13 us
    all_to_all x1, starting transfers between devices, exchange(): lax.all_to_all(value, ('table', 'ray'), split_axis=0, concat_axis=0, tile...  4.66 us
    unnamed x9, local copies, waits for them, and re-layouts  2.92 us
    pallas_call x1, Pallas kernels, on_device(): call(first_kernel, [full, lists, tile, tile, tile, pltpu.VMEM((8, LANES),...  2.09 us
    pallas_call x1, Pallas kernels, on_device(): call(network_kernel, [((16, 512), f32)], [VMEM] * 3)  0.99 us
    pallas_call x1, Pallas kernels, on_device(): call(pack_kernel, [((64, 8, LANES), f32)], [HBM] * 4, [pltpu.VMEM((2, 512...  0.97 us
  transfers between devices with their start and end apart: 2, of which 1 were waited for; matrix products, arithmetic and copies ran while one was open for 6% of the time, Pallas kernels for 5%

profile of v10, /device:TPU:0, one launch (start us, length us, event | category | flops | bytes accessed | tf_op | source)
XLA Modules:
  0.0 46.0 jit_solution(5758286374849114826)
XLA Ops:
  0.6 1.0 %shard_map.129 = f32[64,8,128]{2,1,0:T(8,128)S(1)} custom-call(s32[2,512]{1,0:T(2,128)} %slot_hbm.1, s32[2,8,512]{2,1,0:T(8,128)} %corners_hbm.1, f32[3,2,512]{2,1,0:T(2,128)} %bitcast.46, f32[2,4,512]{2,1,0:T(4,128)} %cot_hbm.1), custom_call_target="tpu_custom_call" | custom-call | tf_op jit(solution)/shard_map/pallas_call | solution.py:433
  1.6 21.9 %all_to_all.10.recv_ref.own_recv_ref = f32[64,8,128]{2,1,0:T(8,128)S(1)} all-to-all(f32[64,8,128]{2,1,0:T(8,128)S(1)} %shard_map.129), channel_id=1, replica_groups={{0,1,2,3,4,5,6,7,8,9,10,11,12,13,14,15,32,33,34,35,36,37,38,39,40,41,42..., dimensions={0} | all-to-all | bytes 524288 | tf_op jit(solution)/shard_map/all_to_all | solution.py:397
  23.5 0.0 collective-permute-start
  23.5 0.0 copy-start
  23.5 2.1 %shard_map.130 = (f32[128,16,128]{2,1,0:T(8,128)S(1)}, s32[4,8,128]{2,1,0:T(8,128)S(1)}, f32[8,8,128]{2,1,0:T(8,128)S(1)}, f32[8,8,128]{2,1,0:T(8,128)S(1)}, f32...) custom-call(s32[64,128]{1,0:T(8,128)} %bitcast.44, ...), custom_call_target="tpu_custom_call" | custom-call | flops 1073741824 | bytes 4194304 | tf_op jit(solution)/shard_map/pallas_call | solution.py:454
  25.6 0.0 collective-permute-done.recv_ref
  25.6 0.0 copy-done
  25.6 5.1 %shard_map.131 = (f32[128,16,128]{2,1,0:T(8,128)S(1)}, f32[128,16,128]{2,1,0:T(8,128)S(1)}, f32[128,16,128]{2,1,0:T(8,128)S(1)}, f32[32,8,128]{2,1,0:T(8,128)}) custom-call(s32[64,128]{1,0:T(8,128)} %bitcast.45, f32[128,16,128]{2,1,0:T(8,128)} %bitcast.43, f32[64,8,128]{2,1,0:T(8,128)S(1)} %collective-permute-done.recv_ref, ...), custom_call_target="tpu_custom_call" | custom-call | tf_op jit(solution)/shard_map/pallas_call | solution.py:461
  30.8 4.7 %all-to-all-start.1 = ((f32[128,2,128]{2,1,0:T(2,128)}), f32[128,2,128]{2,1,0:T(2,128)S(1)}, u32[]{:S(2)}, u32[]{:S(2)}) async-start(f32[128,2,128]{2,1,0:T(2,128)} %bitcast.22), calls=%async_computation.1 | async-start | bytes 262144 | tf_op jit(solution)/shard_map/all_to_all | solution.py:397
  35.4 1.0 %copy.20 = f32[2,64,4,512]{3,2,1,0:T(4,128)} copy(f32[2,64,4,512]{3,2,1,0:T(4,128)S(1)} %bitcast.39) | data formatting | bytes 2097152
  36.4 1.0 %copy.21 = f32[2,64,4,512]{3,2,1,0:T(4,128)} copy(f32[2,64,4,512]{3,2,1,0:T(4,128)S(1)} %bitcast.38) | data formatting | bytes 2097152
  37.4 0.0 copy-start.1
  37.4 0.0 copy-start.2
  37.4 1.0 %copy.22 = f32[2,64,4,512]{3,2,1,0:T(4,128)} copy(f32[2,64,4,512]{3,2,1,0:T(4,128)S(1)} %bitcast.37) | data formatting | bytes 2097152
  38.4 6.7 %all-to-all-done.1 = f32[128,2,128]{2,1,0:T(2,128)S(1)} async-done(((f32[128,2,128]{2,1,0:T(2,128)}), f32[128,2,128]{2,1,0:T(2,128)S(1)}, u32[]{:S(2)}, u32[]{:S(2)}) %all-to-all-start.1) | async-done | bytes 131104 | tf_op jit(solution)/shard_map/all_to_all | solution.py:397
  45.0 0.0 copy-done.1
  45.0 0.0 copy-done.2
  45.0 1.0 %shard_map.132 = f32[16,512]{1,0:T(8,128)} custom-call(f32[32,8,128]{2,1,0:T(8,128)S(1)} %bitcast.41, f32[8,64]{1,0:T(8,128)S(1)} %bitcast.42, f32[16,64]{1,0:T(8,128)S(1)} %copy-done.1), custom_call_target="tpu_custom_call" | custom-call | tf_op jit(solution)/shard_map/pallas_call | solution.py:472
Async XLA Ops:
  23.5 2.1 %collective-permute-start = (f32[64,8,128]{2,1,0:T(8,128)S(1)}, f32[64,8,128]{2,1,0:T(8,128)S(1)}, u32[]{:S(2)}, u32[]{:S(2)}) collective-permute-start(f32[64,8,128]{2,1,0:T(8,128)S(1)} %all_to_all.10.recv_ref.own_recv_ref), channel_id=1, source_target_pairs={{0,16},{16,0},{32,48},{48,32},{64,80},{80,64},{96,112},{112,96},{1... | collective-permute-start | bytes 786440 | tf_op jit(solution)/shard_map/ppermute | solution.py:408
  23.5 2.1 %copy-start = (f32[2,64,4,512]{3,2,1,0:T(4,128)S(1)}, f32[2,64,4,512]{3,2,1,0:T(4,128)}, u32[]{:S(2)}) copy-start(f32[2,64,4,512]{3,2,1,0:T(4,128)} %param.10) | copy-start | bytes 3145732
  30.8 14.3 %all-to-all-start.1 = ((f32[128,2,128]{2,1,0:T(2,128)}), f32[128,2,128]{2,1,0:T(2,128)S(1)}, u32[]{:S(2)}, u32[]{:S(2)}) async-start(f32[128,2,128]{2,1,0:T(2,128)} %bitcast.22), calls=%async_computation.1 | async-start | bytes 262144 | tf_op jit(solution)/shard_map/all_to_all | solution.py:397
  37.4 7.6 %copy-start.1 = (f32[16,64]{1,0:T(8,128)S(1)}, f32[16,64]{1,0:T(8,128)}, u32[]{:S(2)}) copy-start(f32[16,64]{1,0:T(8,128)} %wout_ref.1) | copy-start | bytes 12292
  37.4 7.6 %copy-start.2 = (f32[64,8]{0,1:T(8,128)S(1)}, f32[64,8]{0,1:T(8,128)}, u32[]{:S(2)}) copy-start(f32[64,8]{0,1:T(8,128)} %param.18) | copy-start | bytes 6148

commit v11 on v10

--- a/solution.py
+++ b/solution.py
@@ -200,11 +200,11 @@
 
         return one_group
 
-    def look(self, table_ref, found_ref, blocks):
+    def look(self, rows_at, found_ref, blocks):
         parity = self.sub // 4
 
         def one_group(lt, carry):
-            rows = jnp.concatenate([table_ref[blocks(lt, slot)] for slot in range(4)], axis=0)
+            rows = jnp.concatenate([rows_at(blocks(lt, slot)) for slot in range(4)], axis=0)
             high = rows.astype(bf16)
             low = (rows - high.astype(f32)).astype(bf16)
             deep, tall = self.hot_rows(lt, range(DEEP)), self.hot_rows(lt, range(DEEP, 8))
@@ -290,14 +290,24 @@
     wait_all(loads[1:])
 
 
+def moments(grad, m1, m2):
+    first = beta_one * m1 + (1.0 - beta_one) * grad
+    second = beta_two * m2 + (1.0 - beta_two) * grad * grad
+    return first, second
+
+
+def stepped(table, first, second):
+    return table - learn_rate * first / (jnp.sqrt(second) + adam_eps)
+
+
 def second_kernel(
     ids_hbm, m2_hbm, recv_ref, own_recv_ref, before_ref, table_ref, m1_ref,
     own_slots_ref, own_hat_ref, own_key_ref, own_column_ref, own_total_ref,
-    tnew_ref, m1new_ref, m2new_ref, out_ref,
-    ids_ref, grad_ref, corner_ref, aux_ref, slots_ref, hat_ref, key_ref, column_ref, cot_ref,
+    grad_ref, m2_ref, out_ref,
+    ids_ref, corner_ref, aux_ref, slots_ref, hat_ref, key_ref, column_ref, cot_ref,
     found_ref, result_ref, sems,
 ):
-    loads = start_all((ids_hbm, m2_hbm), (ids_ref, m2new_ref), sems)
+    loads = start_all((ids_hbm, m2_hbm), (ids_ref, m2_ref), sems)
     grad_ref[...] = before_ref[...]
     result_ref[...] = jnp.zeros_like(result_ref)
     spare = (corner_ref, aux_ref, slots_ref, hat_ref, key_ref, column_ref, cot_ref)
@@ -306,25 +316,18 @@
     passes = gradients(half, grad_ref, blocks, loads[0].wait)
     loads[1].wait()
 
-    def update(step, carry):
-        at = pl.ds(step * 4, 4)
-        grad = grad_ref[at]
-        first = beta_one * m1_ref[at] + (1.0 - beta_one) * grad
-        second = beta_two * m2new_ref[at] + (1.0 - beta_two) * grad * grad
-        m1new_ref[at] = first
-        m2new_ref[at] = second
-        tnew_ref[at] = table_ref[at] - learn_rate * first / (jnp.sqrt(second) + adam_eps)
-        return carry
-
-    lax.fori_loop(0, 32, update, 0)
+    def rows_at(block):
+        first, second = moments(grad_ref[block], m1_ref[block], m2_ref[block])
+        return stepped(table_ref[block], first, second)
+
     own = Half(own_recv_ref, corner_ref, aux_ref, own_slots_ref, own_hat_ref, own_key_ref, own_column_ref, cot_ref)
     results = [result_ref.at[pl.ds(0, 16)], result_ref.at[pl.ds(16, 16)]]
     for part, finder, result in ((own, own_blocks, results[0]), (half, blocks, results[1])):
-        each(8, part.look(tnew_ref, found_ref, finder))
+        each(8, part.look(rows_at, found_ref, finder))
         each(4, part.spread(found_ref, result))
 
     def more_passes(part, finder, result, count):
-        look, spread = part.look(tnew_ref, found_ref, finder), part.spread(found_ref, result)
+        look, spread = part.look(rows_at, found_ref, finder), part.spread(found_ref, result)
 
         def again(number, carry):
             part.gather(number, False)
@@ -347,6 +350,33 @@
         for v in range(4):
             out_ref[(2 * h + core) * 4 + v] = tile_blocks(result_ref[4 * h + v])
             out_ref[(2 * h + 1 - core) * 4 + v] = tile_blocks(result_ref[16 + 4 * h + v])
+
+
+def third_kernel(grad_ref, m2_ref, m1_hbm, table_hbm, tnew_hbm, m1new_hbm, m2new_hbm, table_ref, m1_ref, m2new_ref, loads, stores):
+    chunks = [pl.ds(32 * n, 32) for n in range(4)]
+    arriving = []
+    for n, chunk in enumerate(chunks):
+        sources = [ref.at[chunk] for ref in (m1_hbm, table_hbm)]
+        arriving.append(start_all(sources, [ref.at[chunk] for ref in (m1_ref, table_ref)], loads.at[n]))
+    leaving = []
+    for n, chunk in enumerate(chunks):
+        wait_all(arriving[n])
+
+        def update(step, carry):
+            at = pl.ds(32 * n + step * 4, 4)
+            first, second = moments(grad_ref[at], m1_ref[at], m2_ref[at])
+            m1_ref[at] = first
+            m2new_ref[at] = second
+            table_ref[at] = stepped(table_ref[at], first, second)
+            return carry
+
+        lax.fori_loop(0, 8, update, 0)
+        leaving += start_all(
+            [ref.at[chunk] for ref in (table_ref, m1_ref, m2new_ref)],
+            [ref.at[chunk] for ref in (tnew_hbm, m1new_hbm, m2new_hbm)],
+            stores.at[n],
+        )
+    wait_all(leaving)
 
 
 def network_kernel(recv_ref, win_ref, wout_ref, out_ref):
@@ -458,17 +488,25 @@
         [id_table, data, data, tile, pltpu.SemaphoreType.DMA((2,))],
         cost_estimate=pl.CostEstimate(flops=1 << 30, bytes_accessed=4 << 20, transcendentals=0),
     )(ids, samples, *in_hbm(rows_of(moment1)))
-    tnew, m1new, m2new, found = call(
+    grad, m2, found = call(
         second_kernel,
-        [full, full, full, ((32, 8, LANES), f32)],
+        [full, full, ((32, 8, LANES), f32)],
         [HBM, HBM] + [VMEM] * 10,
         [
-            id_table, full, data, data, lists, tile, tile, tile, tile, tile,
+            id_table, data, data, lists, tile, tile, tile, tile, tile,
             pltpu.VMEM((32, 8, LANES), f32),
             pltpu.SemaphoreType.DMA((2,)),
         ],
     )(ids, *in_hbm(rows_of(moment2)), others, samples, grad, rows_of(table), m1, slots, hat, key, column, total)
     back = exchange(found.reshape(128, 2, LANES)).reshape(32, 8, LANES)
+    tnew, m1new, m2new = call(
+        third_kernel,
+        [(rows, f32)] * 3,
+        [VMEM] * 2 + [HBM] * 2,
+        [full, full, full, pltpu.SemaphoreType.DMA((4, 2)), pltpu.SemaphoreType.DMA((4, 3))],
+        [HBM] * 3,
+        cost_estimate=pl.CostEstimate(flops=20 << 20, bytes_accessed=7 << 20, transcendentals=0),
+    )(grad, m2, *in_hbm(rows_of(moment1), rows_of(table)))
     (mlp_out,) = call(network_kernel, [((16, 512), f32)], [VMEM] * 3)(back, weight_in.T, weight_out)
     shape = table.shape
     return (rows_back(tnew, shape), rows_back(m1new, shape), rows_back(m2new, shape), mlp_out)

time: 46.9 us -> 46.3 us (0.987)
  local copies, waits for them, and re-layouts: 2.92 us -> 0.02 us
  Pallas kernels: 9.18 us -> 11.7 us
    unnamed x9 -> x6, local copies, waits for them, and re-layouts: 2.92 us -> 0.02 us
    pallas_call x1 -> x2, Pallas kernels: 5.13 us -> 7.66 us  [the longest x1 4.49 us: on_device(): call(second_kernel, [full, full, ((32, 8, LANES), f32)], [HBM, HBM] + [VM...]
  transfers between devices with their start and end apart: 2 -> 2, of which waited for: 1 -> 1; matrix products, arithmetic and copies ran while one was open for 6% -> 0% of each run, Pallas kernels for 5% -> 12%
where the time goes in v11:
time: 46.3 us; the launch traced here: 45.4 us
  blocking collectives  21.9 us (47%)
  Pallas kernels  11.7 us (25%)
  waiting for transfers between devices  6.39 us (14%)
  starting transfers between devices  4.66 us (10%)
  between operations  0.71 us (2%)
    all_to_all x1, blocking collectives, exchange(): lax.all_to_all(value, ('table', 'ray'), split_axis=0, concat_axis=0, tile...  21.9 us
    all_to_all x1, waiting for transfers between devices, exchange(): lax.all_to_all(value, ('table', 'ray'), split_axis=0, concat_axis=0, tile...  6.39 us
    all_to_all x1, starting transfers between devices, exchange(): lax.all_to_all(value, ('table', 'ray'), split_axis=0, concat_axis=0, tile...  4.66 us
    pallas_call x1, Pallas kernels, on_device(): call(second_kernel, [full, full, ((32, 8, LANES), f32)], [HBM, HBM] + [VM...  4.49 us
    pallas_call x1, Pallas kernels, on_device(): call(third_kernel, [(rows, f32)] * 3, [VMEM] * 2 + [HBM] * 2, [full, full...  3.16 us
    pallas_call x1, Pallas kernels, on_device(): call(first_kernel, [full, lists, tile, tile, tile, pltpu.VMEM((8, LANES),...  2.09 us
    pallas_call x1, Pallas kernels, on_device(): call(network_kernel, [((16, 512), f32)], [VMEM] * 3)  0.99 us
    pallas_call x1, Pallas kernels, on_device(): call(pack_kernel, [((64, 8, LANES), f32)], [HBM] * 4, [pltpu.VMEM((2, 512...  0.97 us
  transfers between devices with their start and end apart: 2, of which 1 were waited for; matrix products, arithmetic and copies ran while one was open for 0% of the time, Pallas kernels for 12%

profile of v11, /device:TPU:0, one launch (start us, length us, event | category | flops | bytes accessed | tf_op | source)
XLA Modules:
  0.0 45.4 jit_solution(11922801442280404751)
XLA Ops:
  0.6 1.0 %shard_map.129 = f32[64,8,128]{2,1,0:T(8,128)S(1)} custom-call(s32[2,512]{1,0:T(2,128)} %slot_hbm.1, s32[2,8,512]{2,1,0:T(8,128)} %corners_hbm.1, f32[3,2,512]{2,1,0:T(2,128)} %bitcast.46, f32[2,4,512]{2,1,0:T(4,128)} %cot_hbm.1), custom_call_target="tpu_custom_call" | custom-call | tf_op jit(solution)/shard_map/pallas_call | solution.py:463
  1.6 21.9 %all_to_all.10.recv_ref.own_recv_ref = f32[64,8,128]{2,1,0:T(8,128)S(1)} all-to-all(f32[64,8,128]{2,1,0:T(8,128)S(1)} %shard_map.129), channel_id=1, replica_groups={{0,1,2,3,4,5,6,7,8,9,10,11,12,13,14,15,32,33,34,35,36,37,38,39,40,41,42..., dimensions={0} | all-to-all | bytes 524288 | tf_op jit(solution)/shard_map/all_to_all | solution.py:427
  23.5 0.0 collective-permute-start
  23.5 0.0 copy-start
  23.5 2.1 %shard_map.130 = (f32[128,16,128]{2,1,0:T(8,128)S(1)}, s32[4,8,128]{2,1,0:T(8,128)S(1)}, f32[8,8,128]{2,1,0:T(8,128)S(1)}, f32[8,8,128]{2,1,0:T(8,128)S(1)}, f32...) custom-call(s32[64,128]{1,0:T(8,128)} %bitcast.44, ...), custom_call_target="tpu_custom_call" | custom-call | flops 1073741824 | bytes 4194304 | tf_op jit(solution)/shard_map/pallas_call | solution.py:484
  25.6 0.0 collective-permute-done.recv_ref
  25.6 0.0 copy-done
  25.6 4.5 %shard_map.131 = (f32[128,16,128]{2,1,0:T(8,128)S(1)}, f32[128,16,128]{2,1,0:T(8,128)S(1)}, f32[32,8,128]{2,1,0:T(8,128)}) custom-call(s32[64,128]{1,0:T(8,128)} %bitcast.45, f32[128,16,128]{2,1,0:T(8,128)} %bitcast.41, f32[64,8,128]{2,1,0:T(8,128)S(1)} %collective-permute-done.recv_ref, f32[64,8,128]{2,1,0:T(8,128)S(1)} %all_to_all.10.recv_ref.own_recv_ref, ...), custom_call_target="tpu_custom_call" | custom-call | tf_op jit(solution)/shard_map/pallas_call | solution.py:491
  30.1 4.7 %all-to-all-start.1 = ((f32[128,2,128]{2,1,0:T(2,128)}), f32[128,2,128]{2,1,0:T(2,128)S(1)}, u32[]{:S(2)}, u32[]{:S(2)}) async-start(f32[128,2,128]{2,1,0:T(2,128)} %bitcast.22), calls=%async_computation.1 | async-start | bytes 262144 | tf_op jit(solution)/shard_map/all_to_all | solution.py:427
  34.8 0.0 copy-start.1
  34.8 0.0 copy-start.2
  34.8 3.2 %shard_map.132 = (f32[128,16,128]{2,1,0:T(8,128)}, f32[128,16,128]{2,1,0:T(8,128)}, f32[128,16,128]{2,1,0:T(8,128)}) custom-call(f32[128,16,128]{2,1,0:T(8,128)S(1)} %get-tuple-element.24.grad_ref, f32[128,16,128]{2,1,0:T(8,128)S(1)} %get-tuple-element.25.m2_ref, f32[128,16,128]{2,1,0:T(8,128)} %bitcast.43, f32[128,16,128]{2,1,0:T(8,128)} %bitcast.37), custom_call_target="tpu_custom_call" | custom-call | flops 20971520 | bytes 7340032 | tf_op jit(solution)/shard_map/pallas_call | solution.py:502
  38.0 6.4 %all-to-all-done.1 = f32[128,2,128]{2,1,0:T(2,128)S(1)} async-done(((f32[128,2,128]{2,1,0:T(2,128)}), f32[128,2,128]{2,1,0:T(2,128)S(1)}, u32[]{:S(2)}, u32[]{:S(2)}) %all-to-all-start.1) | async-done | bytes 131104 | tf_op jit(solution)/shard_map/all_to_all | solution.py:427
  44.4 0.0 copy-done.1
  44.4 0.0 copy-done.2
  44.4 1.0 %shard_map.133 = f32[16,512]{1,0:T(8,128)} custom-call(f32[32,8,128]{2,1,0:T(8,128)S(1)} %bitcast.39, f32[8,64]{1,0:T(8,128)S(1)} %bitcast.40, f32[16,64]{1,0:T(8,128)S(1)} %copy-done.1), custom_call_target="tpu_custom_call" | custom-call | tf_op jit(solution)/shard_map/pallas_call | solution.py:510
Async XLA Ops:
  23.5 2.1 %collective-permute-start = (f32[64,8,128]{2,1,0:T(8,128)S(1)}, f32[64,8,128]{2,1,0:T(8,128)S(1)}, u32[]{:S(2)}, u32[]{:S(2)}) collective-permute-start(f32[64,8,128]{2,1,0:T(8,128)S(1)} %all_to_all.10.recv_ref.own_recv_ref), channel_id=1, source_target_pairs={{0,16},{16,0},{32,48},{48,32},{64,80},{80,64},{96,112},{112,96},{1... | collective-permute-start | bytes 786440 | tf_op jit(solution)/shard_map/ppermute | solution.py:438
  23.5 2.1 %copy-start = (f32[2,64,4,512]{3,2,1,0:T(4,128)S(1)}, f32[2,64,4,512]{3,2,1,0:T(4,128)}, u32[]{:S(2)}) copy-start(f32[2,64,4,512]{3,2,1,0:T(4,128)} %param.10) | copy-start | bytes 3145732
  30.1 14.2 %all-to-all-start.1 = ((f32[128,2,128]{2,1,0:T(2,128)}), f32[128,2,128]{2,1,0:T(2,128)S(1)}, u32[]{:S(2)}, u32[]{:S(2)}) async-start(f32[128,2,128]{2,1,0:T(2,128)} %bitcast.22), calls=%async_computation.1 | async-start | bytes 262144 | tf_op jit(solution)/shard_map/all_to_all | solution.py:427
  34.8 9.6 %copy-start.1 = (f32[16,64]{1,0:T(8,128)S(1)}, f32[16,64]{1,0:T(8,128)}, u32[]{:S(2)}) copy-start(f32[16,64]{1,0:T(8,128)} %wout_ref.1) | copy-start | bytes 12292
  34.8 9.6 %copy-start.2 = (f32[64,8]{0,1:T(8,128)S(1)}, f32[64,8]{0,1:T(8,128)}, u32[]{:S(2)}) copy-start(f32[64,8]{0,1:T(8,128)} %param.18) | copy-start | bytes 6148

commit v12 on v11

--- a/solution.py
+++ b/solution.py
@@ -282,7 +282,7 @@
     grad_ref, slots_ref, hat_ref, key_ref, column_ref, total_ref, m1_ref,
     ids_ref, corner_ref, aux_ref, cot_ref, sems,
 ):
-    loads = start_all((ids_hbm, m1_hbm), (ids_ref, m1_ref), sems)
+    loads = start_all((ids_hbm, m1_hbm.at[pl.ds(0, 64)]), (ids_ref, m1_ref), sems)
     grad_ref[...] = jnp.zeros_like(grad_ref)
     half = Half(recv_ref, corner_ref, aux_ref, slots_ref, hat_ref, key_ref, column_ref, cot_ref)
     gradients(half, grad_ref, block_finder(ids_ref, 0), loads[0].wait)
@@ -301,20 +301,22 @@
 
 
 def second_kernel(
-    ids_hbm, m2_hbm, recv_ref, own_recv_ref, before_ref, table_ref, m1_ref,
+    ids_hbm, m1_hbm, m2_hbm, recv_ref, own_recv_ref, before_ref, table_ref, m1_zero_ref,
     own_slots_ref, own_hat_ref, own_key_ref, own_column_ref, own_total_ref,
     grad_ref, m2_ref, out_ref,
-    ids_ref, corner_ref, aux_ref, slots_ref, hat_ref, key_ref, column_ref, cot_ref,
+    ids_ref, m1_ref, corner_ref, aux_ref, slots_ref, hat_ref, key_ref, column_ref, cot_ref,
     found_ref, result_ref, sems,
 ):
-    loads = start_all((ids_hbm, m2_hbm), (ids_ref, m2_ref), sems)
+    low, high = pl.ds(0, 64), pl.ds(64, 64)
+    sources = (ids_hbm, m1_hbm.at[high], m2_hbm, m1_zero_ref)
+    loads = start_all(sources, (ids_ref, m1_ref.at[high], m2_ref, m1_ref.at[low]), sems)
     grad_ref[...] = before_ref[...]
     result_ref[...] = jnp.zeros_like(result_ref)
     spare = (corner_ref, aux_ref, slots_ref, hat_ref, key_ref, column_ref, cot_ref)
     half = Half(recv_ref, *spare)
     blocks, own_blocks = block_finder(ids_ref, 1), block_finder(ids_ref, 0)
     passes = gradients(half, grad_ref, blocks, loads[0].wait)
-    loads[1].wait()
+    wait_all(loads[1:])
 
     def rows_at(block):
         first, second = moments(grad_ref[block], m1_ref[block], m2_ref[block])
@@ -483,7 +485,7 @@
     id_table = pltpu.SMEM((64, LANES), i32)
     grad, slots, hat, key, column, total, m1 = call(
         first_kernel,
-        [full, lists, tile, tile, tile, pltpu.VMEM((8, LANES), i32), full],
+        [full, lists, tile, tile, tile, pltpu.VMEM((8, LANES), i32), pltpu.VMEM((64, 16, LANES), f32)],
         [HBM, VMEM, HBM],
         [id_table, data, data, tile, pltpu.SemaphoreType.DMA((2,))],
         cost_estimate=pl.CostEstimate(flops=1 << 30, bytes_accessed=4 << 20, transcendentals=0),
@@ -491,13 +493,13 @@
     grad, m2, found = call(
         second_kernel,
         [full, full, ((32, 8, LANES), f32)],
-        [HBM, HBM] + [VMEM] * 10,
+        [HBM] * 3 + [VMEM] * 10,
         [
-            id_table, data, data, lists, tile, tile, tile, tile, tile,
+            id_table, full, data, data, lists, tile, tile, tile, tile, tile,
             pltpu.VMEM((32, 8, LANES), f32),
-            pltpu.SemaphoreType.DMA((2,)),
+            pltpu.SemaphoreType.DMA((4,)),
         ],
-    )(ids, *in_hbm(rows_of(moment2)), others, samples, grad, rows_of(table), m1, slots, hat, key, column, total)
+    )(ids, *in_hbm(rows_of(moment1), rows_of(moment2)), others, samples, grad, rows_of(table), m1, slots, hat, key, column, total)
     back = exchange(found.reshape(128, 2, LANES)).reshape(32, 8, LANES)
     tnew, m1new, m2new = call(
         third_kernel,

time: 46.3 us -> 46.2 us (level)
  no operation moved by 1% of the time
where the time goes in v12:
time: 46.2 us; the launch traced here: 45.3 us
  blocking collectives  21.9 us (47%)
  Pallas kernels  11.6 us (25%)
  waiting for transfers between devices  6.39 us (14%)
  starting transfers between devices  4.67 us (10%)
  between operations  0.71 us (2%)
    all_to_all x1, blocking collectives, exchange(): lax.all_to_all(value, ('table', 'ray'), split_axis=0, concat_axis=0, tile...  21.9 us
    all_to_all x1, waiting for transfers between devices, exchange(): lax.all_to_all(value, ('table', 'ray'), split_axis=0, concat_axis=0, tile...  6.39 us
    all_to_all x1, starting transfers between devices, exchange(): lax.all_to_all(value, ('table', 'ray'), split_axis=0, concat_axis=0, tile...  4.67 us
    pallas_call x1, Pallas kernels, on_device(): call(second_kernel, [full, full, ((32, 8, LANES), f32)], [HBM] * 3 + [VME...  4.44 us
    pallas_call x1, Pallas kernels, on_device(): call(third_kernel, [(rows, f32)] * 3, [VMEM] * 2 + [HBM] * 2, [full, full...  3.16 us
    pallas_call x1, Pallas kernels, on_device(): call(first_kernel, [full, lists, tile, tile, tile, pltpu.VMEM((8, LANES),...  2.09 us
    pallas_call x1, Pallas kernels, on_device(): call(network_kernel, [((16, 512), f32)], [VMEM] * 3)  0.99 us
    pallas_call x1, Pallas kernels, on_device(): call(pack_kernel, [((64, 8, LANES), f32)], [HBM] * 4, [pltpu.VMEM((2, 512...  0.97 us
  transfers between devices with their start and end apart: 2, of which 1 were waited for; matrix products, arithmetic and copies ran while one was open for 0% of the time, Pallas kernels for 12%

profile of v12, /device:TPU:0, one launch (start us, length us, event | category | flops | bytes accessed | tf_op | source)
XLA Modules:
  0.0 45.3 jit_solution(574676133267897917)
XLA Ops:
  0.6 1.0 %shard_map.129 = f32[64,8,128]{2,1,0:T(8,128)S(1)} custom-call(s32[2,512]{1,0:T(2,128)} %slot_hbm.1, s32[2,8,512]{2,1,0:T(8,128)} %corners_hbm.1, f32[3,2,512]{2,1,0:T(2,128)} %bitcast.47, f32[2,4,512]{2,1,0:T(4,128)} %cot_hbm.1), custom_call_target="tpu_custom_call" | custom-call | tf_op jit(solution)/shard_map/pallas_call | solution.py:465
  1.6 21.9 %all_to_all.10.recv_ref.own_recv_ref = f32[64,8,128]{2,1,0:T(8,128)S(1)} all-to-all(f32[64,8,128]{2,1,0:T(8,128)S(1)} %shard_map.129), channel_id=1, replica_groups={{0,1,2,3,4,5,6,7,8,9,10,11,12,13,14,15,32,33,34,35,36,37,38,39,40,41,42..., dimensions={0} | all-to-all | bytes 524288 | tf_op jit(solution)/shard_map/all_to_all | solution.py:429
  23.5 0.0 collective-permute-start
  23.5 0.0 copy-start
  23.5 2.1 %shard_map.130 = (f32[128,16,128]{2,1,0:T(8,128)S(1)}, s32[4,8,128]{2,1,0:T(8,128)S(1)}, f32[8,8,128]{2,1,0:T(8,128)S(1)}, f32[8,8,128]{2,1,0:T(8,128)S(1)}, f32...) custom-call(s32[64,128]{1,0:T(8,128)} %bitcast.45, ...), custom_call_target="tpu_custom_call" | custom-call | flops 1073741824 | bytes 4194304 | tf_op jit(solution)/shard_map/pallas_call | solution.py:486
  25.6 0.0 collective-permute-done.recv_ref
  25.6 0.0 copy-done
  25.6 4.4 %shard_map.131 = (f32[128,16,128]{2,1,0:T(8,128)S(1)}, f32[128,16,128]{2,1,0:T(8,128)S(1)}, f32[32,8,128]{2,1,0:T(8,128)}) custom-call(s32[64,128]{1,0:T(8,128)} %bitcast.46, f32[128,16,128]{2,1,0:T(8,128)} %bitcast.42, f32[128,16,128]{2,1,0:T(8,128)} %bitcast.44, f32[64,8,128]{2,1,0:T(8,128)S(1)} %collective-permute-done.recv_ref, ...), custom_call_target="tpu_custom_call" | custom-call | tf_op jit(solution)/shard_map/pallas_call | solution.py:493
  30.1 4.7 %all-to-all-start.1 = ((f32[128,2,128]{2,1,0:T(2,128)}), f32[128,2,128]{2,1,0:T(2,128)S(1)}, u32[]{:S(2)}, u32[]{:S(2)}) async-start(f32[128,2,128]{2,1,0:T(2,128)} %bitcast.24), calls=%async_computation.1 | async-start | bytes 262144 | tf_op jit(solution)/shard_map/all_to_all | solution.py:429
  34.8 0.0 copy-start.1
  34.8 0.0 copy-start.2
  34.8 3.2 %shard_map.132 = (f32[128,16,128]{2,1,0:T(8,128)}, f32[128,16,128]{2,1,0:T(8,128)}, f32[128,16,128]{2,1,0:T(8,128)}) custom-call(f32[128,16,128]{2,1,0:T(8,128)S(1)} %get-tuple-element.24.grad_ref, f32[128,16,128]{2,1,0:T(8,128)S(1)} %get-tuple-element.25.m2_ref, f32[128,16,128]{2,1,0:T(8,128)} %bitcast.43, f32[128,16,128]{2,1,0:T(8,128)} %bitcast.37), custom_call_target="tpu_custom_call" | custom-call | flops 20971520 | bytes 7340032 | tf_op jit(solution)/shard_map/pallas_call | solution.py:504
  37.9 6.4 %all-to-all-done.1 = f32[128,2,128]{2,1,0:T(2,128)S(1)} async-done(((f32[128,2,128]{2,1,0:T(2,128)}), f32[128,2,128]{2,1,0:T(2,128)S(1)}, u32[]{:S(2)}, u32[]{:S(2)}) %all-to-all-start.1) | async-done | bytes 131104 | tf_op jit(solution)/shard_map/all_to_all | solution.py:429
  44.3 0.0 copy-done.1
  44.3 0.0 copy-done.2
  44.3 1.0 %shard_map.133 = f32[16,512]{1,0:T(8,128)} custom-call(f32[32,8,128]{2,1,0:T(8,128)S(1)} %bitcast.39, f32[8,64]{1,0:T(8,128)S(1)} %bitcast.40, f32[16,64]{1,0:T(8,128)S(1)} %copy-done.1), custom_call_target="tpu_custom_call" | custom-call | tf_op jit(solution)/shard_map/pallas_call | solution.py:512
Async XLA Ops:
  23.5 2.1 %collective-permute-start = (f32[64,8,128]{2,1,0:T(8,128)S(1)}, f32[64,8,128]{2,1,0:T(8,128)S(1)}, u32[]{:S(2)}, u32[]{:S(2)}) collective-permute-start(f32[64,8,128]{2,1,0:T(8,128)S(1)} %all_to_all.10.recv_ref.own_recv_ref), channel_id=1, source_target_pairs={{0,16},{16,0},{32,48},{48,32},{64,80},{80,64},{96,112},{112,96},{1... | collective-permute-start | bytes 786440 | tf_op jit(solution)/shard_map/ppermute | solution.py:440
  23.5 2.1 %copy-start = (f32[2,64,4,512]{3,2,1,0:T(4,128)S(1)}, f32[2,64,4,512]{3,2,1,0:T(4,128)}, u32[]{:S(2)}) copy-start(f32[2,64,4,512]{3,2,1,0:T(4,128)} %param.10) | copy-start | bytes 3145732
  30.1 14.3 %all-to-all-start.1 = ((f32[128,2,128]{2,1,0:T(2,128)}), f32[128,2,128]{2,1,0:T(2,128)S(1)}, u32[]{:S(2)}, u32[]{:S(2)}) async-start(f32[128,2,128]{2,1,0:T(2,128)} %bitcast.24), calls=%async_computation.1 | async-start | bytes 262144 | tf_op jit(solution)/shard_map/all_to_all | solution.py:429
  34.8 9.6 %copy-start.1 = (f32[16,64]{1,0:T(8,128)S(1)}, f32[16,64]{1,0:T(8,128)}, u32[]{:S(2)}) copy-start(f32[16,64]{1,0:T(8,128)} %wout_ref.1) | copy-start | bytes 12292
  34.8 9.6 %copy-start.2 = (f32[64,8]{0,1:T(8,128)S(1)}, f32[64,8]{0,1:T(8,128)}, u32[]{:S(2)}) copy-start(f32[64,8]{0,1:T(8,128)} %param.18) | copy-start | bytes 6148
